TPU v7x, 32 devices: a whole 2x2x4 slice. The times are simulated.
32 devices in a mesh: ctx: 8 (over y, x, core), head: 4 (over z).
Axes of the slice: x: 2, y: 2, z: 4, core: 2. Of those that a mesh axis runs over, the one named last changes fastest.
Arguments:
- queries: bfloat16 [4096, 4096], P(('ctx', 'head')), may hold values from -128 to 128
- vis_feats: bfloat16 [4096, 8192], P('ctx', 'head'), may hold values from -16 to 16
- kv_weight: bfloat16 [8192, 1024], P('head'), may hold values from -0.044194174 to 0.044194174
- key_gain: float32 [128], replicated, may hold values from 0.1 to 1.9
- cross_mask: int32 [4096, 4], P('ctx'), may hold values 0 or 1
- image_tokens: int32 [4], replicated, may hold values from 1 to 512, 1280 in all
- image_owner: int32 [4], replicated, may hold values from 0 to 7, as said below
Outputs:
- attended: bfloat16 [4096, 4096], P(('ctx', 'head'))
Inputs may be any that keep to these rules, and one draw needn't show every extreme that they name: `image_tokens`: they sum to 1280; the largest is exactly 512. `image_owner`: four distinct context indices; the first and the last index of ctx always hold an image.
All inputs are finite; a program needn't handle non-finite values. No bound on the sum of `cross_mask` on one device may be relied on, other than what follows from the above.
Results may differ from a plain program's by a relative error of at most 0.0014.
The roundings to bfloat16 on the way count: a program that leaves them out, or rounds other values in their place, can miss the bound.
Values may be sent and summed in bfloat16 or wider, within the bound.
No kernel may reach another device: no remote copies, remote signals or barrier semaphores. Data moves between devices by JAX's collectives and lax.ppermute only.
A program may use at most 64 MiB of HBM per device.

v0:
```python
import jax
import jax.numpy as jnp
from jax import lax
from jax.sharding import PartitionSpec as P

EPSILON = 1e-05
FLOOR_SCORE = -1e30


def swapped(value, axis, bit):
    mask = 2**bit
    pairs = [(source, source ^ mask) for source in range(lax.axis_size(axis))]
    return lax.ppermute(value, axis, pairs)


def broadcast(shard, axis, root):
    mine = lax.axis_index(axis) == root
    return lax.psum(jnp.where(mine, shard, jnp.zeros_like(shard)), axis)


def normalize_keys(stacked, key_gain):
    raw_keys = stacked[..., 0, :, :]
    square_mean = jnp.mean(raw_keys * raw_keys, axis=-2, keepdims=True)
    normed = raw_keys * lax.rsqrt(square_mean + EPSILON) * key_gain[:, None]
    joined = jnp.stack([normed, stacked[..., 1, :, :]], axis=-3)
    return joined.astype(jnp.bfloat16)


def arrange_keys(received, image_tokens):
    cap_rows = received[0].shape[-1]
    count_img = len(received)
    img_ids = jnp.arange(count_img, dtype=jnp.int32)
    laid_out = jnp.concatenate(received, axis=-1)
    positions = jnp.arange(count_img * cap_rows, dtype=jnp.int32)[:, None]
    member = (positions // cap_rows == img_ids[None, :]) & (
        positions % cap_rows < image_tokens[None, :]
    )
    return (laid_out, member.astype(jnp.float32))


def attend_rows(query_rows, mask_rows, key_cols, value_cols, member):
    row_count = query_rows.shape[0]
    rows_per_block = min(512, row_count)
    count_of_blocks = row_count // rows_per_block
    blocked_queries = query_rows.reshape((count_of_blocks, rows_per_block) + query_rows.shape[1:])
    mask_blocks = mask_rows.reshape(count_of_blocks, rows_per_block, mask_rows.shape[1])
    factor = query_rows.shape[-1] ** (-0.5)
    member_rows = member.T

    def one_block(block_pair):
        query_block, mask_block = block_pair
        allowed = jnp.dot(mask_block.astype(jnp.float32), member_rows) > 0.5
        allowed = allowed[:, None, :]
        scores = (
            jnp.einsum("rnd,dk->rnk", query_block, key_cols, preferred_element_type=jnp.float32)
            * factor
        )
        largest = jnp.max(jnp.where(allowed, scores, FLOOR_SCORE), axis=-1, keepdims=True)
        weights = jnp.where(allowed, jnp.exp(scores - largest), 0.0)
        summed = jnp.sum(weights, axis=-1, keepdims=True)
        mixed_out = jnp.einsum(
            "rnk,dk->rnd",
            weights.astype(jnp.bfloat16),
            value_cols,
            preferred_element_type=jnp.float32,
        )
        return (mixed_out / jnp.maximum(summed, 1.0)).astype(jnp.bfloat16)

    return lax.map(one_block, (blocked_queries, mask_blocks)).reshape(query_rows.shape)


def shards(queries, vis_feats, kv_weight, key_gain, cross_mask, image_tokens, image_owner):
    head_count = lax.axis_size("head")
    head_index = lax.axis_index("head")
    count_img = image_owner.shape[0]
    width_kv = kv_weight.shape[1]
    head_dim = key_gain.shape[0]
    kv_heads = width_kv // (2 * head_dim)
    tok_rows = queries.shape[0]
    query_heads = queries.shape[1] // head_dim
    per_kv = head_count // kv_heads
    share_part = lax.psum_scatter(
        lax.dot_general(
            kv_weight, vis_feats, (((0,), (1,)), ((), ())), preferred_element_type=jnp.float32
        ),
        "head",
        scatter_dimension=0,
        tiled=True,
    )
    for bit_index in range(per_kv.bit_length() - 1):
        partner = swapped(share_part, "head", bit_index)
        low_half = (head_index >> bit_index) % 2 == 0
        share_part = jnp.where(
            low_half,
            jnp.concatenate([share_part, partner], 0),
            jnp.concatenate([partner, share_part], 0),
        )
    local_kv = normalize_keys(share_part.reshape(1, 2, head_dim, -1), key_gain)[0].reshape(
        2 * head_dim, -1
    )
    received = [
        broadcast(local_kv, "ctx", image_owner[img_index]) for img_index in range(count_img)
    ]
    laid_out, member = arrange_keys(received, image_tokens)
    key_cols = laid_out[:head_dim]
    value_cols = laid_out[head_dim:]
    group_size = query_heads // head_count
    grouped = queries.reshape(tok_rows, head_count, group_size, head_dim)
    exchanged = lax.all_to_all(grouped, "head", split_axis=1, concat_axis=0, tiled=True)
    rows_all = exchanged.shape[0]
    flat_rows = exchanged.reshape(rows_all, exchanged.shape[2], head_dim)
    attended_heads = attend_rows(flat_rows, cross_mask, key_cols, value_cols, member).reshape(
        exchanged.shape
    )
    restored = lax.all_to_all(attended_heads, "head", split_axis=0, concat_axis=1, tiled=True)
    return restored.reshape(tok_rows, query_heads * head_dim)


def solution(mesh):
    return jax.shard_map(
        shards,
        mesh=mesh,
        in_specs=(
            P(("ctx", "head"), None),
            P("ctx", "head"),
            P("head", None),
            P(),
            P("ctx", None),
            P(),
            P(),
        ),
        out_specs=P(("ctx", "head"), None),
        check_vma=False,
    )
```

profile of v0, /device:TPU:0, one launch (start us, length us, event | category | flops | bytes accessed | tf_op | source)
XLA Modules:
  0.0 219.0 jit_solution(8036381709302970630)
XLA Ops:
  6.5 0.0 reduce-scatter.2.cloned.1.call-start
  6.6 1.5 copy-done
  8.1 5.9 %fusion.36 = f32[1024,512]{1,0:T(8,128)} fusion(bf16[2048,1024]{1,0:T(8,128)(2,1)} %param.9, bf16[512,2048]{1,0:T(8,128)(2,1)S(1)} %copy-done), kind=kOutput, calls=%fused_computation.55 | convolution fusion | flops 2147483648 | bytes 8388608 | tf_op jit(solution)/shard_map/dot_general | solution.py:83
  14.0 0.0 reduce-scatter.2.cloned.1.call-update
  14.0 1.6 copy.29
  15.7 1.3 copy.30
  17.0 6.3 %all-to-all-start = ((bf16[128,4,8,128]{3,0,2,1:T(8,128)(2,1)}), bf16[128,4,8,128]{3,0,2,1:T(8,128)(2,1)S(1)}, u32[]{:S(2)}, u32[]{:S(2)}) async-start(bf16[128,4,8,128]{3,0,2,1:T(8,128)(2,1)} %copy.30), calls=%async_computation.1 | async-start | bytes 2097152 | tf_op jit(solution)/shard_map/all_to_all | solution.py:109
  23.3 0.0 all-reduce.3.cloned.1.call-start
  23.4 0.7 fusion.34
  26.5 54.1 %reduce-scatter.2.cloned.1.call-done = f32[256,512]{1,0:T(8,128)} async-done(((f32[1024,512]{1,0:T(8,128)}), f32[256,512]{1,0:T(8,128)}) %reduce-scatter.2.cloned.1.call-update) | async-done | bytes 524304 | tf_op jit(solution)/shard_map/reduce_scatter | solution.py:82
  80.5 1.0 slice.49
  81.5 1.0 multiply_reduce_fusion
  82.5 1.0 multiply_convert_fusion
  83.6 0.9 broadcast_select_fusion
  84.5 1.8 copy.41
  86.3 1.8 copy.39
  88.0 1.8 copy.40
  89.8 0.8 copy.38
  90.7 0.0 all-reduce.3.cloned.1.call-update
  90.7 2.6 %compare_bitcast_fusion = pred[512,2048]{0,1:T(8,128)(4,1)} fusion(s32[4]{0:T(128)S(1)} %copy-done.4, s32[2048]{0:T(1024)S(1)} %get-tuple-element.41, s32[2048]{0:T(1024)S(1)} %get-tuple-element.40, s32[512,4]{0,1:T(4,128)S(1)} %copy-done.3), kind=kOutput, calls=%fused_computation.12 | convolution fusion | flops 9463808 | bytes 1073168 | tf_op jit(solution)/shard_map/while/body/eval_jaxpr/dot_general | solution.py:52
  93.3 1.1 copy.31
  94.4 54.2 %all-reduce.3.cloned.1.call-done = (bf16[256,512]{0,1:T(8,128)(2,1)}, bf16[256,512]{0,1:T(8,128)(2,1)}, bf16[256,512]{0,1:T(8,128)(2,1)}, bf16[256,512]{0,1:T(8,128)(2,1)}) async-done(((bf16[256,512]{0,1:T(8,128)(2,1)}, bf16[256,512]{0,1:T(8,128)(2,1)}, bf16[256,512]{0,1:T(8,128)(2,1)}, bf16[256,512]{0,1:T(8,128)(2,1)}), (bf16[256,512]{0,1:T(8,128)(2,1)}, bf16[256,512]{0,1:T(8,128)(2,1)}, ...) | async-done | bytes 1048592 | tf_op jit(solution)/shard_map/psum | solution.py:18
  148.5 1.0 constant_dynamic-update-slice_fusion.3
  149.5 1.0 constant_dynamic-update-slice_fusion.2
  150.5 1.0 constant_dynamic-update-slice_fusion.1
  151.4 1.0 constant_dynamic-update-slice_fusion
  152.4 17.6 %fusion.35 = (f32[512,8]{0,1:T(8,128)S(1)}, bf16[512,8,2048]{0,2,1:T(8,128)(2,1)}) fusion(pred[512,2048]{0,1:T(8,128)(4,1)} %compare_bitcast_fusion, bf16[512,8,128]{2,0,1:T(8,128)(2,1)} %bitcast.66, bf16[256,2048]{0,1:T(8,128)(2,1)S(1)} %constant_dynamic-update-slice_fusion), kind=kOutput, calls=%fused_computation.54 | convolution fusion | flops 4353689600 | bytes 22036480 | tf_op jit(solution)/shard_map/while/body/eval_jaxpr/sub | solution.py:59
  170.0 10.8 %fusion.14 = bf16[512,1,8,128]{3,0,2,1:T(8,128)(2,1)S(1)} fusion(bf16[512,8,2048]{0,2,1:T(8,128)(2,1)} %get-tuple-element.39, f32[512,8]{0,1:T(8,128)S(1)} %broadcast_maximum_fusion, bf16[256,2048]{0,1:T(8,128)(2,1)S(1)} %constant_dynamic-update-slice_fusion), kind=kOutput, calls=%fused_computation.15 | convolution fusion | flops 2148532224 | bytes 18366464 | tf_op jit(solution)/shard_map/while/body/eval_jaxpr/rnk,dk->rnd/dot_general | solution.py:61
  180.8 0.7 copy.34
  181.5 29.3 %all_to_all.30 = bf16[512,1,8,128]{3,2,1,0:T(8,128)(2,1)S(1)} all-to-all(bf16[512,1,8,128]{3,2,1,0:T(8,128)(2,1)S(1)} %copy.34), channel_id=1, replica_groups=mesh['ctx'=8,'head'=4] {'head'}, dimensions={0} | all-to-all | bytes 2097152 | tf_op jit(solution)/shard_map/all_to_all | solution.py:115
  210.7 0.2 copy.35
  210.9 1.3 reshape.149
  (13 shorter events, 0.0 us)
Async XLA Ops:
  6.5 1.6 copy-start
  6.5 16.8 %copy-start.1 = (s32[4]{0:T(128)S(1)}, s32[4]{0:T(128)}, u32[]{:S(2)}) copy-start(s32[4]{0:T(128)} %param.13) | copy-start | bytes 52
  6.5 76.0 %copy-start.2 = (f32[128]{0:T(128)S(1)}, f32[128]{0:T(128)}, u32[]{:S(2)}) copy-start(f32[128]{0:T(128)} %param.10) | copy-start | bytes 1540
  6.5 84.2 %copy-start.4 = (s32[4]{0:T(128)S(1)}, s32[4]{0:T(128)}, u32[]{:S(2)}) copy-start(s32[4]{0:T(128)} %param.12) | copy-start | bytes 52
  6.5 84.2 %copy-start.3 = (s32[512,4]{0,1:T(4,128)S(1)}, s32[512,4]{0,1:T(4,128)}, u32[]{:S(2)}) copy-start(s32[512,4]{0,1:T(4,128)} %param.11) | copy-start | bytes 24580
  6.5 74.0 %reduce-scatter.2.cloned.1.call-start = ((), (), s32[]{:S(2)}) async-start(), calls=%async_computation.3 | async-start | bytes 2621440 | tf_op jit(solution)/shard_map/reduce_scatter | solution.py:82
  17.0 76.3 %all-to-all-start = ((bf16[128,4,8,128]{3,0,2,1:T(8,128)(2,1)}), bf16[128,4,8,128]{3,0,2,1:T(8,128)(2,1)S(1)}, u32[]{:S(2)}, u32[]{:S(2)}) async-start(bf16[128,4,8,128]{3,0,2,1:T(8,128)(2,1)} %copy.30), calls=%async_computation.1 | async-start | bytes 2097152 | tf_op jit(solution)/shard_map/all_to_all | solution.py:109
  23.3 125.2 %all-reduce.3.cloned.1.call-start = ((), (), s32[]{:S(2)}) async-start(), calls=%async_computation.4 | async-start | bytes 2097152 | tf_op jit(solution)/shard_map/psum | solution.py:18
Sparse Core Ops, SparseCore 0:
  14.2 66.3 reduce-scatter.1
  90.8 57.6 all-reduce.2
where the time goes:
time: 220 us; the launch traced here: 219 us
  waiting for transfers between devices  108 us (49%)
  matrix products  36.8 us (17%)
  blocking collectives  29.3 us (13%)
  local copies, waits for them, and re-layouts  19.4 us (9%)
  between operations  16 us (7%)
  starting transfers between devices  6.38 us (3%)
  other arithmetic  2.95 us (1%)
    psum x1, waiting for transfers between devices, broadcast(): return lax.psum(jnp.where(mine, shard, jnp.zeros_like(shard)), axis)  54.2 us
    reduce_scatter x1, waiting for transfers between devices, shards(): lax.psum_scatter(lax.dot_general(kv_weight, vis_feats, (((0,), (1,)), (()...  54.1 us
    all_to_all x1, blocking collectives, shards(): lax.all_to_all(attended_heads, 'head', split_axis=0, concat_axis=1, tiled...  29.3 us
    sub x1, matrix products, one_block(): weights = jnp.where(allowed, jnp.exp(scores - largest), 0.0)  17.6 us
    dot_general x1, matrix products, one_block(): jnp.einsum('rnk,dk->rnd', weights.astype(jnp.bfloat16), value_cols, prefe...  10.8 us
    all_to_all x1, starting transfers between devices, shards(): lax.all_to_all(grouped, 'head', split_axis=1, concat_axis=0, tiled=True)  6.34 us
    select_n x4, local copies, waits for them, and re-layouts, broadcast(): return lax.psum(jnp.where(mine, shard, jnp.zeros_like(shard)), axis)  6.19 us
    unnamed x14, local copies, waits for them, and re-layouts  6.07 us
  transfers between devices with their start and end apart: 3, of which 2 were waited for; matrix products, arithmetic and copies ran while one was open for 8% of the time, Pallas kernels for 0%

commit v1 on v0

v1 whole, which is shorter than its diff:
```python
import functools
import math

import jax
import jax.numpy as jnp
from jax import lax
from jax.experimental import pallas as pl
from jax.experimental.pallas import tpu as pltpu
from jax.sharding import PartitionSpec as P

EPSILON = 1e-05
FLOOR_SCORE = -1e30
KV_TOTAL = 1280


def swapped(value, axis, bit):
    mask = 2**bit
    pairs = [(source, source ^ mask) for source in range(lax.axis_size(axis))]
    return lax.ppermute(value, axis, pairs)


def project(chunk_ids, vis_feats, kv_weight, chunk_count, pair):
    rows, width = vis_feats.shape
    wanted = chunk_ids.shape[0]
    kv_heads = kv_weight.shape[1] // pair
    per_kv = chunk_count // kv_heads
    block_rows = rows // per_kv

    def kernel(ids_ref, feats_ref, weight_ref, out_ref):
        out_ref[0] = jnp.dot(feats_ref[...], weight_ref[...], preferred_element_type=jnp.float32)

    return pl.pallas_call(
        kernel,
        grid_spec=pltpu.PrefetchScalarGridSpec(
            num_scalar_prefetch=1,
            grid=(wanted,),
            in_specs=[
                pl.BlockSpec((block_rows, width), lambda n, ids: (ids[n] % per_kv, 0)),
                pl.BlockSpec((width, pair), lambda n, ids: (0, ids[n] // per_kv)),
            ],
            out_specs=pl.BlockSpec((1, block_rows, pair), lambda n, ids: (n, 0, 0)),
        ),
        out_shape=jax.ShapeDtypeStruct((wanted, block_rows, pair), jnp.float32),
        name="project",
    )(chunk_ids, vis_feats, kv_weight)


def finish_chunk(scalars, own, from_left, from_right, key_gain):
    rows, width = own.shape
    head_dim = width // 2
    half = KV_TOTAL // 2
    pieces = len(from_left)

    def kernel(*refs):
        scalars_ref, own_ref = refs[:2]
        left_refs = refs[2 : 2 + pieces]
        right_refs = refs[2 + pieces : 2 + 2 * pieces]
        gain_ref, out_ref = refs[2 + 2 * pieces :]
        sub = rows // pieces
        placed = []
        for piece in range(pieces):
            total = own_ref[piece * sub : (piece + 1) * sub, :] + left_refs[piece][...]
            total = total + right_refs[piece][...]
            raw = total[:, :head_dim]
            mean = jnp.mean(raw * raw, axis=-1, keepdims=True)
            keys = raw * lax.rsqrt(mean + EPSILON) * gain_ref[...]
            placed.append(jnp.concatenate([keys, total[:, head_dim:]], axis=1).astype(jnp.bfloat16))
        data = jnp.concatenate(placed, axis=0)
        start, count, first = scalars_ref[0], scalars_ref[1], scalars_ref[2]
        token = lax.broadcasted_iota(jnp.int32, (half, rows), 1) + first
        token = jnp.where(token < count, token, -2 * KV_TOTAL)
        row = lax.broadcasted_iota(jnp.int32, (half, rows), 0)
        for part in range(2):
            match = (row + (scalars_ref[3 + part] - start)) == token
            chosen = jnp.where(match, 1.0, 0.0).astype(jnp.bfloat16)
            out = jnp.dot(chosen, data, preferred_element_type=jnp.float32)
            out_ref[part] = out.astype(jnp.bfloat16)

    vmem = pl.BlockSpec(memory_space=pltpu.VMEM)
    return pl.pallas_call(
        kernel,
        in_specs=[pl.BlockSpec(memory_space=pltpu.SMEM)] + [vmem] * (2 + 2 * pieces),
        out_specs=vmem,
        out_shape=jax.ShapeDtypeStruct((2, half, width), jnp.bfloat16),
        name="finish",
    )(scalars, own, *from_left, *from_right, key_gain[None, :])


def attend(head_ids, blocks, queries, row_mask, token_bias, previous):
    rows, width = queries.shape
    count = len(blocks)
    half = KV_TOTAL // 2
    head_dim = blocks[0][0].shape[1] // 2
    group = width // (head_dim * attend.kv_heads)
    block_width = group * head_dim
    factor = head_dim ** (-0.5) * math.log2(math.e)
    stack = 2

    def kernel(*refs):
        ids_ref, queries_ref, mask_ref, bias_ref = refs[:4]
        block_refs = refs[4 : 4 + 2 * count]
        refs = refs[4 + 2 * count :]
        if previous is not None:
            refs = refs[1:]
        out_ref, keys_ref, values_ref, query_ref, result_ref, sems = refs
        keys_ref[:, head_dim:] = bias_ref[...]
        some = jnp.min(mask_ref[:, : attend.images].astype(jnp.float32), axis=1, keepdims=True) < 0.5
        for n in range(count):

            @pl.when(ids_ref[n] >= 0)
            def _():
                column = pl.multiple_of(ids_ref[n] * block_width, block_width)
                fetch = pltpu.make_async_copy(
                    queries_ref.at[:, pl.ds(column, block_width)], query_ref, sems.at[0]
                )
                fetch.start()
                for side in range(2):
                    span = slice(side * half, (side + 1) * half)
                    keys_ref[span, :head_dim] = block_refs[2 * n + side][:, :head_dim]
                    values_ref[span, :] = block_refs[2 * n + side][:, head_dim:]
                fetch.wait()
                for first in range(0, group, stack):
                    left = jnp.concatenate(
                        [
                            jnp.concatenate(
                                [query_ref[:, j * head_dim : (j + 1) * head_dim], mask_ref[...]],
                                axis=1,
                            )
                            for j in range(first, first + stack)
                        ],
                        axis=0,
                    )
                    scores = lax.dot_general(
                        left,
                        keys_ref[...],
                        (((1,), (1,)), ((), ())),
                        preferred_element_type=jnp.float32,
                    )
                    largest = jnp.max(scores, axis=1, keepdims=True)
                    weights = jnp.exp2((scores - largest) * factor)
                    summed = jnp.sum(weights, axis=1, keepdims=True)
                    mixed = jnp.dot(
                        weights.astype(jnp.bfloat16),
                        values_ref[...],
                        preferred_element_type=jnp.float32,
                    )
                    mixed = mixed / jnp.maximum(summed, 1.0)
                    for j in range(stack):
                        one = jnp.where(some, mixed[j * rows : (j + 1) * rows], 0.0)
                        at = (first + j) * head_dim
                        result_ref[:, at : at + head_dim] = one.astype(jnp.bfloat16)
                store = pltpu.make_async_copy(
                    result_ref, out_ref.at[:, pl.ds(column, block_width)], sems.at[1]
                )
                store.start()
                store.wait()

    vmem = pl.BlockSpec(memory_space=pltpu.VMEM)
    anywhere = pl.BlockSpec(memory_space=pl.ANY)
    operands = [head_ids, queries, row_mask, token_bias]
    in_specs = [pl.BlockSpec(memory_space=pltpu.SMEM), anywhere, vmem, vmem]
    for mine, other in blocks:
        operands += [mine, other]
        in_specs += [vmem, vmem]
    aliases = {}
    if previous is not None:
        aliases = {len(operands): 0}
        operands.append(previous)
        in_specs.append(anywhere)
    return pl.pallas_call(
        kernel,
        in_specs=in_specs,
        out_specs=anywhere,
        out_shape=jax.ShapeDtypeStruct((rows, width), jnp.bfloat16),
        scratch_shapes=[
            pltpu.VMEM((2 * half, 2 * head_dim), jnp.bfloat16),
            pltpu.VMEM((2 * half, head_dim), jnp.bfloat16),
            pltpu.VMEM((rows, block_width), jnp.bfloat16),
            pltpu.VMEM((rows, block_width), jnp.bfloat16),
            pltpu.SemaphoreType.DMA((2,)),
        ],
        input_output_aliases=aliases,
        name="attend",
    )(*operands)


def sum_over_head(vis_feats, kv_weight, pair, pieces):
    count = lax.axis_size("head")
    here = lax.axis_index("head")
    first = project((count - 1 - here)[None].astype(jnp.int32), vis_feats, kv_weight, count, pair)
    parts = project(jnp.arange(count, dtype=jnp.int32), vis_feats, kv_weight, count, pair)
    sub = parts.shape[1] // pieces

    def part(index, piece):
        index = jnp.clip(index, 0, count - 1)
        cut = lax.dynamic_slice(parts, (index, piece * sub, 0), (1, sub, parts.shape[2]))
        return cut[0]

    to_right, to_left = [None] * pieces, [None] * pieces
    for hop in range(1, count):
        right_pairs = [(i, i + 1) for i in range(min(hop, count - 1))]
        left_pairs = [(count - 1 - i, count - 2 - i) for i in range(min(hop, count - 1))]
        for piece in range(pieces):
            if hop == 1:
                cut = first[0, piece * sub : (piece + 1) * sub]
                right, left = cut, cut
            else:
                right = part(here + count - hop, piece) + to_right[piece]
                left = part(here - count + hop, piece) + to_left[piece]
            to_right[piece] = lax.ppermute(right, "head", right_pairs)
            to_left[piece] = lax.ppermute(left, "head", left_pairs)
    own = lax.dynamic_slice(parts, (here, 0, 0), (1,) + parts.shape[1:])[0]
    return own, to_right, to_left


def shards(queries, vis_feats, kv_weight, key_gain, cross_mask, image_tokens, image_owner):
    head_count = lax.axis_size("head")
    head_index = lax.axis_index("head")
    ctx_index = lax.axis_index("ctx")
    ctx_bits = lax.axis_size("ctx").bit_length() - 1
    images = image_owner.shape[0]
    head_dim = key_gain.shape[0]
    kv_heads = kv_weight.shape[1] // (2 * head_dim)
    per_kv = head_count // kv_heads
    rows = queries.shape[0]
    half = KV_TOTAL // 2

    own, from_left, from_right = sum_over_head(vis_feats, kv_weight, 2 * head_dim, 2)

    ends = jnp.cumsum(image_tokens)
    starts = ends - image_tokens
    mine = image_owner == ctx_index
    core = ctx_index % 2
    scalars = jnp.stack(
        [
            jnp.sum(jnp.where(mine, starts, 0)),
            jnp.sum(jnp.where(mine, image_tokens, 0)),
            (head_index % per_kv) * own.shape[0],
            half * core,
            half * (1 - core),
        ]
    ).astype(jnp.int32)
    packed = finish_chunk(scalars, own, from_left, from_right, key_gain)
    if per_kv > 1:
        groups = [[k * per_kv + j for j in range(per_kv)] for k in range(kv_heads)]
        packed = lax.psum(packed, "head", axis_index_groups=groups)
    block = packed[0] + swapped(packed[1], "ctx", 0)
    keys, values = block[:, :head_dim], block[:, head_dim:]
    for step in range(1, ctx_bits):
        keys = keys + swapped(keys, "ctx", step)
        values = values + swapped(values, "ctx", ctx_bits - step)
    block = jnp.concatenate([keys, values], axis=1)

    row_slice = lax.dynamic_slice_in_dim(cross_mask, head_index * rows, rows, 0)
    row_mask = jnp.concatenate(
        [1.0 - row_slice.astype(jnp.float32), jnp.ones((rows, 1), jnp.float32)], axis=1
    )
    row_mask = jnp.pad(row_mask, ((0, 0), (0, head_dim - images - 1))).astype(jnp.bfloat16)
    position = (jnp.arange(KV_TOTAL, dtype=jnp.int32) + half * core) % KV_TOTAL
    inside = (position[:, None] >= starts[None]) & (position[:, None] < ends[None])
    inside = jnp.concatenate([inside, position[:, None] >= ends[None, -1:]], axis=1)
    token_bias = jnp.where(inside, FLOOR_SCORE, 0.0)
    token_bias = jnp.pad(token_bias, ((0, 0), (0, head_dim - images - 1))).astype(jnp.bfloat16)

    attend.kv_heads = kv_heads
    attend.images = images
    run = functools.partial(
        attend, queries=queries, row_mask=row_mask, token_bias=token_bias
    )
    if per_kv > 1:
        groups = [[k * per_kv + j for k in range(kv_heads)] for j in range(per_kv)]
        gathered = lax.all_gather(block, "head", axis_index_groups=groups)
        other = swapped(gathered, "ctx", 0)
        out = None
        for k in range(kv_heads):
            ids = jnp.full((1,), k, jnp.int32)
            out = run(ids, [(gathered[k], other[k])], previous=out)
        return out

    to_right, to_left = block, block
    arrived = [([head_index], [block])]
    for hop in range(1, head_count):
        right_pairs = [(i, i + 1) for i in range(hop - 1, head_count - 1)]
        left_pairs = [(head_count - 1 - i, head_count - 2 - i) for i, _ in right_pairs]
        to_right = lax.ppermute(to_right, "head", right_pairs)
        to_left = lax.ppermute(to_left, "head", left_pairs)
        below, above = head_index - hop, head_index + hop
        above = jnp.where(above < head_count, above, -1)
        arrived.append(([below, above], [to_right, to_left]))
    out = None
    for ids, blocks in arrived:
        pairs = [(one, swapped(one, "ctx", 0)) for one in blocks]
        out = run(jnp.stack(ids).astype(jnp.int32), pairs, previous=out)
    return out


def solution(mesh):
    return jax.shard_map(
        shards,
        mesh=mesh,
        in_specs=(
            P(("ctx", "head"), None),
            P("ctx", "head"),
            P("head", None),
            P(),
            P("ctx", None),
            P(),
            P(),
        ),
        out_specs=P(("ctx", "head"), None),
        check_vma=False,
    )
```

time: 220 us -> 142 us (0.65)
  waiting for transfers between devices: 108 us -> 34.4 us
  starting transfers between devices: 6.38 us -> 49.5 us
  matrix products: 36.8 us -> 0 us
  Pallas kernels: 0 us -> 36.3 us
  blocking collectives: 29.3 us -> 0 us
  between operations: 16 us -> 0.62 us
  local copies, waits for them, and re-layouts: 19.4 us -> 9.23 us
  other arithmetic: 2.95 us -> 11.4 us
    psum x1 -> x0, waiting for transfers between devices: 54.2 us -> none  [broadcast(): return lax.psum(jnp.where(mine, shard, jnp.zeros_like(shard)), axis)]
    reduce_scatter x1 -> x0, waiting for transfers between devices: 54.1 us -> none  [shards(): lax.psum_scatter(lax.dot_general(kv_weight, vis_feats, (((0,), (1,)), (()...]
    ppermute x0 -> x30, starting transfers between devices: none -> 49.5 us  [the longest x6 27.2 us: sum_over_head(): to_right[piece] = lax.ppermute(right, 'head', right_pairs)]
    pallas_call x0 -> x7, Pallas kernels: none -> 36.3 us  [the longest x4 23 us: attend(): pl.pallas_call(kernel, in_specs=in_specs, out_specs=anywhere, out_shape=j...]
    ppermute x0 -> x30, waiting for transfers between devices: none -> 34.4 us  [the longest x3 13.5 us: shards(): to_left = lax.ppermute(to_left, 'head', left_pairs)]
    all_to_all x1 -> x0, blocking collectives: 29.3 us -> none  [shards(): lax.all_to_all(attended_heads, 'head', split_axis=0, concat_axis=1, tiled...]
    dot_general x3 -> x0, matrix products: 19.2 us -> none  [the longest x1 10.8 us: one_block(): jnp.einsum('rnk,dk->rnd', weights.astype(jnp.bfloat16), value_cols, prefe...]
    sub x1 -> x0, matrix products: 17.6 us -> none  [one_block(): weights = jnp.where(allowed, jnp.exp(scores - largest), 0.0)]
  transfers between devices with their start and end apart: 3 -> 30, of which waited for: 2 -> 13; matrix products, arithmetic and copies ran while one was open for 8% -> 9% of each run, Pallas kernels for 0% -> 17%
where the time goes in v1:
time: 142 us; the launch traced here: 141 us
  starting transfers between devices  49.5 us (35%)
  Pallas kernels  36.3 us (26%)
  waiting for transfers between devices  34.4 us (24%)
  other arithmetic  11.4 us (8%)
  local copies, waits for them, and re-layouts  9.23 us (6%)
    ppermute x6, starting transfers between devices, sum_over_head(): to_right[piece] = lax.ppermute(right, 'head', right_pairs)  27.2 us
    pallas_call x4, Pallas kernels, attend(): pl.pallas_call(kernel, in_specs=in_specs, out_specs=anywhere, out_shape=j...  23 us
    ppermute x3, waiting for transfers between devices, shards(): to_left = lax.ppermute(to_left, 'head', left_pairs)  13.5 us
    ppermute x12, waiting for transfers between devices, swapped(): return lax.ppermute(value, axis, pairs)  10.8 us
    pallas_call x2, Pallas kernels, project(): pl.pallas_call(kernel, grid_spec=pltpu.PrefetchScalarGridSpec(num_scalar_...  10.5 us
    ppermute x6, starting transfers between devices, sum_over_head(): to_left[piece] = lax.ppermute(left, 'head', left_pairs)  7.39 us
    ppermute x12, starting transfers between devices, swapped(): return lax.ppermute(value, axis, pairs)  6.79 us
    add x3, other arithmetic, sum_over_head(): left = part(here - count + hop, piece) + to_left[piece]  5.95 us
  transfers between devices with their start and end apart: 30, of which 13 were waited for; matrix products, arithmetic and copies ran while one was open for 9% of the time, Pallas kernels for 17%

profile of v1, /device:TPU:0, one launch (start us, length us, event | category | flops | bytes accessed | tf_op | source)
XLA Modules:
  0.0 141.4 jit_solution(4819608657400313947)
XLA Ops:
  0.0 3.4 %project.3 = f32[1,512,256]{2,1,0:T(8,128)} custom-call(s32[1]{0:T(128)} %bitcast.12.ids_ref, bf16[512,2048]{1,0:T(8,128)(2,1)} %feats_ref.3, bf16[2048,1024]{1,0:T(8,128)(2,1)} %weight_ref.3), custom_call_target="tpu_custom_call" | custom-call | tf_op jit(solution)/shard_map/project/pallas_call | solution.py:32
  5.8 5.0 %collective-permute-start.3 = (f32[256,256]{1,0:T(8,128)S(1)}, f32[256,256]{1,0:T(8,128)S(1)}, u32[]{:S(2)}, u32[]{:S(2)}) collective-permute-start(f32[256,256]{1,0:T(8,128)S(1)} %get-tuple-element.15), channel_id=1, source_target_pairs={{0,1},{4,5},{8,9},{12,13},{16,17},{20,21},{24,25},{28,29}} | collective-permute-start | bytes 786440 | tf_op jit(solution)/shard_map/ppermute | solution.py:210
  13.3 7.1 %project.2 = f32[4,512,256]{2,1,0:T(8,128)} custom-call(s32[4]{0:T(128)} %iota.13.ids_ref, bf16[512,2048]{1,0:T(8,128)(2,1)} %feats_ref.3, bf16[2048,1024]{1,0:T(8,128)(2,1)} %weight_ref.3), custom_call_target="tpu_custom_call" | custom-call | tf_op jit(solution)/shard_map/project/pallas_call | solution.py:32
  20.4 1.9 %bitcast_add_fusion = f32[256,256]{1,0:T(8,128)} fusion(f32[256,256]{1,0:T(8,128)} %collective-permute-done.9, f32[4,512,256]{2,1,0:T(8,128)} %project.2, s32[]{:T(128)S(6)} %min.20), kind=kLoop, calls=%fused_computation.7 | loop fusion | flops 65536 | bytes 786436 | tf_op jit(solution)/shard_map/add | solution.py:209
  24.4 2.2 %bitcast_add_fusion.1 = (f32[256,256]{1,0:T(8,128)S(1)}, f32[256,256]{1,0:T(8,128)S(1)}, f32[256,256]{1,0:T(8,128)S(1)}, f32[256,256]{1,0:T(8,128)}) fusion(f32[256,256]{1,0:T(8,128)} %collective-permute-done.10, f32[4,512,256]{2,1,0:T(8,128)} %project.2, s32[]{:T(128)S(6)} %min.19, f32[256,256]{1,0:T(8,128)} %copy-done.13, s32[]{:T(128)S(6)} %min.20, ...), kind=kLoop, calls=%fused_computation.8 | loop fusion | flops 262144 | bytes 3145740 | tf_op jit(solution)/shard_map/add | solution.py:209
  26.7 9.4 %collective-permute-start.1 = (f32[256,256]{1,0:T(8,128)}, f32[256,256]{1,0:T(8,128)S(1)}, u32[]{:S(2)}, u32[]{:S(2)}) collective-permute-start(f32[256,256]{1,0:T(8,128)} %get-tuple-element.11), channel_id=1, source_target_pairs={{0,1},{1,2},{4,5},{5,6},{8,9},{9,10},{12,13},{13,14},{16,17},{17,1... | collective-permute-start | bytes 786440 | tf_op jit(solution)/shard_map/ppermute | solution.py:210
  36.1 3.5 %collective-permute-start.4 = (f32[256,256]{1,0:T(8,128)S(1)}, f32[256,256]{1,0:T(8,128)S(1)}, u32[]{:S(2)}, u32[]{:S(2)}) collective-permute-start(f32[256,256]{1,0:T(8,128)S(1)} %get-tuple-element.10), channel_id=1, source_target_pairs={{0,1},{1,2},{4,5},{5,6},{8,9},{9,10},{12,13},{13,14},{16,17},{17,1... | collective-permute-start | bytes 786440 | tf_op jit(solution)/shard_map/ppermute | solution.py:210
  39.6 1.4 collective-permute-start.7
  43.1 3.5 %collective-permute-done.4 = f32[256,256]{1,0:T(8,128)S(1)} collective-permute-done((f32[256,256]{1,0:T(8,128)S(1)}, f32[256,256]{1,0:T(8,128)S(1)}, u32[]{:S(2)}, u32[]{:S(2)}) %collective-permute-start.4) | collective-permute-done | bytes 262176 | tf_op jit(solution)/shard_map/ppermute | solution.py:210
  46.6 1.8 %bitcast_add_fusion.3 = (f32[256,256]{1,0:T(8,128)S(1)}, f32[256,256]{1,0:T(8,128)S(1)}, f32[256,256]{1,0:T(8,128)}) fusion(f32[256,256]{1,0:T(8,128)} %collective-permute-done.7, f32[4,512,256]{2,1,0:T(8,128)S(1)} %copy-done.1, s32[]{:T(128)S(6)} %min.19, f32[256,256]{1,0:T(8,128)S(1)} %collective-permute-done.4, s32[]{:T(128)S(6)} %min.17, ...), kind=kLoop, calls=%fused_computation.10 | loop fusion | flops 196608 | bytes 2359304 | tf_op jit(solution)/shard_map/add | solution.py:209
  48.4 6.1 %collective-permute-start.2 = (f32[256,256]{1,0:T(8,128)}, f32[256,256]{1,0:T(8,128)S(1)}, u32[]{:S(2)}, u32[]{:S(2)}) collective-permute-start(f32[256,256]{1,0:T(8,128)} %get-tuple-element.14), channel_id=1, source_target_pairs={{0,1},{1,2},{2,3},{4,5},{5,6},{6,7},{8,9},{9,10},{10,11},{12,13},{... | collective-permute-start | bytes 786440 | tf_op jit(solution)/shard_map/ppermute | solution.py:210
  54.5 1.9 %collective-permute-start.5 = (f32[256,256]{1,0:T(8,128)S(1)}, f32[256,256]{1,0:T(8,128)S(1)}, u32[]{:S(2)}, u32[]{:S(2)}) collective-permute-start(f32[256,256]{1,0:T(8,128)S(1)} %get-tuple-element.13), channel_id=1, source_target_pairs={{0,1},{1,2},{2,3},{4,5},{5,6},{6,7},{8,9},{9,10},{10,11},{12,13},{... | collective-permute-start | bytes 786440 | tf_op jit(solution)/shard_map/ppermute | solution.py:210
  58.5 1.9 %stack.53.refs_0_ = s32[5]{0:T(128)} concatenate(s32[1]{0:T(128)} %bitcast.5, s32[1]{0:T(128)} %bitcast.6, s32[1]{0:T(128)} %constant.87.clone.1, s32[1]{0:T(128)} %bitcast.7, s32[1]{0:T(128)} %bitcast.8), dimensions={0} | concatenate | bytes 40 | tf_op jit(solution)/shard_map/stack | solution.py:234
  61.2 1.5 %collective-permute-done.5.refs_3_ = f32[256,256]{1,0:T(8,128)S(1)} collective-permute-done((f32[256,256]{1,0:T(8,128)S(1)}, f32[256,256]{1,0:T(8,128)S(1)}, u32[]{:S(2)}, u32[]{:S(2)}) %collective-permute-start.5) | collective-permute-done | bytes 262176 | tf_op jit(solution)/shard_map/ppermute | solution.py:210
  62.7 2.1 %collective-permute-done.8.refs_4_ = f32[256,256]{1,0:T(8,128)} collective-permute-done((f32[256,256]{1,0:T(8,128)S(1)}, f32[256,256]{1,0:T(8,128)}, u32[]{:S(2)}, u32[]{:S(2)}) %collective-permute-start.8) | collective-permute-done | bytes 262176 | tf_op jit(solution)/shard_map/ppermute | solution.py:211
  64.8 2.8 %finish.1 = bf16[2,640,256]{2,1,0:T(8,128)(2,1)} custom-call(s32[5]{0:T(128)} %stack.53.refs_0_, f32[512,256]{1,0:T(8,128)} %dynamic-slice_bitcast_fusion.refs_1_, f32[256,256]{1,0:T(8,128)} %copy-done.14, f32[256,256]{1,0:T(8,128)} %copy-done.15, f32[256,256]{1,0:T(8,128)} %collective-permute-done.8.refs_4_, f32[256,256]{1,0:T(8,128)} %collective-permute-done.11.refs_5_, ...), custom_call_target="tpu_custom_call" | custom-call | tf_op jit(solution)/shard_map/finish/pallas_call | solution.py:80
  68.7 1.6 %collective-permute-done.12 = bf16[640,256]{1,0:T(8,128)(2,1)S(1)} collective-permute-done((bf16[640,256]{1,0:T(8,128)(2,1)S(1)}, bf16[640,256]{1,0:T(8,128)(2,1)S(1)}, u32[]{:S(2)}, u32[]{:S(2)}) %collective-permute-start.12) | collective-permute-done | bytes 327712 | tf_op jit(solution)/shard_map/ppermute | solution.py:19
  71.4 1.6 %collective-permute-start.13 = (bf16[640,128]{1,0:T(8,128)(2,1)S(1)}, bf16[640,128]{1,0:T(8,128)(2,1)S(1)}, u32[]{:S(2)}, u32[]{:S(2)}) collective-permute-start(bf16[640,128]{1,0:T(8,128)(2,1)S(1)} %get-tuple-element.19), channel_id=1, source_target_pairs={{0,8},{4,12},{8,0},{12,4},{16,24},{20,28},{24,16},{28,20},{1,9},{5... | collective-permute-start | bytes 491528 | tf_op jit(solution)/shard_map/ppermute | solution.py:19
  72.9 1.5 %collective-permute-start.15 = (bf16[640,128]{1,0:T(8,128)(2,1)S(1)}, bf16[640,128]{1,0:T(8,128)(2,1)S(1)}, u32[]{:S(2)}, u32[]{:S(2)}) collective-permute-start(bf16[640,128]{1,0:T(8,128)(2,1)S(1)} %get-tuple-element.20), channel_id=1, source_target_pairs={{0,16},{4,20},{8,24},{12,28},{16,0},{20,4},{24,8},{28,12},{1,17},{... | collective-permute-start | bytes 491528 | tf_op jit(solution)/shard_map/ppermute | solution.py:19
  74.4 3.2 %collective-permute-done.13 = bf16[640,128]{1,0:T(8,128)(2,1)S(1)} collective-permute-done((bf16[640,128]{1,0:T(8,128)(2,1)S(1)}, bf16[640,128]{1,0:T(8,128)(2,1)S(1)}, u32[]{:S(2)}, u32[]{:S(2)}) %collective-permute-start.13) | collective-permute-done | bytes 163872 | tf_op jit(solution)/shard_map/ppermute | solution.py:19
  78.9 1.6 %collective-permute-start.14 = (bf16[640,128]{1,0:T(8,128)(2,1)S(1)}, bf16[640,128]{1,0:T(8,128)(2,1)S(1)}, u32[]{:S(2)}, u32[]{:S(2)}) collective-permute-start(bf16[640,128]{1,0:T(8,128)(2,1)S(1)} %get-tuple-element.17), channel_id=1, source_target_pairs={{0,16},{4,20},{8,24},{12,28},{16,0},{20,4},{24,8},{28,12},{1,17},{... | collective-permute-start | bytes 491528 | tf_op jit(solution)/shard_map/ppermute | solution.py:19
  81.1 3.3 %collective-permute-done.14 = bf16[640,128]{1,0:T(8,128)(2,1)S(1)} collective-permute-done((bf16[640,128]{1,0:T(8,128)(2,1)S(1)}, bf16[640,128]{1,0:T(8,128)(2,1)S(1)}, u32[]{:S(2)}, u32[]{:S(2)}) %collective-permute-start.14) | collective-permute-done | bytes 163872 | tf_op jit(solution)/shard_map/ppermute | solution.py:19
  84.4 1.5 %collective-permute-done.16 = bf16[640,128]{1,0:T(8,128)(2,1)S(1)} collective-permute-done((bf16[640,128]{1,0:T(8,128)(2,1)S(1)}, bf16[640,128]{1,0:T(8,128)(2,1)S(1)}, u32[]{:S(2)}, u32[]{:S(2)}) %collective-permute-start.16) | collective-permute-done | bytes 163872 | tf_op jit(solution)/shard_map/ppermute | solution.py:19
  85.9 3.0 %collective-permute-start.17 = (bf16[640,256]{1,0:T(8,128)(2,1)S(1)}, bf16[640,256]{1,0:T(8,128)(2,1)S(1)}, u32[]{:S(2)}, u32[]{:S(2)}) collective-permute-start(bf16[640,256]{1,0:T(8,128)(2,1)S(1)} %pad_maximum_fusion.refs_4_), channel_id=1, source_target_pairs={{0,1},{1,2},{2,3},{4,5},{5,6},{6,7},{8,9},{9,10},{10,11},{12,13},{... | collective-permute-start | bytes 983048 | tf_op jit(solution)/shard_map/ppermute | solution.py:285
  91.6 2.3 %collective-permute-done.17.refs_4_ = bf16[640,256]{1,0:T(8,128)(2,1)S(1)} collective-permute-done((bf16[640,256]{1,0:T(8,128)(2,1)S(1)}, bf16[640,256]{1,0:T(8,128)(2,1)S(1)}, u32[]{:S(2)}, u32[]{:S(2)}) %collective-permute-start.17) | collective-permute-done | bytes 327712 | tf_op jit(solution)/shard_map/ppermute | solution.py:285
  94.5 3.5 %collective-permute-done.21.refs_6_ = bf16[640,256]{1,0:T(8,128)(2,1)S(1)} collective-permute-done((bf16[640,256]{1,0:T(8,128)(2,1)S(1)}, bf16[640,256]{1,0:T(8,128)(2,1)S(1)}, u32[]{:S(2)}, u32[]{:S(2)}) %collective-permute-start.21) | collective-permute-done | bytes 327712 | tf_op jit(solution)/shard_map/ppermute | solution.py:286
  101.7 5.3 %collective-permute-done.22.refs_6_ = bf16[640,256]{1,0:T(8,128)(2,1)S(1)} collective-permute-done((bf16[640,256]{1,0:T(8,128)(2,1)S(1)}, bf16[640,256]{1,0:T(8,128)(2,1)S(1)}, u32[]{:S(2)}, u32[]{:S(2)}) %collective-permute-start.22) | collective-permute-done | bytes 327712 | tf_op jit(solution)/shard_map/ppermute | solution.py:286
  111.1 4.8 %collective-permute-done.23.refs_6_ = bf16[640,256]{1,0:T(8,128)(2,1)S(1)} collective-permute-done((bf16[640,256]{1,0:T(8,128)(2,1)S(1)}, bf16[640,256]{1,0:T(8,128)(2,1)S(1)}, u32[]{:S(2)}, u32[]{:S(2)}) %collective-permute-start.23) | collective-permute-done | bytes 327712 | tf_op jit(solution)/shard_map/ppermute | solution.py:286
  116.7 5.6 %attend.4.refs_8_ = bf16[128,4096]{1,0:T(8,128)(2,1)} custom-call(s32[1]{0:T(128)} %bitcast.28.refs_0_, bf16[128,4096]{1,0:T(8,128)(2,1)} %refs_1_.7, bf16[128,128]{1,0:T(8,128)(2,1)} %fusion.1.refs_2_, bf16[1280,128]{1,0:T(8,128)(2,1)} %pad.13.refs_3_, bf16[640,256]{1,0:T(8,128)(2,1)} %copy-done.2, bf16[640,256]{1,0:T(8,128)(2,1)} %copy-done.12), custom_call_target="tpu_custom_call" | custom-call | tf_op jit(solution)/shard_map/attend/pallas_call | solution.py:170
  122.3 5.9 %attend.5.refs_8_ = bf16[128,4096]{1,0:T(8,128)(2,1)} custom-call(s32[2]{0:T(128)} %pad_add_fusion.2.refs_0_, bf16[128,4096]{1,0:T(8,128)(2,1)} %refs_1_.7, bf16[128,128]{1,0:T(8,128)(2,1)} %fusion.1.refs_2_, bf16[1280,128]{1,0:T(8,128)(2,1)} %pad.13.refs_3_, bf16[640,256]{1,0:T(8,128)(2,1)} %copy-done.3, ...), custom_call_target="tpu_custom_call", output_to_operand_aliasing={{}: (8, {})} | custom-call | tf_op jit(solution)/shard_map/attend/pallas_call | solution.py:170
  128.9 5.7 %attend.6.refs_8_ = bf16[128,4096]{1,0:T(8,128)(2,1)} custom-call(s32[2]{0:T(128)} %pad_add_fusion.1.refs_0_, bf16[128,4096]{1,0:T(8,128)(2,1)} %refs_1_.7, bf16[128,128]{1,0:T(8,128)(2,1)} %fusion.1.refs_2_, bf16[1280,128]{1,0:T(8,128)(2,1)} %pad.13.refs_3_, bf16[640,256]{1,0:T(8,128)(2,1)} %copy-done.5, ...), custom_call_target="tpu_custom_call", output_to_operand_aliasing={{}: (8, {})} | custom-call | tf_op jit(solution)/shard_map/attend/pallas_call | solution.py:170
  135.3 5.9 %attend.7 = bf16[128,4096]{1,0:T(8,128)(2,1)} custom-call(s32[2]{0:T(128)} %pad_add_fusion.refs_0_, bf16[128,4096]{1,0:T(8,128)(2,1)} %refs_1_.7, bf16[128,128]{1,0:T(8,128)(2,1)} %fusion.1.refs_2_, bf16[1280,128]{1,0:T(8,128)(2,1)} %pad.13.refs_3_, bf16[640,256]{1,0:T(8,128)(2,1)} %copy-done.7, ...), custom_call_target="tpu_custom_call", output_to_operand_aliasing={{}: (8, {})} | custom-call | tf_op jit(solution)/shard_map/attend/pallas_call | solution.py:170
  (101 shorter events, 29.2 us)
Async XLA Ops:
  0.0 99.6 %copy-start = (s32[512,4]{0,1:T(4,128)S(1)}, s32[512,4]{0,1:T(4,128)}, u32[]{:S(2)}) copy-start(s32[512,4]{0,1:T(4,128)} %param.11) | copy-start | bytes 24580
  4.4 16.0 %collective-permute-start.9 = (f32[256,256]{1,0:T(8,128)S(1)}, f32[256,256]{1,0:T(8,128)}, u32[]{:S(2)}, u32[]{:S(2)}) collective-permute-start(f32[256,256]{1,0:T(8,128)S(1)} %get-tuple-element.15), channel_id=1, source_target_pairs={{3,2},{7,6},{11,10},{15,14},{19,18},{23,22},{27,26},{31,30}} | collective-permute-start | bytes 786440 | tf_op jit(solution)/shard_map/ppermute | solution.py:211
  5.8 17.9 %collective-permute-start.3 = (f32[256,256]{1,0:T(8,128)S(1)}, f32[256,256]{1,0:T(8,128)S(1)}, u32[]{:S(2)}, u32[]{:S(2)}) collective-permute-start(f32[256,256]{1,0:T(8,128)S(1)} %get-tuple-element.15), channel_id=1, source_target_pairs={{0,1},{4,5},{8,9},{12,13},{16,17},{20,21},{24,25},{28,29}} | collective-permute-start | bytes 786440 | tf_op jit(solution)/shard_map/ppermute | solution.py:210
  10.8 12.9 %collective-permute-start = (f32[256,256]{1,0:T(8,128)S(1)}, f32[256,256]{1,0:T(8,128)S(1)}, u32[]{:S(2)}, u32[]{:S(2)}) collective-permute-start(f32[256,256]{1,0:T(8,128)S(1)} %get-tuple-element.16), channel_id=1, source_target_pairs={{0,1},{4,5},{8,9},{12,13},{16,17},{20,21},{24,25},{28,29}} | collective-permute-start | bytes 786440 | tf_op jit(solution)/shard_map/ppermute | solution.py:210
  12.1 11.6 %collective-permute-start.6 = (f32[256,256]{1,0:T(8,128)S(1)}, f32[256,256]{1,0:T(8,128)S(1)}, u32[]{:S(2)}, u32[]{:S(2)}) collective-permute-start(f32[256,256]{1,0:T(8,128)S(1)} %get-tuple-element.16), channel_id=1, source_target_pairs={{3,2},{7,6},{11,10},{15,14},{19,18},{23,22},{27,26},{31,30}} | collective-permute-start | bytes 786440 | tf_op jit(solution)/shard_map/ppermute | solution.py:211
  22.3 2.1 %collective-permute-start.10 = (f32[256,256]{1,0:T(8,128)}, f32[256,256]{1,0:T(8,128)}, u32[]{:S(2)}, u32[]{:S(2)}) collective-permute-start(f32[256,256]{1,0:T(8,128)} %bitcast_add_fusion), channel_id=1, source_target_pairs={{3,2},{2,1},{7,6},{6,5},{11,10},{10,9},{15,14},{14,13},{19,18},{18... | collective-permute-start | bytes 786440 | tf_op jit(solution)/shard_map/ppermute | solution.py:211
  23.7 34.0 %copy-start.17 = (s32[4]{0:T(128)S(1)}, s32[4]{0:T(128)}, u32[]{:S(2)}) copy-start(s32[4]{0:T(128)} %param.13) | copy-start | bytes 52
  26.7 16.4 %collective-permute-start.1 = (f32[256,256]{1,0:T(8,128)}, f32[256,256]{1,0:T(8,128)S(1)}, u32[]{:S(2)}, u32[]{:S(2)}) collective-permute-start(f32[256,256]{1,0:T(8,128)} %get-tuple-element.11), channel_id=1, source_target_pairs={{0,1},{1,2},{4,5},{5,6},{8,9},{9,10},{12,13},{13,14},{16,17},{17,1... | collective-permute-start | bytes 786440 | tf_op jit(solution)/shard_map/ppermute | solution.py:210
  36.1 10.5 %collective-permute-start.4 = (f32[256,256]{1,0:T(8,128)S(1)}, f32[256,256]{1,0:T(8,128)S(1)}, u32[]{:S(2)}, u32[]{:S(2)}) collective-permute-start(f32[256,256]{1,0:T(8,128)S(1)} %get-tuple-element.10), channel_id=1, source_target_pairs={{0,1},{1,2},{4,5},{5,6},{8,9},{9,10},{12,13},{13,14},{16,17},{17,1... | collective-permute-start | bytes 786440 | tf_op jit(solution)/shard_map/ppermute | solution.py:210
  39.6 7.0 %collective-permute-start.7 = (f32[256,256]{1,0:T(8,128)S(1)}, f32[256,256]{1,0:T(8,128)}, u32[]{:S(2)}, u32[]{:S(2)}) collective-permute-start(f32[256,256]{1,0:T(8,128)S(1)} %get-tuple-element.9), channel_id=1, source_target_pairs={{3,2},{2,1},{7,6},{6,5},{11,10},{10,9},{15,14},{14,13},{19,18},{18... | collective-permute-start | bytes 786440 | tf_op jit(solution)/shard_map/ppermute | solution.py:211
  41.2 20.0 %collective-permute-start.11 = (f32[256,256]{1,0:T(8,128)S(1)}, f32[256,256]{1,0:T(8,128)}, u32[]{:S(2)}, u32[]{:S(2)}) collective-permute-start(f32[256,256]{1,0:T(8,128)S(1)} %get-tuple-element.8), channel_id=1, source_target_pairs={{3,2},{2,1},{1,0},{7,6},{6,5},{5,4},{11,10},{10,9},{9,8},{15,14},{... | collective-permute-start | bytes 786440 | tf_op jit(solution)/shard_map/ppermute | solution.py:211
  48.4 12.8 %collective-permute-start.2 = (f32[256,256]{1,0:T(8,128)}, f32[256,256]{1,0:T(8,128)S(1)}, u32[]{:S(2)}, u32[]{:S(2)}) collective-permute-start(f32[256,256]{1,0:T(8,128)} %get-tuple-element.14), channel_id=1, source_target_pairs={{0,1},{1,2},{2,3},{4,5},{5,6},{6,7},{8,9},{9,10},{10,11},{12,13},{... | collective-permute-start | bytes 786440 | tf_op jit(solution)/shard_map/ppermute | solution.py:210
  54.5 8.2 %collective-permute-start.5 = (f32[256,256]{1,0:T(8,128)S(1)}, f32[256,256]{1,0:T(8,128)S(1)}, u32[]{:S(2)}, u32[]{:S(2)}) collective-permute-start(f32[256,256]{1,0:T(8,128)S(1)} %get-tuple-element.13), channel_id=1, source_target_pairs={{0,1},{1,2},{2,3},{4,5},{5,6},{6,7},{8,9},{9,10},{10,11},{12,13},{... | collective-permute-start | bytes 786440 | tf_op jit(solution)/shard_map/ppermute | solution.py:210
  56.4 8.4 %collective-permute-start.8 = (f32[256,256]{1,0:T(8,128)S(1)}, f32[256,256]{1,0:T(8,128)}, u32[]{:S(2)}, u32[]{:S(2)}) collective-permute-start(f32[256,256]{1,0:T(8,128)S(1)} %get-tuple-element.12), channel_id=1, source_target_pairs={{3,2},{2,1},{1,0},{7,6},{6,5},{5,4},{11,10},{10,9},{9,8},{15,14},{... | collective-permute-start | bytes 786440 | tf_op jit(solution)/shard_map/ppermute | solution.py:211
  68.6 1.7 %collective-permute-start.12 = (bf16[640,256]{1,0:T(8,128)(2,1)S(1)}, bf16[640,256]{1,0:T(8,128)(2,1)S(1)}, u32[]{:S(2)}, u32[]{:S(2)}) collective-permute-start(bf16[640,256]{1,0:T(8,128)(2,1)S(1)} %slice_bitcast_fusion), channel_id=1, source_target_pairs={{0,4},{4,0},{8,12},{12,8},{16,20},{20,16},{24,28},{28,24},{1,5},{5... | collective-permute-start | bytes 983048 | tf_op jit(solution)/shard_map/ppermute | solution.py:19
  71.4 6.3 %collective-permute-start.13 = (bf16[640,128]{1,0:T(8,128)(2,1)S(1)}, bf16[640,128]{1,0:T(8,128)(2,1)S(1)}, u32[]{:S(2)}, u32[]{:S(2)}) collective-permute-start(bf16[640,128]{1,0:T(8,128)(2,1)S(1)} %get-tuple-element.19), channel_id=1, source_target_pairs={{0,8},{4,12},{8,0},{12,4},{16,24},{20,28},{24,16},{28,20},{1,9},{5... | collective-permute-start | bytes 491528 | tf_op jit(solution)/shard_map/ppermute | solution.py:19
  72.9 6.0 %collective-permute-start.15 = (bf16[640,128]{1,0:T(8,128)(2,1)S(1)}, bf16[640,128]{1,0:T(8,128)(2,1)S(1)}, u32[]{:S(2)}, u32[]{:S(2)}) collective-permute-start(bf16[640,128]{1,0:T(8,128)(2,1)S(1)} %get-tuple-element.20), channel_id=1, source_target_pairs={{0,16},{4,20},{8,24},{12,28},{16,0},{20,4},{24,8},{28,12},{1,17},{... | collective-permute-start | bytes 491528 | tf_op jit(solution)/shard_map/ppermute | solution.py:19
  78.9 5.4 %collective-permute-start.14 = (bf16[640,128]{1,0:T(8,128)(2,1)S(1)}, bf16[640,128]{1,0:T(8,128)(2,1)S(1)}, u32[]{:S(2)}, u32[]{:S(2)}) collective-permute-start(bf16[640,128]{1,0:T(8,128)(2,1)S(1)} %get-tuple-element.17), channel_id=1, source_target_pairs={{0,16},{4,20},{8,24},{12,28},{16,0},{20,4},{24,8},{28,12},{1,17},{... | collective-permute-start | bytes 491528 | tf_op jit(solution)/shard_map/ppermute | solution.py:19
  80.5 5.3 %collective-permute-start.16 = (bf16[640,128]{1,0:T(8,128)(2,1)S(1)}, bf16[640,128]{1,0:T(8,128)(2,1)S(1)}, u32[]{:S(2)}, u32[]{:S(2)}) collective-permute-start(bf16[640,128]{1,0:T(8,128)(2,1)S(1)} %get-tuple-element.18), channel_id=1, source_target_pairs={{0,8},{4,12},{8,0},{12,4},{16,24},{20,28},{24,16},{28,20},{1,9},{5... | collective-permute-start | bytes 491528 | tf_op jit(solution)/shard_map/ppermute | solution.py:19
  85.9 7.9 %collective-permute-start.17 = (bf16[640,256]{1,0:T(8,128)(2,1)S(1)}, bf16[640,256]{1,0:T(8,128)(2,1)S(1)}, u32[]{:S(2)}, u32[]{:S(2)}) collective-permute-start(bf16[640,256]{1,0:T(8,128)(2,1)S(1)} %pad_maximum_fusion.refs_4_), channel_id=1, source_target_pairs={{0,1},{1,2},{2,3},{4,5},{5,6},{6,7},{8,9},{9,10},{10,11},{12,13},{... | collective-permute-start | bytes 983048 | tf_op jit(solution)/shard_map/ppermute | solution.py:285
  88.9 9.1 %collective-permute-start.21 = (bf16[640,256]{1,0:T(8,128)(2,1)S(1)}, bf16[640,256]{1,0:T(8,128)(2,1)S(1)}, u32[]{:S(2)}, u32[]{:S(2)}) collective-permute-start(bf16[640,256]{1,0:T(8,128)(2,1)S(1)} %pad_maximum_fusion.refs_4_), channel_id=1, source_target_pairs={{3,2},{2,1},{1,0},{7,6},{6,5},{5,4},{11,10},{10,9},{9,8},{15,14},{... | collective-permute-start | bytes 983048 | tf_op jit(solution)/shard_map/ppermute | solution.py:286
  93.9 7.2 %collective-permute-start.18 = (bf16[640,256]{1,0:T(8,128)(2,1)S(1)}, bf16[640,256]{1,0:T(8,128)(2,1)S(1)}, u32[]{:S(2)}, u32[]{:S(2)}) collective-permute-start(bf16[640,256]{1,0:T(8,128)(2,1)S(1)} %collective-permute-done.17.refs_4_), channel_id=1, source_target_pairs={{1,2},{2,3},{5,6},{6,7},{9,10},{10,11},{13,14},{14,15},{17,18},{18... | collective-permute-start | bytes 983048 | tf_op jit(solution)/shard_map/ppermute | solution.py:285
  98.0 9.0 %collective-permute-start.22 = (bf16[640,256]{1,0:T(8,128)(2,1)S(1)}, bf16[640,256]{1,0:T(8,128)(2,1)S(1)}, u32[]{:S(2)}, u32[]{:S(2)}) collective-permute-start(bf16[640,256]{1,0:T(8,128)(2,1)S(1)} %collective-permute-done.21.refs_6_), channel_id=1, source_target_pairs={{2,1},{1,0},{6,5},{5,4},{10,9},{9,8},{14,13},{13,12},{18,17},{17,1... | collective-permute-start | bytes 983048 | tf_op jit(solution)/shard_map/ppermute | solution.py:286
  100.5 9.6 %collective-permute-start.29 = (bf16[640,256]{1,0:T(8,128)(2,1)S(1)}, bf16[640,256]{1,0:T(8,128)(2,1)S(1)}, u32[]{:S(2)}, u32[]{:S(2)}) collective-permute-start(bf16[640,256]{1,0:T(8,128)(2,1)S(1)} %pad_maximum_fusion.refs_4_), channel_id=1, source_target_pairs={{0,4},{4,0},{8,12},{12,8},{16,20},{20,16},{24,28},{28,24},{1,5},{5... | collective-permute-start | bytes 983048 | tf_op jit(solution)/shard_map/ppermute | solution.py:19
  100.5 10.1 %collective-permute-start.27 = (bf16[640,256]{1,0:T(8,128)(2,1)S(1)}, bf16[640,256]{1,0:T(8,128)(2,1)S(1)}, u32[]{:S(2)}, u32[]{:S(2)}) collective-permute-start(bf16[640,256]{1,0:T(8,128)(2,1)S(1)} %collective-permute-done.17.refs_4_), channel_id=1, source_target_pairs={{0,4},{4,0},{8,12},{12,8},{16,20},{20,16},{24,28},{28,24},{1,5},{5... | collective-permute-start | bytes 983048 | tf_op jit(solution)/shard_map/ppermute | solution.py:19
  101.0 9.6 %collective-permute-start.19 = (bf16[640,256]{1,0:T(8,128)(2,1)S(1)}, bf16[640,256]{1,0:T(8,128)(2,1)S(1)}, u32[]{:S(2)}, u32[]{:S(2)}) collective-permute-start(bf16[640,256]{1,0:T(8,128)(2,1)S(1)} %collective-permute-done.18.refs_4_), channel_id=1, source_target_pairs={{2,3},{6,7},{10,11},{14,15},{18,19},{22,23},{26,27},{30,31}} | collective-permute-start | bytes 983048 | tf_op jit(solution)/shard_map/ppermute | solution.py:285
  107.0 9.0 %collective-permute-start.23 = (bf16[640,256]{1,0:T(8,128)(2,1)S(1)}, bf16[640,256]{1,0:T(8,128)(2,1)S(1)}, u32[]{:S(2)}, u32[]{:S(2)}) collective-permute-start(bf16[640,256]{1,0:T(8,128)(2,1)S(1)} %collective-permute-done.22.refs_6_), channel_id=1, source_target_pairs={{1,0},{5,4},{9,8},{13,12},{17,16},{21,20},{25,24},{29,28}} | collective-permute-start | bytes 983048 | tf_op jit(solution)/shard_map/ppermute | solution.py:286
  110.0 12.2 %collective-permute-start.28 = (bf16[640,256]{1,0:T(8,128)(2,1)S(1)}, bf16[640,256]{1,0:T(8,128)(2,1)}, u32[]{:S(2)}, u32[]{:S(2)}) collective-permute-start(bf16[640,256]{1,0:T(8,128)(2,1)S(1)} %collective-permute-done.21.refs_6_), channel_id=1, source_target_pairs={{0,4},{4,0},{8,12},{12,8},{16,20},{20,16},{24,28},{28,24},{1,5},{5... | collective-permute-start | bytes 983048 | tf_op jit(solution)/shard_map/ppermute | solution.py:19
  110.1 18.1 %collective-permute-start.25 = (bf16[640,256]{1,0:T(8,128)(2,1)S(1)}, bf16[640,256]{1,0:T(8,128)(2,1)S(1)}, u32[]{:S(2)}, u32[]{:S(2)}) collective-permute-start(bf16[640,256]{1,0:T(8,128)(2,1)S(1)} %collective-permute-done.18.refs_4_), channel_id=1, source_target_pairs={{0,4},{4,0},{8,12},{12,8},{16,20},{20,16},{24,28},{28,24},{1,5},{5... | collective-permute-start | bytes 983048 | tf_op jit(solution)/shard_map/ppermute | solution.py:19
  110.6 17.6 %collective-permute-start.26 = (bf16[640,256]{1,0:T(8,128)(2,1)S(1)}, bf16[640,256]{1,0:T(8,128)(2,1)}, u32[]{:S(2)}, u32[]{:S(2)}) collective-permute-start(bf16[640,256]{1,0:T(8,128)(2,1)S(1)} %collective-permute-done.22.refs_6_), channel_id=1, source_target_pairs={{0,4},{4,0},{8,12},{12,8},{16,20},{20,16},{24,28},{28,24},{1,5},{5... | collective-permute-start | bytes 983048 | tf_op jit(solution)/shard_map/ppermute | solution.py:19
  110.7 24.0 %collective-permute-start.20 = (bf16[640,256]{1,0:T(8,128)(2,1)S(1)}, bf16[640,256]{1,0:T(8,128)(2,1)S(1)}, u32[]{:S(2)}, u32[]{:S(2)}) collective-permute-start(bf16[640,256]{1,0:T(8,128)(2,1)S(1)} %collective-permute-done.19.refs_4_), channel_id=1, source_target_pairs={{0,4},{4,0},{8,12},{12,8},{16,20},{20,16},{24,28},{28,24},{1,5},{5... | collective-permute-start | bytes 983048 | tf_op jit(solution)/shard_map/ppermute | solution.py:19
  115.9 18.7 %collective-permute-start.24 = (bf16[640,256]{1,0:T(8,128)(2,1)S(1)}, bf16[640,256]{1,0:T(8,128)(2,1)}, u32[]{:S(2)}, u32[]{:S(2)}) collective-permute-start(bf16[640,256]{1,0:T(8,128)(2,1)S(1)} %collective-permute-done.23.refs_6_), channel_id=1, source_target_pairs={{0,4},{4,0},{8,12},{12,8},{16,20},{20,16},{24,28},{28,24},{1,5},{5... | collective-permute-start | bytes 983048 | tf_op jit(solution)/shard_map/ppermute | solution.py:19
  (16 other events, 233.7 us)

commit v2 on v1

v2 whole, which is shorter than its diff:
```python
import math

import jax
import jax.numpy as jnp
from jax import lax
from jax.experimental import pallas as pl
from jax.experimental.pallas import tpu as pltpu
from jax.sharding import PartitionSpec as P

EPSILON = 1e-05
FLOOR_SCORE = -1e30
KV_TOTAL = 1280
PIECES = 2
MIB = 2**20

VMEM = pl.BlockSpec(memory_space=pltpu.VMEM)
SMEM = pl.BlockSpec(memory_space=pltpu.SMEM)
ANYWHERE = pl.BlockSpec(memory_space=pl.ANY)


def params(mib):
    return pltpu.CompilerParams(vmem_limit_bytes=mib * MIB)


def swapped(value, axis, bit):
    mask = 2**bit
    pairs = [(source, source ^ mask) for source in range(lax.axis_size(axis))]
    return lax.ppermute(value, axis, pairs)


def project(chunk_ids, vis_feats, kv_weight, chunk_count, pair):
    rows, width = vis_feats.shape
    wanted = chunk_ids.shape[0]
    per_kv = chunk_count // (kv_weight.shape[1] // pair)
    block_rows = rows // per_kv
    sub = block_rows // PIECES

    def kernel(ids_ref, feats_ref, weight_ref, *refs):
        out_refs, (buffer, sems) = refs[: wanted * PIECES], refs[wanted * PIECES :]

        def fetch(n):
            column = pl.multiple_of((ids_ref[n] // per_kv) * pair, pair)
            return pltpu.make_async_copy(
                weight_ref.at[:, pl.ds(column, pair)], buffer.at[n % 2], sems.at[n % 2]
            )

        fetch(0).start()
        for n in range(wanted):
            if n + 1 < wanted:
                fetch(n + 1).start()
            fetch(n).wait()
            for piece in range(PIECES):
                row = (ids_ref[n] % per_kv) * block_rows + piece * sub if per_kv > 1 else piece * sub
                row = row if per_kv == 1 else pl.multiple_of(row, sub)
                out_refs[n * PIECES + piece][...] = jnp.dot(
                    feats_ref[pl.ds(row, sub), :], buffer[n % 2], preferred_element_type=jnp.float32
                )

    flat = pl.pallas_call(
        kernel,
        in_specs=[SMEM, VMEM, ANYWHERE],
        out_specs=[VMEM] * (wanted * PIECES),
        out_shape=[jax.ShapeDtypeStruct((sub, pair), jnp.float32)] * (wanted * PIECES),
        scratch_shapes=[
            pltpu.VMEM((2, width, pair), kv_weight.dtype),
            pltpu.SemaphoreType.DMA((2,)),
        ],
        compiler_params=params(16),
        cost_estimate=pl.CostEstimate(
            flops=2 * wanted * block_rows * width * pair,
            bytes_accessed=wanted * width * pair * 2,
            transcendentals=0,
        ),
        name="project",
    )(chunk_ids, vis_feats, kv_weight)
    return [flat[n * PIECES : (n + 1) * PIECES] for n in range(wanted)]


def sum_over_head(vis_feats, kv_weight, pair):
    count = lax.axis_size("head")
    here = lax.axis_index("head")

    def parts_at(offsets):
        ids = jnp.stack([(here + offset) % count for offset in offsets]).astype(jnp.int32)
        return dict(zip(offsets, project(ids, vis_feats, kv_weight, count, pair)))

    ends = project((count - 1 - here)[None].astype(jnp.int32), vis_feats, kv_weight, count, pair)[0]
    parts = {}
    for hop in list(range(2, count)) + [count]:
        fresh = [o % count for o in dict.fromkeys((count - hop, hop)) if o % count not in parts]
        if hop == 2 or count > 4:
            if fresh:
                parts.update(parts_at(fresh))
        elif hop == 3:
            parts.update(parts_at(fresh + [0]))
    if 0 not in parts:
        parts.update(parts_at([0]))

    to_right, to_left = [None] * PIECES, [None] * PIECES
    for hop in range(1, count):
        senders = range(min(hop, count - 1))
        right_pairs = [(i, i + 1) for i in senders]
        left_pairs = [(count - 1 - i, count - 2 - i) for i in senders]
        for piece in range(PIECES):
            if hop == 1 and count > 3:
                arrived = lax.ppermute(ends[piece], "head", right_pairs + left_pairs)
                to_right[piece] = to_left[piece] = arrived
                continue
            if hop == 1:
                right = left = ends[piece]
            elif hop == 2 and count == 4:
                right = left = parts[2][piece] + to_right[piece]
            else:
                right = parts[count - hop][piece] + to_right[piece]
                left = parts[hop][piece] + to_left[piece]
            to_right[piece] = lax.ppermute(right, "head", right_pairs)
            to_left[piece] = lax.ppermute(left, "head", left_pairs)
    return parts[0], to_right, to_left


def finish_chunk(own, from_left, from_right, key_gain, image_tokens, image_owner, per_kv):
    rows, width = own[0].shape
    rows = rows * PIECES
    head_dim = width // 2
    half = KV_TOTAL // 2
    images = image_owner.shape[0]
    place = jnp.stack([lax.axis_index("ctx"), lax.axis_index("head") % per_kv]).astype(jnp.int32)

    def kernel(*refs):
        place_ref, tokens_ref, owner_ref = refs[:3]
        own_refs = refs[3 : 3 + PIECES]
        left_refs = refs[3 + PIECES : 3 + 2 * PIECES]
        right_refs = refs[3 + 2 * PIECES : 3 + 3 * PIECES]
        gain_ref, mine_ref, other_ref = refs[3 + 3 * PIECES :]
        placed = []
        for piece in range(PIECES):
            total = own_refs[piece][...] + left_refs[piece][...] + right_refs[piece][...]
            raw = total[:, :head_dim]
            mean = jnp.mean(raw * raw, axis=-1, keepdims=True)
            keys = raw * lax.rsqrt(mean + EPSILON) * gain_ref[...]
            placed.append(jnp.concatenate([keys, total[:, head_dim:]], axis=1).astype(jnp.bfloat16))
        data = jnp.concatenate(placed, axis=0)
        ctx = place_ref[0]
        start, count, before = jnp.int32(0), jnp.int32(0), jnp.int32(0)
        for i in range(images):
            here = owner_ref[i] == ctx
            start = jnp.where(here, before, start)
            count = jnp.where(here, tokens_ref[i], count)
            before = before + tokens_ref[i]
        token = lax.broadcasted_iota(jnp.int32, (half, rows), 1) + place_ref[1] * rows
        token = jnp.where(token < count, token, -2 * KV_TOTAL)
        row = lax.broadcasted_iota(jnp.int32, (half, rows), 0)
        core = ctx % 2
        for ref, side in ((other_ref, 1 - core), (mine_ref, core)):
            match = (row + (side * half - start)) == token
            chosen = jnp.where(match, 1.0, 0.0).astype(jnp.bfloat16)
            ref[...] = jnp.dot(chosen, data, preferred_element_type=jnp.float32).astype(jnp.bfloat16)

    return pl.pallas_call(
        kernel,
        in_specs=[SMEM] * 3 + [VMEM] * (3 * PIECES + 1),
        out_specs=[VMEM] * 2,
        out_shape=[jax.ShapeDtypeStruct((half, width), jnp.bfloat16)] * 2,
        compiler_params=params(16),
        cost_estimate=pl.CostEstimate(
            flops=4 * half * rows * width, bytes_accessed=12 * rows * width, transcendentals=0
        ),
        name="finish",
    )(place, image_tokens, image_owner, *own, *from_left, *from_right, key_gain[None, :])


def mask_columns(cross_mask, image_tokens, head_dim, rows):
    images = image_tokens.shape[0]
    row_slice = lax.dynamic_slice_in_dim(cross_mask, lax.axis_index("head") * rows, rows, 0)
    row_mask = jnp.pad(
        1.0 - row_slice.astype(jnp.float32), ((0, 0), (0, head_dim - images)), constant_values=1.0
    ).astype(jnp.bfloat16)

    def kernel(tokens_ref, out_ref):
        row = lax.broadcasted_iota(jnp.int32, out_ref.shape, 0)
        column = lax.broadcasted_iota(jnp.int32, out_ref.shape, 1)
        before = jnp.int32(0)
        bias = jnp.zeros(out_ref.shape, jnp.float32)
        for i in range(images + 1):
            after = before + tokens_ref[i] if i < images else jnp.int32(KV_TOTAL)
            inside = (column == i) & (row >= before) & (row < after)
            bias = jnp.where(inside, FLOOR_SCORE, bias)
            before = after
        out_ref[...] = bias.astype(jnp.bfloat16)

    token_bias = pl.pallas_call(
        kernel,
        in_specs=[SMEM],
        out_specs=VMEM,
        out_shape=jax.ShapeDtypeStruct((KV_TOTAL, head_dim), jnp.bfloat16),
        compiler_params=params(8),
        name="token_bias",
    )(image_tokens)
    return row_mask, token_bias


def attend(head_ids, blocks, queries, row_mask, token_bias, kv_heads, images, previous):
    rows, width = queries.shape
    count = len(blocks)
    head_dim = blocks[0].shape[1] // 2
    block_width = width // kv_heads
    group = block_width // head_dim
    factor = head_dim ** (-0.5) * math.log2(math.e)
    stack = min(2, group)

    def kernel(*refs):
        ids_ref, queries_ref, mask_ref, bias_ref = refs[:4]
        block_refs = refs[4 : 4 + count]
        out_ref, keys_ref, query_ref, result_ref, sems = refs[4 + count + (previous is not None) :]
        keys_ref[:, head_dim:] = bias_ref[...]
        some = jnp.min(mask_ref[:, :images].astype(jnp.float32), axis=1, keepdims=True) < 0.5
        for n in range(count):

            @pl.when(ids_ref[n] >= 0)
            def _():
                column = pl.multiple_of(ids_ref[n] * block_width, block_width)
                fetch = pltpu.make_async_copy(
                    queries_ref.at[:, pl.ds(column, block_width)], query_ref, sems.at[0]
                )
                fetch.start()
                keys_ref[:, :head_dim] = block_refs[n][:, :head_dim]
                fetch.wait()
                for first in range(0, group, stack):
                    left = jnp.concatenate(
                        [
                            jnp.concatenate(
                                [query_ref[:, j * head_dim : (j + 1) * head_dim], mask_ref[...]],
                                axis=1,
                            )
                            for j in range(first, first + stack)
                        ],
                        axis=0,
                    )
                    scores = lax.dot_general(
                        left,
                        keys_ref[...],
                        (((1,), (1,)), ((), ())),
                        preferred_element_type=jnp.float32,
                    )
                    largest = jnp.max(scores, axis=1, keepdims=True)
                    weights = jnp.exp2((scores - largest) * factor)
                    summed = jnp.sum(weights, axis=1, keepdims=True)
                    mixed = jnp.dot(
                        weights.astype(jnp.bfloat16),
                        block_refs[n][:, head_dim:],
                        preferred_element_type=jnp.float32,
                    )
                    mixed = mixed / jnp.maximum(summed, 1.0)
                    for j in range(stack):
                        one = jnp.where(some, mixed[j * rows : (j + 1) * rows], 0.0)
                        at = (first + j) * head_dim
                        result_ref[:, at : at + head_dim] = one.astype(jnp.bfloat16)
                store = pltpu.make_async_copy(
                    result_ref, out_ref.at[:, pl.ds(column, block_width)], sems.at[1]
                )
                store.start()
                store.wait()

    operands = [head_ids, queries, row_mask, token_bias, *blocks]
    in_specs = [SMEM, ANYWHERE] + [VMEM] * (2 + count)
    aliases = {}
    if previous is not None:
        aliases = {len(operands): 0}
        operands.append(previous)
        in_specs.append(ANYWHERE)
    return pl.pallas_call(
        kernel,
        in_specs=in_specs,
        out_specs=ANYWHERE,
        out_shape=jax.ShapeDtypeStruct((rows, width), jnp.bfloat16),
        scratch_shapes=[
            pltpu.VMEM((KV_TOTAL, 2 * head_dim), jnp.bfloat16),
            pltpu.VMEM((rows, block_width), jnp.bfloat16),
            pltpu.VMEM((rows, block_width), jnp.bfloat16),
            pltpu.SemaphoreType.DMA((2,)),
        ],
        input_output_aliases=aliases,
        compiler_params=params(24),
        cost_estimate=pl.CostEstimate(
            flops=6 * count * rows * group * KV_TOTAL * head_dim,
            bytes_accessed=count * rows * block_width * 4,
            transcendentals=count * rows * group * KV_TOTAL,
        ),
        name="attend",
    )(*operands)


def shards(queries, vis_feats, kv_weight, key_gain, cross_mask, image_tokens, image_owner):
    head_count = lax.axis_size("head")
    head_index = lax.axis_index("head")
    ctx_count = lax.axis_size("ctx")
    core = lax.axis_index("ctx") % 2
    ctx_bits = ctx_count.bit_length() - 1
    head_dim = key_gain.shape[0]
    kv_heads = kv_weight.shape[1] // (2 * head_dim)
    per_kv = head_count // kv_heads
    rows = queries.shape[0]

    row_mask, token_bias = mask_columns(cross_mask, image_tokens, head_dim, rows)
    own, from_left, from_right = sum_over_head(vis_feats, kv_weight, 2 * head_dim)
    block, other = finish_chunk(
        own, from_left, from_right, key_gain, image_tokens, image_owner, per_kv
    )
    if per_kv > 1:
        groups = [[k * per_kv + j for j in range(per_kv)] for k in range(kv_heads)]
        block, other = lax.psum((block, other), "head", axis_index_groups=groups)

    block = block + swapped(other, "ctx", 0)
    for step in range(1, ctx_bits):
        pairs = [(c, c ^ (2**step if c % 2 == 0 else 2 ** (ctx_bits - step))) for c in range(ctx_count)]
        block = block + lax.ppermute(block, "ctx", pairs)
    other = swapped(block, "ctx", 0)
    block = jnp.where(
        core == 0, jnp.concatenate([block, other], 0), jnp.concatenate([other, block], 0)
    )

    def run(ids, blocks, previous):
        ids = jnp.stack(ids).astype(jnp.int32)
        return attend(
            ids, blocks, queries, row_mask, token_bias, kv_heads, image_tokens.shape[0], previous
        )

    if per_kv > 1:
        groups = [[k * per_kv + j for k in range(kv_heads)] for j in range(per_kv)]
        gathered = lax.all_gather(block, "head", axis_index_groups=groups)
        out = None
        for k in range(kv_heads):
            out = run([jnp.int32(k)], [gathered[k]], out)
        return out

    def place(c, h):
        return c * head_count + h

    out = run([head_index], [block], None)
    passing = block
    side = 1 - 2 * core
    for hop in range(1, head_count):
        pairs = []
        for c in range(ctx_count):
            for i in range(hop - 1, head_count - 1):
                if c % 2 == 0:
                    pairs.append((place(c, i), place(c, i + 1)))
                else:
                    pairs.append((place(c, head_count - 1 - i), place(c, head_count - 2 - i)))
        passing = lax.ppermute(passing, ("ctx", "head"), pairs)
        passing, out = lax.optimization_barrier((passing, out))
        ids = [head_index - hop * side, head_index + hop * side]
        ids = [jnp.where((i >= 0) & (i < head_count), i, -1) for i in ids]
        out = run(ids, [passing, swapped(passing, "ctx", 0)], out)
    return out


def solution(mesh):
    return jax.shard_map(
        shards,
        mesh=mesh,
        in_specs=(
            P(("ctx", "head"), None),
            P("ctx", "head"),
            P("head", None),
            P(),
            P("ctx", None),
            P(),
            P(),
        ),
        out_specs=P(("ctx", "head"), None),
        check_vma=False,
    )
```

time: 142 us -> 114 us (0.80)
  Pallas kernels: 36.3 us -> 23 us
  other arithmetic: 11.4 us -> 1.14 us
  local copies, waits for them, and re-layouts: 9.23 us -> 6.14 us
    pallas_call x7 -> x9, Pallas kernels: 36.3 us -> 23 us  [the longest x4 16 us: attend(): pl.pallas_call(kernel, in_specs=in_specs, out_specs=ANYWHERE, out_shape=j...]
    ppermute x6 -> x4, starting transfers between devices: 27.2 us -> 19.1 us  [sum_over_head(): to_right[piece] = lax.ppermute(right, 'head', right_pairs)]
    add x7 -> x9, other arithmetic: 7.11 us -> 0.47 us  [the longest x2 0.17 us: shards(): block = block + lax.ppermute(block, 'ctx', pairs)]
    ppermute x12 -> x5, starting transfers between devices: 6.79 us -> 12.3 us  [swapped(): return lax.ppermute(value, axis, pairs)]
    ppermute x6 -> x7, starting transfers between devices: 8.16 us -> 13.7 us  [the longest x2 6.28 us: sum_over_head(): arrived = lax.ppermute(ends[piece], 'head', right_pairs + left_pairs)]
    ppermute x6 -> x4, waiting for transfers between devices: 2.15 us -> 7.16 us  [sum_over_head(): to_left[piece] = lax.ppermute(left, 'head', left_pairs)]
    ppermute x12 -> x5, waiting for transfers between devices: 10.8 us -> 6.72 us  [swapped(): return lax.ppermute(value, axis, pairs)]
    unnamed x37 -> x21, local copies, waits for them, and re-layouts: 2.29 us -> 6.12 us
  transfers between devices with their start and end apart: 30 -> 20, of which waited for: 13 -> 13; matrix products, arithmetic and copies ran while one was open for 9% -> 1% of each run, Pallas kernels for 17% -> 15%
where the time goes in v2:
time: 114 us
  starting transfers between devices  49 us (43%)
  waiting for transfers between devices  33.7 us (30%)
  Pallas kernels  23 us (20%)
  local copies, waits for them, and re-layouts  6.14 us (5%)
    ppermute x4, starting transfers between devices, sum_over_head(): to_right[piece] = lax.ppermute(right, 'head', right_pairs)  19.1 us
    pallas_call x4, Pallas kernels, attend(): pl.pallas_call(kernel, in_specs=in_specs, out_specs=ANYWHERE, out_shape=j...  16 us
    ppermute x5, starting transfers between devices, swapped(): return lax.ppermute(value, axis, pairs)  12.3 us
    ppermute x2, waiting for transfers between devices, shards(): block = block + lax.ppermute(block, 'ctx', pairs)  11.1 us
    ppermute x4, waiting for transfers between devices, sum_over_head(): to_left[piece] = lax.ppermute(left, 'head', left_pairs)  7.16 us
    ppermute x5, waiting for transfers between devices, swapped(): return lax.ppermute(value, axis, pairs)  6.72 us
    ppermute x2, starting transfers between devices, sum_over_head(): arrived = lax.ppermute(ends[piece], 'head', right_pairs + left_pairs)  6.28 us
    unnamed x21, local copies, waits for them, and re-layouts  6.12 us
  transfers between devices with their start and end apart: 20, of which 13 were waited for; matrix products, arithmetic and copies ran while one was open for 1% of the time, Pallas kernels for 15%

profile of v2, /device:TPU:0, one launch (start us, length us, event | category | flops | bytes accessed | tf_op | source)
XLA Modules:
  0.0 113.6 jit_solution(7152442188688901847)
XLA Ops:
  0.0 2.2 %copy-done.1 = bf16[2048,1024]{1,0:T(8,128)(2,1)S(1)} copy-done((bf16[2048,1024]{1,0:T(8,128)(2,1)S(1)}, bf16[2048,1024]{1,0:T(8,128)(2,1)}, u32[]{:S(2)}) %copy-start.1) | copy-done | bytes 4194328
  2.2 1.6 %copy-done.4 = bf16[512,2048]{1,0:T(8,128)(2,1)S(1)} copy-done((bf16[512,2048]{1,0:T(8,128)(2,1)S(1)}, bf16[512,2048]{1,0:T(8,128)(2,1)}, u32[]{:S(2)}) %copy-start.4) | copy-done | bytes 2097176
  4.7 5.0 %collective-permute-start.3 = (f32[256,256]{1,0:T(8,128)S(1)}, f32[256,256]{1,0:T(8,128)S(1)}, u32[]{:S(2)}, u32[]{:S(2)}) collective-permute-start(f32[256,256]{1,0:T(8,128)S(1)} %get-tuple-element.30), channel_id=1, source_target_pairs={{0,1},{3,2},{4,5},{7,6},{8,9},{11,10},{12,13},{15,14},{16,17},{19,... | collective-permute-start | bytes 786440 | tf_op jit(solution)/shard_map/ppermute | solution.py:106
  9.7 1.3 %collective-permute-start = (f32[256,256]{1,0:T(8,128)S(1)}, f32[256,256]{1,0:T(8,128)S(1)}, u32[]{:S(2)}, u32[]{:S(2)}) collective-permute-start(f32[256,256]{1,0:T(8,128)S(1)} %get-tuple-element.27), channel_id=1, source_target_pairs={{0,1},{3,2},{4,5},{7,6},{8,9},{11,10},{12,13},{15,14},{16,17},{19,... | collective-permute-start | bytes 786440 | tf_op jit(solution)/shard_map/ppermute | solution.py:106
  11.0 2.2 %copy-done.2 = bf16[2048,1024]{1,0:T(8,128)(2,1)S(1)} copy-done((bf16[2048,1024]{1,0:T(8,128)(2,1)S(1)}, bf16[2048,1024]{1,0:T(8,128)(2,1)}, u32[]{:S(2)}) %copy-start.2) | copy-done | bytes 4194328
  14.1 2.2 %collective-permute-done.3 = f32[256,256]{1,0:T(8,128)S(1)} collective-permute-done((f32[256,256]{1,0:T(8,128)S(1)}, f32[256,256]{1,0:T(8,128)S(1)}, u32[]{:S(2)}, u32[]{:S(2)}) %collective-permute-start.3) | collective-permute-done | bytes 262176 | tf_op jit(solution)/shard_map/ppermute | solution.py:106
  17.0 5.0 %collective-permute-start.4 = (f32[256,256]{1,0:T(8,128)S(1)}, f32[256,256]{1,0:T(8,128)S(1)}, u32[]{:S(2)}, u32[]{:S(2)}) collective-permute-start(f32[256,256]{1,0:T(8,128)S(1)} %add.79), channel_id=1, source_target_pairs={{0,1},{1,2},{4,5},{5,6},{8,9},{9,10},{12,13},{13,14},{16,17},{17,1... | collective-permute-start | bytes 786440 | tf_op jit(solution)/shard_map/ppermute | solution.py:116
  22.8 5.2 %collective-permute-start.1 = (f32[256,256]{1,0:T(8,128)S(1)}, f32[256,256]{1,0:T(8,128)S(1)}, u32[]{:S(2)}, u32[]{:S(2)}) collective-permute-start(f32[256,256]{1,0:T(8,128)S(1)} %add.77), channel_id=1, source_target_pairs={{0,1},{1,2},{4,5},{5,6},{8,9},{9,10},{12,13},{13,14},{16,17},{17,1... | collective-permute-start | bytes 786440 | tf_op jit(solution)/shard_map/ppermute | solution.py:116
  28.1 3.2 %project.3 = (f32[256,256]{1,0:T(8,128)S(1)}, f32[256,256]{1,0:T(8,128)S(1)}, f32[256,256]{1,0:T(8,128)S(1)}, f32[256,256]{1,0:T(8,128)S(1)}, f32[256,256]{1,0:T(8,128)S(1)}, /*index=5*/f32[256,256]{1,0:T(8,128)S(1)}) custom-call(s32[3]{0:T(128)S(1)} %pad_add_fusion.2.ids_ref, bf16[512,2048]{1,0:T(8,128)(2,1)S(1)} %copy-done.5, bf16[2048,1024]{1,0:T(8,128)(2,1)S(1)} %copy-done.3), custom_call_target="tpu_custom_call" | custom-call | flops 1610612736 | bytes 3145728 | tf_op jit(solution)/shard_map/project/pallas_call | solution.py:59
  32.1 4.5 %collective-permute-start.2 = (f32[256,256]{1,0:T(8,128)S(1)}, f32[256,256]{1,0:T(8,128)S(1)}, u32[]{:S(2)}, u32[]{:S(2)}) collective-permute-start(f32[256,256]{1,0:T(8,128)S(1)} %add.78), channel_id=1, source_target_pairs={{0,1},{1,2},{2,3},{4,5},{5,6},{6,7},{8,9},{9,10},{10,11},{12,13},{... | collective-permute-start | bytes 786440 | tf_op jit(solution)/shard_map/ppermute | solution.py:116
  36.7 4.3 %collective-permute-start.5 = (f32[256,256]{1,0:T(8,128)S(1)}, f32[256,256]{1,0:T(8,128)S(1)}, u32[]{:S(2)}, u32[]{:S(2)}) collective-permute-start(f32[256,256]{1,0:T(8,128)S(1)} %add.80), channel_id=1, source_target_pairs={{0,1},{1,2},{2,3},{4,5},{5,6},{6,7},{8,9},{9,10},{10,11},{12,13},{... | collective-permute-start | bytes 786440 | tf_op jit(solution)/shard_map/ppermute | solution.py:116
  41.1 1.3 %collective-permute-start.7 = (f32[256,256]{1,0:T(8,128)S(1)}, f32[256,256]{1,0:T(8,128)S(1)}, u32[]{:S(2)}, u32[]{:S(2)}) collective-permute-start(f32[256,256]{1,0:T(8,128)S(1)} %add.81), channel_id=1, source_target_pairs={{3,2},{2,1},{1,0},{7,6},{6,5},{5,4},{11,10},{10,9},{9,8},{15,14},{... | collective-permute-start | bytes 786440 | tf_op jit(solution)/shard_map/ppermute | solution.py:117
  42.5 1.3 %collective-permute-start.9 = (f32[256,256]{1,0:T(8,128)S(1)}, f32[256,256]{1,0:T(8,128)S(1)}, u32[]{:S(2)}, u32[]{:S(2)}) collective-permute-start(f32[256,256]{1,0:T(8,128)S(1)} %add.82), channel_id=1, source_target_pairs={{3,2},{2,1},{1,0},{7,6},{6,5},{5,4},{11,10},{10,9},{9,8},{15,14},{... | collective-permute-start | bytes 786440 | tf_op jit(solution)/shard_map/ppermute | solution.py:117
  43.8 2.3 %collective-permute-done.5.refs_6_ = f32[256,256]{1,0:T(8,128)S(1)} collective-permute-done((f32[256,256]{1,0:T(8,128)S(1)}, f32[256,256]{1,0:T(8,128)S(1)}, u32[]{:S(2)}, u32[]{:S(2)}) %collective-permute-start.5) | collective-permute-done | bytes 262176 | tf_op jit(solution)/shard_map/ppermute | solution.py:116
  46.1 4.3 %collective-permute-done.7.refs_7_ = f32[256,256]{1,0:T(8,128)S(1)} collective-permute-done((f32[256,256]{1,0:T(8,128)S(1)}, f32[256,256]{1,0:T(8,128)S(1)}, u32[]{:S(2)}, u32[]{:S(2)}) %collective-permute-start.7) | collective-permute-done | bytes 262176 | tf_op jit(solution)/shard_map/ppermute | solution.py:117
  50.5 2.8 %collective-permute-done.9.refs_8_ = f32[256,256]{1,0:T(8,128)S(1)} collective-permute-done((f32[256,256]{1,0:T(8,128)S(1)}, f32[256,256]{1,0:T(8,128)S(1)}, u32[]{:S(2)}, u32[]{:S(2)}) %collective-permute-start.9) | collective-permute-done | bytes 262176 | tf_op jit(solution)/shard_map/ppermute | solution.py:117
  53.3 1.2 %finish.1 = (bf16[640,256]{1,0:T(8,128)(2,1)S(1)}, bf16[640,256]{1,0:T(8,128)(2,1)S(1)}) custom-call(s32[2]{0:T(128)S(1)} %pad_add_fusion.1.refs_0_, s32[4]{0:T(128)S(1)} %copy-done.6, s32[4]{0:T(128)S(1)} %copy-done.7, f32[256,256]{1,0:T(8,128)S(1)} %get-tuple-element.23.refs_3_, f32[256,256]{1,0:T(8,128)S(1)} %get-tuple-element.24.refs_4_, ...), custom_call_target="tpu_custom_call" | custom-call | flops 335544320 | bytes 1572864 | tf_op jit(solution)/shard_map/finish/pallas_call | solution.py:159
  54.5 1.6 %collective-permute-done.10 = bf16[640,256]{1,0:T(8,128)(2,1)S(1)} collective-permute-done((bf16[640,256]{1,0:T(8,128)(2,1)S(1)}, bf16[640,256]{1,0:T(8,128)(2,1)S(1)}, u32[]{:S(2)}, u32[]{:S(2)}) %collective-permute-start.10) | collective-permute-done | bytes 327712 | tf_op jit(solution)/shard_map/ppermute | solution.py:28
  56.3 1.6 %collective-permute-start.11 = (bf16[640,256]{1,0:T(8,128)(2,1)S(1)}, bf16[640,256]{1,0:T(8,128)(2,1)S(1)}, u32[]{:S(2)}, u32[]{:S(2)}) collective-permute-start(bf16[640,256]{1,0:T(8,128)(2,1)S(1)} %add.83), channel_id=1, source_target_pairs={{0,8},{4,20},{8,0},{12,28},{16,24},{20,4},{24,16},{28,12},{1,9},{5... | collective-permute-start | bytes 983048 | tf_op jit(solution)/shard_map/ppermute | solution.py:316
  57.8 5.6 %collective-permute-done.11 = bf16[640,256]{1,0:T(8,128)(2,1)S(1)} collective-permute-done((bf16[640,256]{1,0:T(8,128)(2,1)S(1)}, bf16[640,256]{1,0:T(8,128)(2,1)S(1)}, u32[]{:S(2)}, u32[]{:S(2)}) %collective-permute-start.11) | collective-permute-done | bytes 327712 | tf_op jit(solution)/shard_map/ppermute | solution.py:316
  63.5 1.6 %collective-permute-start.12 = (bf16[640,256]{1,0:T(8,128)(2,1)S(1)}, bf16[640,256]{1,0:T(8,128)(2,1)S(1)}, u32[]{:S(2)}, u32[]{:S(2)}) collective-permute-start(bf16[640,256]{1,0:T(8,128)(2,1)S(1)} %add.84), channel_id=1, source_target_pairs={{0,16},{4,12},{8,24},{12,4},{16,0},{20,28},{24,8},{28,20},{1,17},{... | collective-permute-start | bytes 983048 | tf_op jit(solution)/shard_map/ppermute | solution.py:316
  65.1 5.6 %collective-permute-done.12 = bf16[640,256]{1,0:T(8,128)(2,1)S(1)} collective-permute-done((bf16[640,256]{1,0:T(8,128)(2,1)S(1)}, bf16[640,256]{1,0:T(8,128)(2,1)S(1)}, u32[]{:S(2)}, u32[]{:S(2)}) %collective-permute-start.12) | collective-permute-done | bytes 327712 | tf_op jit(solution)/shard_map/ppermute | solution.py:316
  70.8 1.6 %collective-permute-done.13 = bf16[640,256]{1,0:T(8,128)(2,1)S(1)} collective-permute-done((bf16[640,256]{1,0:T(8,128)(2,1)S(1)}, bf16[640,256]{1,0:T(8,128)(2,1)S(1)}, u32[]{:S(2)}, u32[]{:S(2)}) %collective-permute-start.13) | collective-permute-done | bytes 327712 | tf_op jit(solution)/shard_map/ppermute | solution.py:28
  72.7 2.9 %collective-permute-start.14 = (bf16[1280,256]{1,0:T(8,128)(2,1)S(1)}, bf16[1280,256]{1,0:T(8,128)(2,1)S(1)}, u32[]{:S(2)}, u32[]{:S(2)}) collective-permute-start(bf16[1280,256]{1,0:T(8,128)(2,1)S(1)} %maximum_select_fusion.refs_4_), channel_id=1, source_target_pairs={{0,1},{1,2},{2,3},{7,6},{6,5},{5,4},{8,9},{9,10},{10,11},{15,14},{... | collective-permute-start | bytes 1966088 | tf_op jit(solution)/shard_map/ppermute | solution.py:350
  76.8 3.5 %attend.4.refs_6_ = bf16[128,4096]{1,0:T(8,128)(2,1)} custom-call(s32[1]{0:T(128)} %bitcast.9.refs_0_, bf16[128,4096]{1,0:T(8,128)(2,1)S(1)} %copy-done.9, bf16[128,128]{1,0:T(8,128)(2,1)S(1)} %pad.5.refs_2_, bf16[1280,128]{1,0:T(8,128)(2,1)S(1)} %token_bias.1.refs_3_, bf16[1280,256]{1,0:T(8,128)(2,1)S(1)} %maximum_select_fusion.refs_4_), custom_call_target="tpu_custom_call" | custom-call | flops 1006632960 | bytes 524288 | tf_op jit(solution)/shard_map/attend/pallas_call | solution.py:271
  80.3 3.3 %collective-permute-done.14.refs_4_ = bf16[1280,256]{1,0:T(8,128)(2,1)S(1)} collective-permute-done((bf16[1280,256]{1,0:T(8,128)(2,1)S(1)}, bf16[1280,256]{1,0:T(8,128)(2,1)S(1)}, u32[]{:S(2)}, u32[]{:S(2)}) %collective-permute-start.14) | collective-permute-done | bytes 655392 | tf_op jit(solution)/shard_map/ppermute | solution.py:350
  85.9 4.2 %attend.5.refs_6_ = bf16[128,4096]{1,0:T(8,128)(2,1)} custom-call(s32[2]{0:T(128)S(1)} %pad_add_fusion.3.refs_0_, bf16[128,4096]{1,0:T(8,128)(2,1)S(1)} %copy-done.9, bf16[128,128]{1,0:T(8,128)(2,1)S(1)} %pad.5.refs_2_, bf16[1280,128]{1,0:T(8,128)(2,1)S(1)} %token_bias.1.refs_3_, ...), custom_call_target="tpu_custom_call", output_to_operand_aliasing={{}: (6, {})} | custom-call | flops 2013265920 | bytes 1048576 | tf_op jit(solution)/shard_map/attend/pallas_call | solution.py:271
  90.1 6.1 %collective-permute-start.18 = (bf16[1280,256]{1,0:T(8,128)(2,1)S(1)}, bf16[1280,256]{1,0:T(8,128)(2,1)S(1)}, u32[]{:S(2)}, u32[]{:S(2)}) collective-permute-start(bf16[1280,256]{1,0:T(8,128)(2,1)S(1)} %collective-permute-done.15.refs_4_), channel_id=1, source_target_pairs={{0,4},{4,0},{8,12},{12,8},{16,20},{20,16},{24,28},{28,24},{1,5},{5... | collective-permute-start | bytes 1966088 | tf_op jit(solution)/shard_map/ppermute | solution.py:28
  97.9 4.0 %attend.6.refs_6_ = bf16[128,4096]{1,0:T(8,128)(2,1)} custom-call(s32[2]{0:T(128)S(1)} %pad_add_fusion.4.refs_0_, bf16[128,4096]{1,0:T(8,128)(2,1)S(1)} %copy-done.9, bf16[128,128]{1,0:T(8,128)(2,1)S(1)} %pad.5.refs_2_, bf16[1280,128]{1,0:T(8,128)(2,1)S(1)} %token_bias.1.refs_3_, ...), custom_call_target="tpu_custom_call", output_to_operand_aliasing={{}: (6, {})} | custom-call | flops 2013265920 | bytes 1048576 | tf_op jit(solution)/shard_map/attend/pallas_call | solution.py:271
  101.9 5.6 %collective-permute-start.19 = (bf16[1280,256]{1,0:T(8,128)(2,1)S(1)}, bf16[1280,256]{1,0:T(8,128)(2,1)S(1)}, u32[]{:S(2)}, u32[]{:S(2)}) collective-permute-start(bf16[1280,256]{1,0:T(8,128)(2,1)S(1)} %collective-permute-done.17.refs_4_), channel_id=1, source_target_pairs={{0,4},{4,0},{8,12},{12,8},{16,20},{20,16},{24,28},{28,24},{1,5},{5... | collective-permute-start | bytes 1966088 | tf_op jit(solution)/shard_map/ppermute | solution.py:28
  107.6 1.6 %collective-permute-done.19.refs_5_ = bf16[1280,256]{1,0:T(8,128)(2,1)S(1)} collective-permute-done((bf16[1280,256]{1,0:T(8,128)(2,1)S(1)}, bf16[1280,256]{1,0:T(8,128)(2,1)S(1)}, u32[]{:S(2)}, u32[]{:S(2)}) %collective-permute-start.19) | collective-permute-done | bytes 655392 | tf_op jit(solution)/shard_map/ppermute | solution.py:28
  109.2 4.2 %attend.7 = bf16[128,4096]{1,0:T(8,128)(2,1)} custom-call(s32[2]{0:T(128)S(1)} %pad_add_fusion.refs_0_, bf16[128,4096]{1,0:T(8,128)(2,1)S(1)} %copy-done.9, bf16[128,128]{1,0:T(8,128)(2,1)S(1)} %pad.5.refs_2_, bf16[1280,128]{1,0:T(8,128)(2,1)S(1)} %token_bias.1.refs_3_, ...), custom_call_target="tpu_custom_call", output_to_operand_aliasing={{}: (6, {})} | custom-call | flops 2013265920 | bytes 1048576 | tf_op jit(solution)/shard_map/attend/pallas_call | solution.py:271
  (56 shorter events, 10.2 us)
Async XLA Ops:
  0.0 76.6 %copy-start = (s32[512,4]{0,1:T(4,128)S(1)}, s32[512,4]{0,1:T(4,128)}, u32[]{:S(2)}) copy-start(s32[512,4]{0,1:T(4,128)} %param.11) | copy-start | bytes 24580
  0.0 2.2 %copy-start.1 = (bf16[2048,1024]{1,0:T(8,128)(2,1)S(1)}, bf16[2048,1024]{1,0:T(8,128)(2,1)}, u32[]{:S(2)}) copy-start(bf16[2048,1024]{1,0:T(8,128)(2,1)} %weight_ref.5) | copy-start | bytes 12582916
  2.2 1.6 %copy-start.4 = (bf16[512,2048]{1,0:T(8,128)(2,1)S(1)}, bf16[512,2048]{1,0:T(8,128)(2,1)}, u32[]{:S(2)}) copy-start(bf16[512,2048]{1,0:T(8,128)(2,1)} %feats_ref.5) | copy-start | bytes 6291460
  3.8 7.2 %copy-start.5 = (bf16[512,2048]{1,0:T(8,128)(2,1)S(1)}, bf16[512,2048]{1,0:T(8,128)(2,1)}, u32[]{:S(2)}) copy-start(bf16[512,2048]{1,0:T(8,128)(2,1)} %feats_ref.5) | copy-start | bytes 6291460
  4.7 11.6 %collective-permute-start.3 = (f32[256,256]{1,0:T(8,128)S(1)}, f32[256,256]{1,0:T(8,128)S(1)}, u32[]{:S(2)}, u32[]{:S(2)}) collective-permute-start(f32[256,256]{1,0:T(8,128)S(1)} %get-tuple-element.30), channel_id=1, source_target_pairs={{0,1},{3,2},{4,5},{7,6},{8,9},{11,10},{12,13},{15,14},{16,17},{19,... | collective-permute-start | bytes 786440 | tf_op jit(solution)/shard_map/ppermute | solution.py:106
  9.7 12.4 %collective-permute-start = (f32[256,256]{1,0:T(8,128)S(1)}, f32[256,256]{1,0:T(8,128)S(1)}, u32[]{:S(2)}, u32[]{:S(2)}) collective-permute-start(f32[256,256]{1,0:T(8,128)S(1)} %get-tuple-element.27), channel_id=1, source_target_pairs={{0,1},{3,2},{4,5},{7,6},{8,9},{11,10},{12,13},{15,14},{16,17},{19,... | collective-permute-start | bytes 786440 | tf_op jit(solution)/shard_map/ppermute | solution.py:106
  11.0 2.2 %copy-start.2 = (bf16[2048,1024]{1,0:T(8,128)(2,1)S(1)}, bf16[2048,1024]{1,0:T(8,128)(2,1)}, u32[]{:S(2)}) copy-start(bf16[2048,1024]{1,0:T(8,128)(2,1)} %weight_ref.5) | copy-start | bytes 12582916
  13.2 14.8 %copy-start.3 = (bf16[2048,1024]{1,0:T(8,128)(2,1)S(1)}, bf16[2048,1024]{1,0:T(8,128)(2,1)}, u32[]{:S(2)}) copy-start(bf16[2048,1024]{1,0:T(8,128)(2,1)} %weight_ref.5) | copy-start | bytes 12582916
  16.4 26.1 %collective-permute-start.8 = (f32[256,256]{1,0:T(8,128)S(1)}, f32[256,256]{1,0:T(8,128)S(1)}, u32[]{:S(2)}, u32[]{:S(2)}) collective-permute-start(f32[256,256]{1,0:T(8,128)S(1)} %add.79), channel_id=1, source_target_pairs={{3,2},{2,1},{7,6},{6,5},{11,10},{10,9},{15,14},{14,13},{19,18},{18... | collective-permute-start | bytes 786440 | tf_op jit(solution)/shard_map/ppermute | solution.py:117
  17.0 19.6 %collective-permute-start.4 = (f32[256,256]{1,0:T(8,128)S(1)}, f32[256,256]{1,0:T(8,128)S(1)}, u32[]{:S(2)}, u32[]{:S(2)}) collective-permute-start(f32[256,256]{1,0:T(8,128)S(1)} %add.79), channel_id=1, source_target_pairs={{0,1},{1,2},{4,5},{5,6},{8,9},{9,10},{12,13},{13,14},{16,17},{17,1... | collective-permute-start | bytes 786440 | tf_op jit(solution)/shard_map/ppermute | solution.py:116
  22.1 18.9 %collective-permute-start.6 = (f32[256,256]{1,0:T(8,128)S(1)}, f32[256,256]{1,0:T(8,128)S(1)}, u32[]{:S(2)}, u32[]{:S(2)}) collective-permute-start(f32[256,256]{1,0:T(8,128)S(1)} %add.77), channel_id=1, source_target_pairs={{3,2},{2,1},{7,6},{6,5},{11,10},{10,9},{15,14},{14,13},{19,18},{18... | collective-permute-start | bytes 786440 | tf_op jit(solution)/shard_map/ppermute | solution.py:117
  22.8 9.2 %collective-permute-start.1 = (f32[256,256]{1,0:T(8,128)S(1)}, f32[256,256]{1,0:T(8,128)S(1)}, u32[]{:S(2)}, u32[]{:S(2)}) collective-permute-start(f32[256,256]{1,0:T(8,128)S(1)} %add.77), channel_id=1, source_target_pairs={{0,1},{1,2},{4,5},{5,6},{8,9},{9,10},{12,13},{13,14},{16,17},{17,1... | collective-permute-start | bytes 786440 | tf_op jit(solution)/shard_map/ppermute | solution.py:116
  32.1 21.2 %copy-start.6 = (s32[4]{0:T(128)S(1)}, s32[4]{0:T(128)}, u32[]{:S(2)}) copy-start(s32[4]{0:T(128)} %refs_1_.5) | copy-start | bytes 52
  32.1 21.2 %copy-start.7 = (s32[4]{0:T(128)S(1)}, s32[4]{0:T(128)}, u32[]{:S(2)}) copy-start(s32[4]{0:T(128)} %refs_2_.1) | copy-start | bytes 52
  32.1 21.2 %copy-start.8 = (f32[128]{0:T(128)S(1)}, f32[128]{0:T(128)}, u32[]{:S(2)}) copy-start(f32[128]{0:T(128)} %param.10) | copy-start | bytes 1540
  32.1 11.7 %collective-permute-start.2 = (f32[256,256]{1,0:T(8,128)S(1)}, f32[256,256]{1,0:T(8,128)S(1)}, u32[]{:S(2)}, u32[]{:S(2)}) collective-permute-start(f32[256,256]{1,0:T(8,128)S(1)} %add.78), channel_id=1, source_target_pairs={{0,1},{1,2},{2,3},{4,5},{5,6},{6,7},{8,9},{9,10},{10,11},{12,13},{... | collective-permute-start | bytes 786440 | tf_op jit(solution)/shard_map/ppermute | solution.py:116
  36.7 9.4 %collective-permute-start.5 = (f32[256,256]{1,0:T(8,128)S(1)}, f32[256,256]{1,0:T(8,128)S(1)}, u32[]{:S(2)}, u32[]{:S(2)}) collective-permute-start(f32[256,256]{1,0:T(8,128)S(1)} %add.80), channel_id=1, source_target_pairs={{0,1},{1,2},{2,3},{4,5},{5,6},{6,7},{8,9},{9,10},{10,11},{12,13},{... | collective-permute-start | bytes 786440 | tf_op jit(solution)/shard_map/ppermute | solution.py:116
  41.1 9.4 %collective-permute-start.7 = (f32[256,256]{1,0:T(8,128)S(1)}, f32[256,256]{1,0:T(8,128)S(1)}, u32[]{:S(2)}, u32[]{:S(2)}) collective-permute-start(f32[256,256]{1,0:T(8,128)S(1)} %add.81), channel_id=1, source_target_pairs={{3,2},{2,1},{1,0},{7,6},{6,5},{5,4},{11,10},{10,9},{9,8},{15,14},{... | collective-permute-start | bytes 786440 | tf_op jit(solution)/shard_map/ppermute | solution.py:117
  42.5 10.8 %collective-permute-start.9 = (f32[256,256]{1,0:T(8,128)S(1)}, f32[256,256]{1,0:T(8,128)S(1)}, u32[]{:S(2)}, u32[]{:S(2)}) collective-permute-start(f32[256,256]{1,0:T(8,128)S(1)} %add.82), channel_id=1, source_target_pairs={{3,2},{2,1},{1,0},{7,6},{6,5},{5,4},{11,10},{10,9},{9,8},{15,14},{... | collective-permute-start | bytes 786440 | tf_op jit(solution)/shard_map/ppermute | solution.py:117
  54.5 1.7 %collective-permute-start.10 = (bf16[640,256]{1,0:T(8,128)(2,1)S(1)}, bf16[640,256]{1,0:T(8,128)(2,1)S(1)}, u32[]{:S(2)}, u32[]{:S(2)}) collective-permute-start(bf16[640,256]{1,0:T(8,128)(2,1)S(1)} %get-tuple-element.34), channel_id=1, source_target_pairs={{0,4},{4,0},{8,12},{12,8},{16,20},{20,16},{24,28},{28,24},{1,5},{5... | collective-permute-start | bytes 983048 | tf_op jit(solution)/shard_map/ppermute | solution.py:28
  56.3 7.1 %collective-permute-start.11 = (bf16[640,256]{1,0:T(8,128)(2,1)S(1)}, bf16[640,256]{1,0:T(8,128)(2,1)S(1)}, u32[]{:S(2)}, u32[]{:S(2)}) collective-permute-start(bf16[640,256]{1,0:T(8,128)(2,1)S(1)} %add.83), channel_id=1, source_target_pairs={{0,8},{4,20},{8,0},{12,28},{16,24},{20,4},{24,16},{28,12},{1,9},{5... | collective-permute-start | bytes 983048 | tf_op jit(solution)/shard_map/ppermute | solution.py:316
  63.5 13.3 %copy-start.9 = (bf16[128,4096]{1,0:T(8,128)(2,1)S(1)}, bf16[128,4096]{1,0:T(8,128)(2,1)}, u32[]{:S(2)}) copy-start(bf16[128,4096]{1,0:T(8,128)(2,1)} %refs_1_.9) | copy-start | bytes 3145732
  63.5 7.1 %collective-permute-start.12 = (bf16[640,256]{1,0:T(8,128)(2,1)S(1)}, bf16[640,256]{1,0:T(8,128)(2,1)S(1)}, u32[]{:S(2)}, u32[]{:S(2)}) collective-permute-start(bf16[640,256]{1,0:T(8,128)(2,1)S(1)} %add.84), channel_id=1, source_target_pairs={{0,16},{4,12},{8,24},{12,4},{16,0},{20,28},{24,8},{28,20},{1,17},{... | collective-permute-start | bytes 983048 | tf_op jit(solution)/shard_map/ppermute | solution.py:316
  70.7 1.7 %collective-permute-start.13 = (bf16[640,256]{1,0:T(8,128)(2,1)S(1)}, bf16[640,256]{1,0:T(8,128)(2,1)S(1)}, u32[]{:S(2)}, u32[]{:S(2)}) collective-permute-start(bf16[640,256]{1,0:T(8,128)(2,1)S(1)} %add.85), channel_id=1, source_target_pairs={{0,4},{4,0},{8,12},{12,8},{16,20},{20,16},{24,28},{28,24},{1,5},{5... | collective-permute-start | bytes 983048 | tf_op jit(solution)/shard_map/ppermute | solution.py:28
  72.7 10.9 %collective-permute-start.14 = (bf16[1280,256]{1,0:T(8,128)(2,1)S(1)}, bf16[1280,256]{1,0:T(8,128)(2,1)S(1)}, u32[]{:S(2)}, u32[]{:S(2)}) collective-permute-start(bf16[1280,256]{1,0:T(8,128)(2,1)S(1)} %maximum_select_fusion.refs_4_), channel_id=1, source_target_pairs={{0,1},{1,2},{2,3},{7,6},{6,5},{5,4},{8,9},{9,10},{10,11},{15,14},{... | collective-permute-start | bytes 1966088 | tf_op jit(solution)/shard_map/ppermute | solution.py:350
  83.6 2.3 %collective-permute-start.16 = (bf16[1280,256]{1,0:T(8,128)(2,1)S(1)}, bf16[1280,256]{1,0:T(8,128)(2,1)S(1)}, u32[]{:S(2)}, u32[]{:S(2)}) collective-permute-start(bf16[1280,256]{1,0:T(8,128)(2,1)S(1)} %collective-permute-done.14.refs_4_), channel_id=1, source_target_pairs={{0,4},{4,0},{8,12},{12,8},{16,20},{20,16},{24,28},{28,24},{1,5},{5... | collective-permute-start | bytes 1966088 | tf_op jit(solution)/shard_map/ppermute | solution.py:28
  84.2 5.9 %collective-permute-start.15 = (bf16[1280,256]{1,0:T(8,128)(2,1)S(1)}, bf16[1280,256]{1,0:T(8,128)(2,1)S(1)}, u32[]{:S(2)}, u32[]{:S(2)}) collective-permute-start(bf16[1280,256]{1,0:T(8,128)(2,1)S(1)} %collective-permute-done.14.refs_4_), channel_id=1, source_target_pairs={{1,2},{2,3},{6,5},{5,4},{9,10},{10,11},{14,13},{13,12},{17,18},{18... | collective-permute-start | bytes 1966088 | tf_op jit(solution)/shard_map/ppermute | solution.py:350
  90.1 7.8 %collective-permute-start.18 = (bf16[1280,256]{1,0:T(8,128)(2,1)S(1)}, bf16[1280,256]{1,0:T(8,128)(2,1)S(1)}, u32[]{:S(2)}, u32[]{:S(2)}) collective-permute-start(bf16[1280,256]{1,0:T(8,128)(2,1)S(1)} %collective-permute-done.15.refs_4_), channel_id=1, source_target_pairs={{0,4},{4,0},{8,12},{12,8},{16,20},{20,16},{24,28},{28,24},{1,5},{5... | collective-permute-start | bytes 1966088 | tf_op jit(solution)/shard_map/ppermute | solution.py:28
  96.2 5.8 %collective-permute-start.17 = (bf16[1280,256]{1,0:T(8,128)(2,1)S(1)}, bf16[1280,256]{1,0:T(8,128)(2,1)S(1)}, u32[]{:S(2)}, u32[]{:S(2)}) collective-permute-start(bf16[1280,256]{1,0:T(8,128)(2,1)S(1)} %collective-permute-done.15.refs_4_), channel_id=1, source_target_pairs={{2,3},{5,4},{10,11},{13,12},{18,19},{21,20},{26,27},{29,28}} | collective-permute-start | bytes 1966088 | tf_op jit(solution)/shard_map/ppermute | solution.py:350
  101.9 7.3 %collective-permute-start.19 = (bf16[1280,256]{1,0:T(8,128)(2,1)S(1)}, bf16[1280,256]{1,0:T(8,128)(2,1)S(1)}, u32[]{:S(2)}, u32[]{:S(2)}) collective-permute-start(bf16[1280,256]{1,0:T(8,128)(2,1)S(1)} %collective-permute-done.17.refs_4_), channel_id=1, source_target_pairs={{0,4},{4,0},{8,12},{12,8},{16,20},{20,16},{24,28},{28,24},{1,5},{5... | collective-permute-start | bytes 1966088 | tf_op jit(solution)/shard_map/ppermute | solution.py:28

commit v3 on v2

v3 whole, which is shorter than its diff:
```python
import math

import jax
import jax.numpy as jnp
from jax import lax
from jax.experimental import pallas as pl
from jax.experimental.pallas import tpu as pltpu
from jax.sharding import PartitionSpec as P

EPSILON = 1e-05
FLOOR_SCORE = -1e30
KV_TOTAL = 1280
STACK = 2
MIB = 2**20

VMEM = pl.BlockSpec(memory_space=pltpu.VMEM)
SMEM = pl.BlockSpec(memory_space=pltpu.SMEM)
ANYWHERE = pl.BlockSpec(memory_space=pl.ANY)
HBM = pl.BlockSpec(memory_space=pltpu.HBM)


def params(mib):
    return pltpu.CompilerParams(vmem_limit_bytes=mib * MIB)


def swapped(value, axis, bit):
    mask = 2**bit
    pairs = [(source, source ^ mask) for source in range(lax.axis_size(axis))]
    return lax.ppermute(value, axis, pairs)


def project(chunk_ids, vis_feats, kv_weight, chunk_count, pair):
    rows, width = vis_feats.shape
    wanted = chunk_ids.shape[0]
    per_kv = chunk_count // (kv_weight.shape[1] // pair)
    block_rows = rows // per_kv
    head_dim = pair // 2
    columns = pair if wanted == 1 else kv_weight.shape[1]
    steps = 4
    few, deep = rows // steps, width // steps

    def kernel(ids_ref, feats_hbm, weight_hbm, *refs):
        out_refs, (feats_ref, weight_ref, sems) = refs[: 2 * wanted], refs[2 * wanted :]
        copies = []
        for n in range(steps):
            span = pl.ds(n * few, few)
            copies.append((feats_hbm.at[span], feats_ref.at[span], sems.at[n]))
        first = pl.multiple_of((ids_ref[0] // per_kv) * pair, pair)
        for n in range(steps):
            span = pl.ds(n * deep, deep)
            source = weight_hbm.at[span, pl.ds(first, pair)] if wanted == 1 else weight_hbm.at[span]
            copies.append((source, weight_ref.at[span], sems.at[steps + n]))
        copies = [pltpu.make_async_copy(*copy) for copy in copies]
        for copy in copies:
            copy.start()
        for copy in copies:
            copy.wait()
        for n in range(wanted):
            column = 0 if wanted == 1 else pl.multiple_of((ids_ref[n] // per_kv) * pair, pair)
            row = 0 if per_kv == 1 else pl.multiple_of((ids_ref[n] % per_kv) * block_rows, block_rows)
            out = jnp.dot(
                feats_ref[pl.ds(row, block_rows), :],
                weight_ref[:, pl.ds(column, pair)],
                preferred_element_type=jnp.float32,
            )
            out_refs[2 * n][...] = out[:, :head_dim]
            out_refs[2 * n + 1][...] = out[:, head_dim:]

    flat = pl.pallas_call(
        kernel,
        in_specs=[SMEM, HBM, HBM],
        out_specs=[VMEM] * (2 * wanted),
        out_shape=[jax.ShapeDtypeStruct((block_rows, head_dim), jnp.float32)] * (2 * wanted),
        scratch_shapes=[
            pltpu.VMEM((rows, width), vis_feats.dtype),
            pltpu.VMEM((width, columns), kv_weight.dtype),
            pltpu.SemaphoreType.DMA((2 * steps,)),
        ],
        compiler_params=params(16),
        cost_estimate=pl.CostEstimate(
            flops=2 * wanted * block_rows * width * pair,
            bytes_accessed=(columns + rows) * width * 2,
            transcendentals=0,
        ),
        name="project",
    )(
        chunk_ids,
        pltpu.with_memory_space_constraint(vis_feats, pltpu.HBM),
        pltpu.with_memory_space_constraint(kv_weight, pltpu.HBM),
    )
    return [flat[2 * n : 2 * n + 2] for n in range(wanted)]


def project_rest(chunk_ids, vis_feats, kv_weight, chunk_count, pair):
    rows, width = vis_feats.shape
    wanted = chunk_ids.shape[0]
    per_kv = chunk_count // (kv_weight.shape[1] // pair)
    block_rows = rows // per_kv
    head_dim = pair // 2

    def kernel(ids_ref, feats_ref, weight_ref, *out_refs):
        for n in range(wanted):
            column = pl.multiple_of((ids_ref[n] // per_kv) * pair, pair)
            row = 0 if per_kv == 1 else pl.multiple_of((ids_ref[n] % per_kv) * block_rows, block_rows)
            out = jnp.dot(
                feats_ref[pl.ds(row, block_rows), :],
                weight_ref[:, pl.ds(column, pair)],
                preferred_element_type=jnp.float32,
            )
            out_refs[2 * n][...] = out[:, :head_dim]
            out_refs[2 * n + 1][...] = out[:, head_dim:]

    flat = pl.pallas_call(
        kernel,
        in_specs=[SMEM, VMEM, VMEM],
        out_specs=[VMEM] * (2 * wanted),
        out_shape=[jax.ShapeDtypeStruct((block_rows, head_dim), jnp.float32)] * (2 * wanted),
        compiler_params=params(8),
        cost_estimate=pl.CostEstimate(
            flops=2 * wanted * block_rows * width * pair,
            bytes_accessed=wanted * pair * width * 2,
            transcendentals=0,
        ),
        name="project_rest",
    )(chunk_ids, vis_feats, kv_weight)
    return [flat[2 * n : 2 * n + 2] for n in range(wanted)]


def sum_over_head(vis_feats, kv_weight, pair, early):
    count = lax.axis_size("head")
    here = lax.axis_index("head")
    first = (count - 1 - here)[None].astype(jnp.int32)
    ends = project(first, vis_feats, kv_weight, count, pair)[0]
    offsets = []
    for hop in range(2, count):
        offsets += [o for o in dict.fromkeys((count - hop, hop)) if o not in offsets]
    offsets.append(0)
    ids = ((here + jnp.array(offsets, jnp.int32)) % count).astype(jnp.int32)
    parts = dict(zip(offsets, project_rest(ids, vis_feats, kv_weight, count, pair)))
    held = lax.optimization_barrier((ends[1], parts[0][0], *early))
    ends = (ends[0], held[0])
    parts[0] = (held[1], parts[0][1])
    early = held[2:]

    to_right, to_left = [None] * 2, [None] * 2
    for hop in range(1, count):
        senders = range(min(hop, count - 1))
        right_pairs = [(i, i + 1) for i in senders]
        left_pairs = [(count - 1 - i, count - 2 - i) for i in senders]
        for piece in range(2):
            if hop == 1 and count > 3:
                arrived = lax.ppermute(ends[piece], "head", right_pairs + left_pairs)
                to_right[piece] = to_left[piece] = arrived
                continue
            if hop == 1:
                right = left = ends[piece]
            elif hop == 2 and count == 4:
                right = left = parts[2][piece] + to_right[piece]
            else:
                right = parts[count - hop][piece] + to_right[piece]
                left = parts[hop][piece] + to_left[piece]
            to_right[piece] = lax.ppermute(right, "head", right_pairs)
            to_left[piece] = lax.ppermute(left, "head", left_pairs)
    return [[parts[0][piece], to_right[piece], to_left[piece]] for piece in range(2)], early


def finish_chunk(partial_sums, key_gain, image_tokens, image_owner, per_kv, are_keys):
    rows, head_dim = partial_sums[0].shape
    half = KV_TOTAL // 2
    images = image_owner.shape[0]
    place = jnp.stack([lax.axis_index("ctx"), lax.axis_index("head") % per_kv]).astype(jnp.int32)

    def kernel(place_ref, tokens_ref, owner_ref, own_ref, left_ref, right_ref, gain_ref, mine_ref, other_ref):
        data = own_ref[...] + left_ref[...] + right_ref[...]
        if are_keys:
            mean = jnp.mean(data * data, axis=-1, keepdims=True)
            data = data * lax.rsqrt(mean + EPSILON) * gain_ref[...]
        data = data.astype(jnp.bfloat16)
        ctx = place_ref[0]
        start, count, before = jnp.int32(0), jnp.int32(0), jnp.int32(0)
        for i in range(images):
            here = owner_ref[i] == ctx
            start = jnp.where(here, before, start)
            count = jnp.where(here, tokens_ref[i], count)
            before = before + tokens_ref[i]
        token = lax.broadcasted_iota(jnp.int32, (half, rows), 1) + place_ref[1] * rows
        token = jnp.where(token < count, token, -2 * KV_TOTAL)
        row = lax.broadcasted_iota(jnp.int32, (half, rows), 0)
        core = ctx % 2
        for ref, side in ((other_ref, 1 - core), (mine_ref, core)):
            match = (row + (side * half - start)) == token
            chosen = jnp.where(match, 1.0, 0.0).astype(jnp.bfloat16)
            ref[...] = jnp.dot(chosen, data, preferred_element_type=jnp.float32).astype(jnp.bfloat16)

    return pl.pallas_call(
        kernel,
        in_specs=[SMEM] * 3 + [VMEM] * 4,
        out_specs=[VMEM] * 2,
        out_shape=[jax.ShapeDtypeStruct((half, head_dim), jnp.bfloat16)] * 2,
        compiler_params=params(16),
        cost_estimate=pl.CostEstimate(
            flops=4 * half * rows * head_dim, bytes_accessed=12 * rows * head_dim, transcendentals=0
        ),
        name="finish",
    )(place, image_tokens, image_owner, *partial_sums, key_gain[None, :])


def mask_columns(cross_mask, image_tokens, head_dim, rows):
    images = image_tokens.shape[0]
    row_slice = lax.dynamic_slice_in_dim(cross_mask, lax.axis_index("head") * rows, rows, 0)
    row_mask = jnp.pad(
        1.0 - row_slice.astype(jnp.float32), ((0, 0), (0, head_dim - images)), constant_values=1.0
    ).astype(jnp.bfloat16)

    def kernel(tokens_ref, out_ref):
        row = lax.broadcasted_iota(jnp.int32, out_ref.shape, 0)
        column = lax.broadcasted_iota(jnp.int32, out_ref.shape, 1)
        before = jnp.int32(0)
        bias = jnp.zeros(out_ref.shape, jnp.float32)
        for i in range(images + 1):
            after = before + tokens_ref[i] if i < images else jnp.int32(KV_TOTAL)
            inside = (column == i) & (row >= before) & (row < after)
            bias = jnp.where(inside, FLOOR_SCORE, bias)
            before = after
        out_ref[...] = bias.astype(jnp.bfloat16)

    token_bias = pl.pallas_call(
        kernel,
        in_specs=[SMEM],
        out_specs=VMEM,
        out_shape=jax.ShapeDtypeStruct((KV_TOTAL, head_dim), jnp.bfloat16),
        compiler_params=params(8),
        name="token_bias",
    )(image_tokens)
    return row_mask, token_bias


def attend(call, own, arrivals, queries, row_mask, token_bias, kv_heads, images, previous):
    rows, width = queries.shape
    tokens, head_dim = own[0].shape
    block_width = width // kv_heads
    group = block_width // head_dim
    factor = head_dim ** (-0.5) * math.log2(math.e)
    stack = min(STACK, group)
    first_hop = (call + 1) // 2
    sources = [own] if call == 0 else [pair for hop in arrivals[first_hop - 1 : call] for pair in hop]
    count = len(sources)
    line = own[2]
    ids = own[3]

    def kernel(*refs):
        ids_ref, queries_ref, mask_ref, bias_ref = refs[:4]
        source_refs = refs[4 : 4 + 2 * count]
        refs = refs[4 + 2 * count + (previous is not None) :]
        out_ref, keys_ref, values_ref, query_ref, result_ref, sems = refs
        here, step = ids_ref[0], ids_ref[1]

        def take(n):
            keys_ref[:, :head_dim] = source_refs[2 * n][...]
            values_ref[...] = source_refs[2 * n + 1][...]

        head = here
        if call == 0:
            take(0)
        else:
            rank = jnp.int32(0)
            for hop in range(1, call + 1):
                for side in range(2):
                    candidate = here + (hop if side else -hop) * step
                    valid = (candidate >= 0) & (candidate < line)
                    rank = rank + jnp.where(valid, 1, 0)
                    chosen = valid & (rank == call)
                    head = jnp.where(chosen, candidate, head)
                    if hop >= first_hop:
                        pl.when(chosen)(lambda n=2 * (hop - first_hop) + side: take(n))
        column = pl.multiple_of(head * block_width, block_width)
        fetch = pltpu.make_async_copy(
            queries_ref.at[:, pl.ds(column, block_width)], query_ref, sems.at[0]
        )
        fetch.start()
        keys_ref[:, head_dim:] = bias_ref[...]
        some = jnp.min(mask_ref[:, :images].astype(jnp.float32), axis=1, keepdims=True) < 0.5
        fetch.wait()
        for first in range(0, group, stack):
            left = jnp.concatenate(
                [
                    jnp.concatenate(
                        [query_ref[:, j * head_dim : (j + 1) * head_dim], mask_ref[...]], axis=1
                    )
                    for j in range(first, first + stack)
                ],
                axis=0,
            )
            scores = lax.dot_general(
                left, keys_ref[...], (((1,), (1,)), ((), ())), preferred_element_type=jnp.float32
            )
            largest = jnp.max(scores, axis=1, keepdims=True)
            weights = jnp.exp2((scores - largest) * factor)
            summed = jnp.sum(weights, axis=1, keepdims=True)
            mixed = jnp.dot(
                weights.astype(jnp.bfloat16), values_ref[...], preferred_element_type=jnp.float32
            )
            mixed = mixed / jnp.maximum(summed, 1.0)
            for j in range(stack):
                one = jnp.where(some, mixed[j * rows : (j + 1) * rows], 0.0)
                at = (first + j) * head_dim
                result_ref[:, at : at + head_dim] = one.astype(jnp.bfloat16)
        store = pltpu.make_async_copy(
            result_ref, out_ref.at[:, pl.ds(column, block_width)], sems.at[1]
        )
        store.start()
        store.wait()

    operands = [ids, queries, row_mask, token_bias]
    for source in sources:
        operands += [source[0], source[1]]
    in_specs = [SMEM, ANYWHERE] + [VMEM] * (len(operands) - 2)
    aliases = {}
    if previous is not None:
        aliases = {len(operands): 0}
        operands.append(previous)
        in_specs.append(ANYWHERE)
    return pl.pallas_call(
        kernel,
        in_specs=in_specs,
        out_specs=ANYWHERE,
        out_shape=jax.ShapeDtypeStruct((rows, width), jnp.bfloat16),
        scratch_shapes=[
            pltpu.VMEM((tokens, 2 * head_dim), jnp.bfloat16),
            pltpu.VMEM((tokens, head_dim), jnp.bfloat16),
            pltpu.VMEM((rows, block_width), jnp.bfloat16),
            pltpu.VMEM((rows, block_width), jnp.bfloat16),
            pltpu.SemaphoreType.DMA((2,)),
        ],
        input_output_aliases=aliases,
        compiler_params=params(24),
        cost_estimate=pl.CostEstimate(
            flops=6 * rows * group * tokens * head_dim,
            bytes_accessed=rows * block_width * 4,
            transcendentals=rows * group * tokens,
        ),
        name="attend",
    )(*operands)


def shards(queries, vis_feats, kv_weight, key_gain, cross_mask, image_tokens, image_owner):
    head_count = lax.axis_size("head")
    head_index = lax.axis_index("head")
    ctx_count = lax.axis_size("ctx")
    core = lax.axis_index("ctx") % 2
    ctx_bits = ctx_count.bit_length() - 1
    head_dim = key_gain.shape[0]
    kv_heads = kv_weight.shape[1] // (2 * head_dim)
    per_kv = head_count // kv_heads
    images = image_tokens.shape[0]

    masks = mask_columns(cross_mask, image_tokens, head_dim, queries.shape[0])
    partial_sums, (row_mask, token_bias) = sum_over_head(vis_feats, kv_weight, 2 * head_dim, masks)

    def spread(piece):
        block, other = finish_chunk(
            partial_sums[piece], key_gain, image_tokens, image_owner, per_kv, piece == 0
        )
        if per_kv > 1:
            groups = [[k * per_kv + j for j in range(per_kv)] for k in range(kv_heads)]
            block, other = lax.psum((block, other), "head", axis_index_groups=groups)
        block = block + swapped(other, "ctx", 0)
        for step in range(1, ctx_bits):
            pairs = [
                (c, c ^ (2**step if c % 2 == 0 else 2 ** (ctx_bits - step))) for c in range(ctx_count)
            ]
            block = block + lax.ppermute(block, "ctx", pairs)
        other = swapped(block, "ctx", 0)
        return jnp.where(
            core == 0, jnp.concatenate([block, other], 0), jnp.concatenate([other, block], 0)
        )

    keys, values = spread(0), spread(1)

    if per_kv > 1:
        groups = [[k * per_kv + j for k in range(kv_heads)] for j in range(per_kv)]
        keys = lax.all_gather(keys, "head", axis_index_groups=groups)
        values = lax.all_gather(values, "head", axis_index_groups=groups)
        out = None
        for k in range(kv_heads):
            ids = jnp.array([k, 1], jnp.int32)
            own = (keys[k], values[k], kv_heads, ids)
            out = attend(0, own, [], queries, row_mask, token_bias, kv_heads, images, out)
        return out

    def place(c, h):
        return c * head_count + h

    own = (keys, values, head_count, jnp.stack([head_index, 1 - 2 * core]).astype(jnp.int32))
    arrivals = []
    out = attend(0, own, arrivals, queries, row_mask, token_bias, kv_heads, images, None)
    passing = [keys, values]
    for hop in range(1, head_count):
        pairs = []
        for c in range(ctx_count):
            for i in range(hop - 1, head_count - 1):
                if c % 2 == 0:
                    pairs.append((place(c, i), place(c, i + 1)))
                else:
                    pairs.append((place(c, head_count - 1 - i), place(c, head_count - 2 - i)))
        crossing = [None, None]
        for piece in range(2):
            passing[piece] = lax.ppermute(passing[piece], ("ctx", "head"), pairs)
            crossing[piece] = swapped(passing[piece], "ctx", 0)
        arrivals.append([tuple(passing), tuple(crossing)])
        out = attend(hop, own, arrivals, queries, row_mask, token_bias, kv_heads, images, out)
    return out


def solution(mesh):
    return jax.shard_map(
        shards,
        mesh=mesh,
        in_specs=(
            P(("ctx", "head"), None),
            P("ctx", "head"),
            P("head", None),
            P(),
            P("ctx", None),
            P(),
            P(),
        ),
        out_specs=P(("ctx", "head"), None),
        check_vma=False,
    )
```

time: 114 us -> 120 us (1.053); the launches traced: 114 us -> 118 us
  waiting for transfers between devices: 33.7 us -> 17.9 us
  starting transfers between devices: 49 us -> 60.7 us
  Pallas kernels: 23 us -> 26.7 us
  other arithmetic: 1.14 us -> 4.8 us
    ppermute x5 -> x10, starting transfers between devices: 7.37 us -> 18.5 us  [the longest x6 12.4 us: shards(): passing[piece] = lax.ppermute(passing[piece], ('ctx', 'head'), pairs)]
    ppermute x5 -> x10, waiting for transfers between devices: 6.72 us -> 0.03 us  [swapped(): return lax.ppermute(value, axis, pairs)]
    ppermute x4, waiting for transfers between devices: 7.16 us -> 1.9 us  [sum_over_head(): to_left[piece] = lax.ppermute(left, 'head', left_pairs)]
    ppermute x5 -> x10, waiting for transfers between devices: 14.5 us -> 9.38 us  [the longest x4 6.23 us: spread(): block = block + lax.ppermute(block, 'ctx', pairs)]
    ppermute x2, waiting for transfers between devices: 2.22 us -> 5.84 us  [sum_over_head(): arrived = lax.ppermute(ends[piece], 'head', right_pairs + left_pairs)]
    ppermute x4, waiting for transfers between devices: 3.1 us -> 0.73 us  [sum_over_head(): to_right[piece] = lax.ppermute(right, 'head', right_pairs)]
    pallas_call x4, Pallas kernels: 16 us -> 17.9 us  [attend(): pl.pallas_call(kernel, in_specs=in_specs, out_specs=ANYWHERE, out_shape=j...]
    pallas_call x4, Pallas kernels: 6.07 us -> 7.75 us  [the longest x1 2.91 us: project_rest(): pl.pallas_call(kernel, in_specs=[SMEM, VMEM, VMEM], out_specs=[VMEM] * (2...]
  transfers between devices with their start and end apart: 20 -> 30, of which waited for: 13 -> 10; matrix products, arithmetic and copies ran while one was open for 1% -> 3% of each run, Pallas kernels for 15% -> 13%
where the time goes in v3:
time: 120 us; the launch traced here: 118 us
  starting transfers between devices  60.7 us (51%)
  Pallas kernels  26.7 us (22%)
  waiting for transfers between devices  17.9 us (15%)
  local copies, waits for them, and re-layouts  7.3 us (6%)
  other arithmetic  4.8 us (4%)
    ppermute x4, starting transfers between devices, sum_over_head(): to_right[piece] = lax.ppermute(right, 'head', right_pairs)  18.6 us
    pallas_call x4, Pallas kernels, attend(): pl.pallas_call(kernel, in_specs=in_specs, out_specs=ANYWHERE, out_shape=j...  17.9 us
    ppermute x10, starting transfers between devices, swapped(): return lax.ppermute(value, axis, pairs)  12.7 us
    ppermute x6, starting transfers between devices, shards(): passing[piece] = lax.ppermute(passing[piece], ('ctx', 'head'), pairs)  12.4 us
    unnamed x23, local copies, waits for them, and re-layouts  7.28 us
    ppermute x2, starting transfers between devices, sum_over_head(): arrived = lax.ppermute(ends[piece], 'head', right_pairs + left_pairs)  6.28 us
    ppermute x4, waiting for transfers between devices, spread(): block = block + lax.ppermute(block, 'ctx', pairs)  6.23 us
    ppermute x4, starting transfers between devices, spread(): block = block + lax.ppermute(block, 'ctx', pairs)  6.04 us
  transfers between devices with their start and end apart: 30, of which 10 were waited for; matrix products, arithmetic and copies ran while one was open for 3% of the time, Pallas kernels for 13%

profile of v3, /device:TPU:0, one launch (start us, length us, event | category | flops | bytes accessed | tf_op | source)
XLA Modules:
  0.0 117.9 jit_solution(10682562536060404420)
XLA Ops:
  1.5 2.2 %copy-done.2 = bf16[2048,1024]{1,0:T(8,128)(2,1)S(1)} copy-done((bf16[2048,1024]{1,0:T(8,128)(2,1)S(1)}, bf16[2048,1024]{1,0:T(8,128)(2,1)}, u32[]{:S(2)}) %copy-start.2) | copy-done | bytes 4194328
  3.7 1.6 %copy-done.3 = bf16[512,2048]{1,0:T(8,128)(2,1)S(1)} copy-done((bf16[512,2048]{1,0:T(8,128)(2,1)S(1)}, bf16[512,2048]{1,0:T(8,128)(2,1)}, u32[]{:S(2)}) %copy-start.3) | copy-done | bytes 2097176
  5.3 2.9 %project_rest.1 = (f32[512,128]{1,0:T(8,128)S(1)}, f32[512,128]{1,0:T(8,128)S(1)}, f32[512,128]{1,0:T(8,128)S(1)}, f32[512,128]{1,0:T(8,128)S(1)}, f32[512,128]{...) custom-call(s32[4]{0:T(128)S(1)} %and_select_fusion.ids_ref, ...), custom_call_target="tpu_custom_call" | custom-call | flops 2147483648 | bytes 4194304 | tf_op jit(solution)/shard_map/project_rest/pallas_call | solution.py:113
  8.2 2.6 %project.1 = (f32[512,128]{1,0:T(8,128)S(1)}, f32[512,128]{1,0:T(8,128)S(1)}) custom-call(s32[1]{0:T(128)} %bitcast.2.ids_ref, bf16[512,2048]{1,0:T(8,128)(2,1)} %feats_ref.1, bf16[2048,1024]{1,0:T(8,128)(2,1)} %weight_ref.1), custom_call_target="tpu_custom_call" | custom-call | flops 536870912 | bytes 3145728 | tf_op jit(solution)/shard_map/project/pallas_call | solution.py:69
  11.9 5.0 %collective-permute-start.11 = (f32[512,128]{1,0:T(8,128)S(1)}, f32[512,128]{1,0:T(8,128)S(1)}, u32[]{:S(2)}, u32[]{:S(2)}) collective-permute-start(f32[512,128]{1,0:T(8,128)S(1)} %get-tuple-element.37), channel_id=1, source_target_pairs={{0,1},{3,2},{4,5},{7,6},{8,9},{11,10},{12,13},{15,14},{16,17},{19,... | collective-permute-start | bytes 786440 | tf_op jit(solution)/shard_map/ppermute | solution.py:152
  16.9 1.3 %collective-permute-start = (f32[512,128]{1,0:T(8,128)S(1)}, f32[512,128]{1,0:T(8,128)S(1)}, u32[]{:S(2)}, u32[]{:S(2)}) collective-permute-start(f32[512,128]{1,0:T(8,128)S(1)} %get-tuple-element.30), channel_id=1, source_target_pairs={{0,1},{3,2},{4,5},{7,6},{8,9},{11,10},{12,13},{15,14},{16,17},{19,... | collective-permute-start | bytes 786440 | tf_op jit(solution)/shard_map/ppermute | solution.py:152
  18.2 5.3 %collective-permute-done.11 = f32[512,128]{1,0:T(8,128)S(1)} collective-permute-done((f32[512,128]{1,0:T(8,128)S(1)}, f32[512,128]{1,0:T(8,128)S(1)}, u32[]{:S(2)}, u32[]{:S(2)}) %collective-permute-start.11) | collective-permute-done | bytes 262176 | tf_op jit(solution)/shard_map/ppermute | solution.py:152
  23.6 4.4 %collective-permute-start.12 = (f32[512,128]{1,0:T(8,128)S(1)}, f32[512,128]{1,0:T(8,128)S(1)}, u32[]{:S(2)}, u32[]{:S(2)}) collective-permute-start(f32[512,128]{1,0:T(8,128)S(1)} %add.70), channel_id=1, source_target_pairs={{0,1},{1,2},{4,5},{5,6},{8,9},{9,10},{12,13},{13,14},{16,17},{17,1... | collective-permute-start | bytes 786440 | tf_op jit(solution)/shard_map/ppermute | solution.py:162
  29.9 1.4 %collective-permute-start.3 = (f32[512,128]{1,0:T(8,128)}, f32[512,128]{1,0:T(8,128)}, u32[]{:S(2)}, u32[]{:S(2)}) collective-permute-start(f32[512,128]{1,0:T(8,128)} %add.64), channel_id=1, source_target_pairs={{3,2},{2,1},{7,6},{6,5},{11,10},{10,9},{15,14},{14,13},{19,18},{18... | collective-permute-start | bytes 786440 | tf_op jit(solution)/shard_map/ppermute | solution.py:163
  31.3 5.0 %collective-permute-start.1 = (f32[512,128]{1,0:T(8,128)}, f32[512,128]{1,0:T(8,128)}, u32[]{:S(2)}, u32[]{:S(2)}) collective-permute-start(f32[512,128]{1,0:T(8,128)} %add.64), channel_id=1, source_target_pairs={{0,1},{1,2},{4,5},{5,6},{8,9},{9,10},{12,13},{13,14},{16,17},{17,1... | collective-permute-start | bytes 786440 | tf_op jit(solution)/shard_map/ppermute | solution.py:162
  36.3 4.0 %collective-permute-start.13 = (f32[512,128]{1,0:T(8,128)S(1)}, f32[512,128]{1,0:T(8,128)S(1)}, u32[]{:S(2)}, u32[]{:S(2)}) collective-permute-start(f32[512,128]{1,0:T(8,128)S(1)} %add.71), channel_id=1, source_target_pairs={{0,1},{1,2},{2,3},{4,5},{5,6},{6,7},{8,9},{9,10},{10,11},{12,13},{... | collective-permute-start | bytes 786440 | tf_op jit(solution)/shard_map/ppermute | solution.py:162
  45.7 5.2 %collective-permute-start.2 = (f32[512,128]{1,0:T(8,128)S(1)}, f32[512,128]{1,0:T(8,128)S(1)}, u32[]{:S(2)}, u32[]{:S(2)}) collective-permute-start(f32[512,128]{1,0:T(8,128)S(1)} %add.65), channel_id=1, source_target_pairs={{0,1},{1,2},{2,3},{4,5},{5,6},{6,7},{8,9},{9,10},{10,11},{12,13},{... | collective-permute-start | bytes 786440 | tf_op jit(solution)/shard_map/ppermute | solution.py:162
  52.4 1.7 %collective-permute-done.4.right_ref = f32[512,128]{1,0:T(8,128)S(1)} collective-permute-done((f32[512,128]{1,0:T(8,128)S(1)}, f32[512,128]{1,0:T(8,128)S(1)}, u32[]{:S(2)}, u32[]{:S(2)}) %collective-permute-start.4) | collective-permute-done | bytes 262176 | tf_op jit(solution)/shard_map/ppermute | solution.py:163
  56.1 1.6 %collective-permute-start.17 = (bf16[640,128]{1,0:T(8,128)(2,1)S(1)}, bf16[640,128]{1,0:T(8,128)(2,1)S(1)}, u32[]{:S(2)}, u32[]{:S(2)}) collective-permute-start(bf16[640,128]{1,0:T(8,128)(2,1)S(1)} %add.73), channel_id=1, source_target_pairs={{0,8},{4,20},{8,0},{12,28},{16,24},{20,4},{24,16},{28,12},{1,9},{5... | collective-permute-start | bytes 491528 | tf_op jit(solution)/shard_map/ppermute | solution.py:372
  57.7 1.3 %collective-permute-start.6 = (bf16[640,128]{1,0:T(8,128)(2,1)S(1)}, bf16[640,128]{1,0:T(8,128)(2,1)S(1)}, u32[]{:S(2)}, u32[]{:S(2)}) collective-permute-start(bf16[640,128]{1,0:T(8,128)(2,1)S(1)} %add.67), channel_id=1, source_target_pairs={{0,8},{4,20},{8,0},{12,28},{16,24},{20,4},{24,16},{28,12},{1,9},{5... | collective-permute-start | bytes 491528 | tf_op jit(solution)/shard_map/ppermute | solution.py:372
  59.0 2.5 %collective-permute-done.17 = bf16[640,128]{1,0:T(8,128)(2,1)S(1)} collective-permute-done((bf16[640,128]{1,0:T(8,128)(2,1)S(1)}, bf16[640,128]{1,0:T(8,128)(2,1)S(1)}, u32[]{:S(2)}, u32[]{:S(2)}) %collective-permute-start.17) | collective-permute-done | bytes 163872 | tf_op jit(solution)/shard_map/ppermute | solution.py:372
  61.5 1.6 %collective-permute-start.18 = (bf16[640,128]{1,0:T(8,128)(2,1)S(1)}, bf16[640,128]{1,0:T(8,128)(2,1)S(1)}, u32[]{:S(2)}, u32[]{:S(2)}) collective-permute-start(bf16[640,128]{1,0:T(8,128)(2,1)S(1)} %add.74), channel_id=1, source_target_pairs={{0,16},{4,12},{8,24},{12,4},{16,0},{20,28},{24,8},{28,20},{1,17},{... | collective-permute-start | bytes 491528 | tf_op jit(solution)/shard_map/ppermute | solution.py:372
  63.3 1.6 %collective-permute-start.7 = (bf16[640,128]{1,0:T(8,128)(2,1)S(1)}, bf16[640,128]{1,0:T(8,128)(2,1)S(1)}, u32[]{:S(2)}, u32[]{:S(2)}) collective-permute-start(bf16[640,128]{1,0:T(8,128)(2,1)S(1)} %add.68), channel_id=1, source_target_pairs={{0,16},{4,12},{8,24},{12,4},{16,0},{20,28},{24,8},{28,20},{1,17},{... | collective-permute-start | bytes 491528 | tf_op jit(solution)/shard_map/ppermute | solution.py:372
  64.8 2.0 %collective-permute-done.18 = bf16[640,128]{1,0:T(8,128)(2,1)S(1)} collective-permute-done((bf16[640,128]{1,0:T(8,128)(2,1)S(1)}, bf16[640,128]{1,0:T(8,128)(2,1)S(1)}, u32[]{:S(2)}, u32[]{:S(2)}) %collective-permute-start.18) | collective-permute-done | bytes 163872 | tf_op jit(solution)/shard_map/ppermute | solution.py:372
  67.0 1.6 %collective-permute-done.7 = bf16[640,128]{1,0:T(8,128)(2,1)S(1)} collective-permute-done((bf16[640,128]{1,0:T(8,128)(2,1)S(1)}, bf16[640,128]{1,0:T(8,128)(2,1)S(1)}, u32[]{:S(2)}, u32[]{:S(2)}) %collective-permute-start.7) | collective-permute-done | bytes 163872 | tf_op jit(solution)/shard_map/ppermute | solution.py:372
  68.9 4.4 %collective-permute-start.20 = (bf16[1280,128]{1,0:T(8,128)(2,1)S(1)}, bf16[1280,128]{1,0:T(8,128)(2,1)S(1)}, u32[]{:S(2)}, u32[]{:S(2)}) collective-permute-start(bf16[1280,128]{1,0:T(8,128)(2,1)S(1)} %maximum_select_fusion.1.refs_5_), channel_id=1, source_target_pairs={{0,1},{1,2},{2,3},{7,6},{6,5},{5,4},{8,9},{9,10},{10,11},{15,14},{... | collective-permute-start | bytes 983048 | tf_op jit(solution)/shard_map/ppermute | solution.py:408
  73.4 3.9 %collective-permute-start.9 = (bf16[1280,128]{1,0:T(8,128)(2,1)S(1)}, bf16[1280,128]{1,0:T(8,128)(2,1)S(1)}, u32[]{:S(2)}, u32[]{:S(2)}) collective-permute-start(bf16[1280,128]{1,0:T(8,128)(2,1)S(1)} %maximum_select_fusion.refs_4_), channel_id=1, source_target_pairs={{0,1},{1,2},{2,3},{7,6},{6,5},{5,4},{8,9},{9,10},{10,11},{15,14},{... | collective-permute-start | bytes 983048 | tf_op jit(solution)/shard_map/ppermute | solution.py:408
  78.8 3.1 %collective-permute-done.9.refs_4_ = bf16[1280,128]{1,0:T(8,128)(2,1)S(1)} collective-permute-done((bf16[1280,128]{1,0:T(8,128)(2,1)S(1)}, bf16[1280,128]{1,0:T(8,128)(2,1)S(1)}, u32[]{:S(2)}, u32[]{:S(2)}) %collective-permute-start.9) | collective-permute-done | bytes 327712 | tf_op jit(solution)/shard_map/ppermute | solution.py:408
  82.8 1.4 %collective-permute-start.25 = (bf16[1280,128]{1,0:T(8,128)(2,1)S(1)}, bf16[1280,128]{1,0:T(8,128)(2,1)}, u32[]{:S(2)}, u32[]{:S(2)}) collective-permute-start(bf16[1280,128]{1,0:T(8,128)(2,1)S(1)} %collective-permute-done.21.refs_9_.refs_5_), channel_id=1, source_target_pairs={{2,3},{5,4},{10,11},{13,12},{18,19},{21,20},{26,27},{29,28}} | collective-permute-start | bytes 983048 | tf_op jit(solution)/shard_map/ppermute | solution.py:408
  84.2 1.4 %collective-permute-start.24 = (bf16[1280,128]{1,0:T(8,128)(2,1)S(1)}, bf16[1280,128]{1,0:T(8,128)(2,1)}, u32[]{:S(2)}, u32[]{:S(2)}) collective-permute-start(bf16[1280,128]{1,0:T(8,128)(2,1)S(1)} %collective-permute-done.10.refs_8_.refs_4_), channel_id=1, source_target_pairs={{2,3},{5,4},{10,11},{13,12},{18,19},{21,20},{26,27},{29,28}} | collective-permute-start | bytes 983048 | tf_op jit(solution)/shard_map/ppermute | solution.py:408
  85.6 5.6 %collective-permute-start.28 = (bf16[1280,128]{1,0:T(8,128)(2,1)S(1)}, bf16[1280,128]{1,0:T(8,128)(2,1)}, u32[]{:S(2)}, u32[]{:S(2)}) collective-permute-start(bf16[1280,128]{1,0:T(8,128)(2,1)S(1)} %collective-permute-done.9.refs_4_), channel_id=1, source_target_pairs={{0,4},{4,0},{8,12},{12,8},{16,20},{20,16},{24,28},{28,24},{1,5},{5... | collective-permute-start | bytes 983048 | tf_op jit(solution)/shard_map/ppermute | solution.py:29
  91.7 2.5 %collective-permute-start.27 = (bf16[1280,128]{1,0:T(8,128)(2,1)}, bf16[1280,128]{1,0:T(8,128)(2,1)S(1)}, u32[]{:S(2)}, u32[]{:S(2)}) collective-permute-start(bf16[1280,128]{1,0:T(8,128)(2,1)} %collective-permute-done.25.refs_9_), channel_id=1, source_target_pairs={{0,4},{4,0},{8,12},{12,8},{16,20},{20,16},{24,28},{28,24},{1,5},{5... | collective-permute-start | bytes 983048 | tf_op jit(solution)/shard_map/ppermute | solution.py:29
  94.2 3.5 %collective-permute-start.26 = (bf16[1280,128]{1,0:T(8,128)(2,1)}, bf16[1280,128]{1,0:T(8,128)(2,1)S(1)}, u32[]{:S(2)}, u32[]{:S(2)}) collective-permute-start(bf16[1280,128]{1,0:T(8,128)(2,1)} %collective-permute-done.24.refs_8_), channel_id=1, source_target_pairs={{0,4},{4,0},{8,12},{12,8},{16,20},{20,16},{24,28},{28,24},{1,5},{5... | collective-permute-start | bytes 983048 | tf_op jit(solution)/shard_map/ppermute | solution.py:29
  99.8 4.0 %attend.4.refs_8_ = bf16[128,4096]{1,0:T(8,128)(2,1)} custom-call(s32[2]{0:T(128)S(1)} %pad_add_fusion.refs_0_, bf16[128,4096]{1,0:T(8,128)(2,1)S(1)} %copy-done.1, bf16[128,128]{1,0:T(8,128)(2,1)S(1)} %pad.5.refs_2_, bf16[1280,128]{1,0:T(8,128)(2,1)S(1)} %token_bias.1.refs_3_, bf16[1280,128]{1,0:T(8,128)(2,1)S(1)} %copy-done.7, bf16[1280,128]{1,0:T(8,128)(2,1)S(1)} %copy-done.5), custom_call_target="tpu_custom_call" | custom-call | flops 1006632960 | bytes 524288 | tf_op jit(solution)/shard_map/attend/pallas_call | solution.py:323
  103.8 4.6 %attend.5.refs_12_ = bf16[128,4096]{1,0:T(8,128)(2,1)} custom-call(s32[2]{0:T(128)S(1)} %pad_add_fusion.refs_0_, bf16[128,4096]{1,0:T(8,128)(2,1)S(1)} %copy-done.1, bf16[128,128]{1,0:T(8,128)(2,1)S(1)} %pad.5.refs_2_, bf16[1280,128]{1,0:T(8,128)(2,1)S(1)} %token_bias.1.refs_3_, ...), custom_call_target="tpu_custom_call", output_to_operand_aliasing={{}: (8, {})} | custom-call | flops 1006632960 | bytes 524288 | tf_op jit(solution)/shard_map/attend/pallas_call | solution.py:323
  108.5 4.6 %attend.6.refs_12_ = bf16[128,4096]{1,0:T(8,128)(2,1)} custom-call(s32[2]{0:T(128)S(1)} %pad_add_fusion.refs_0_, bf16[128,4096]{1,0:T(8,128)(2,1)S(1)} %copy-done.1, bf16[128,128]{1,0:T(8,128)(2,1)S(1)} %pad.5.refs_2_, bf16[1280,128]{1,0:T(8,128)(2,1)S(1)} %token_bias.1.refs_3_, ...), custom_call_target="tpu_custom_call", output_to_operand_aliasing={{}: (12, {})} | custom-call | flops 1006632960 | bytes 524288 | tf_op jit(solution)/shard_map/attend/pallas_call | solution.py:323
  113.1 4.7 %attend.7 = bf16[128,4096]{1,0:T(8,128)(2,1)} custom-call(s32[2]{0:T(128)S(1)} %pad_add_fusion.refs_0_, bf16[128,4096]{1,0:T(8,128)(2,1)S(1)} %copy-done.1, bf16[128,128]{1,0:T(8,128)(2,1)S(1)} %pad.5.refs_2_, bf16[1280,128]{1,0:T(8,128)(2,1)S(1)} %token_bias.1.refs_3_, ...), custom_call_target="tpu_custom_call", output_to_operand_aliasing={{}: (12, {})} | custom-call | flops 1006632960 | bytes 524288 | tf_op jit(solution)/shard_map/attend/pallas_call | solution.py:323
  (80 shorter events, 18.8 us)
Async XLA Ops:
  8.2 43.0 %copy-start.9 = (s32[4]{0:T(128)S(1)}, s32[4]{0:T(128)}, u32[]{:S(2)}) copy-start(s32[4]{0:T(128)} %owner_ref.3) | copy-start | bytes 52
  11.9 11.6 %collective-permute-start.11 = (f32[512,128]{1,0:T(8,128)S(1)}, f32[512,128]{1,0:T(8,128)S(1)}, u32[]{:S(2)}, u32[]{:S(2)}) collective-permute-start(f32[512,128]{1,0:T(8,128)S(1)} %get-tuple-element.37), channel_id=1, source_target_pairs={{0,1},{3,2},{4,5},{7,6},{8,9},{11,10},{12,13},{15,14},{16,17},{19,... | collective-permute-start | bytes 786440 | tf_op jit(solution)/shard_map/ppermute | solution.py:152
  16.9 12.3 %collective-permute-start = (f32[512,128]{1,0:T(8,128)S(1)}, f32[512,128]{1,0:T(8,128)S(1)}, u32[]{:S(2)}, u32[]{:S(2)}) collective-permute-start(f32[512,128]{1,0:T(8,128)S(1)} %get-tuple-element.30), channel_id=1, source_target_pairs={{0,1},{3,2},{4,5},{7,6},{8,9},{11,10},{12,13},{15,14},{16,17},{19,... | collective-permute-start | bytes 786440 | tf_op jit(solution)/shard_map/ppermute | solution.py:152
  23.6 12.7 %collective-permute-start.12 = (f32[512,128]{1,0:T(8,128)S(1)}, f32[512,128]{1,0:T(8,128)S(1)}, u32[]{:S(2)}, u32[]{:S(2)}) collective-permute-start(f32[512,128]{1,0:T(8,128)S(1)} %add.70), channel_id=1, source_target_pairs={{0,1},{1,2},{4,5},{5,6},{8,9},{9,10},{12,13},{13,14},{16,17},{17,1... | collective-permute-start | bytes 786440 | tf_op jit(solution)/shard_map/ppermute | solution.py:162
  28.0 12.4 %collective-permute-start.14 = (f32[512,128]{1,0:T(8,128)S(1)}, f32[512,128]{1,0:T(8,128)S(1)}, u32[]{:S(2)}, u32[]{:S(2)}) collective-permute-start(f32[512,128]{1,0:T(8,128)S(1)} %add.70), channel_id=1, source_target_pairs={{3,2},{2,1},{7,6},{6,5},{11,10},{10,9},{15,14},{14,13},{19,18},{18... | collective-permute-start | bytes 786440 | tf_op jit(solution)/shard_map/ppermute | solution.py:163
  29.9 12.5 %collective-permute-start.3 = (f32[512,128]{1,0:T(8,128)}, f32[512,128]{1,0:T(8,128)}, u32[]{:S(2)}, u32[]{:S(2)}) collective-permute-start(f32[512,128]{1,0:T(8,128)} %add.64), channel_id=1, source_target_pairs={{3,2},{2,1},{7,6},{6,5},{11,10},{10,9},{15,14},{14,13},{19,18},{18... | collective-permute-start | bytes 786440 | tf_op jit(solution)/shard_map/ppermute | solution.py:163
  31.3 13.4 %collective-permute-start.1 = (f32[512,128]{1,0:T(8,128)}, f32[512,128]{1,0:T(8,128)}, u32[]{:S(2)}, u32[]{:S(2)}) collective-permute-start(f32[512,128]{1,0:T(8,128)} %add.64), channel_id=1, source_target_pairs={{0,1},{1,2},{4,5},{5,6},{8,9},{9,10},{12,13},{13,14},{16,17},{17,1... | collective-permute-start | bytes 786440 | tf_op jit(solution)/shard_map/ppermute | solution.py:162
  36.3 61.5 %copy-start.1 = (bf16[128,4096]{1,0:T(8,128)(2,1)S(1)}, bf16[128,4096]{1,0:T(8,128)(2,1)}, u32[]{:S(2)}) copy-start(bf16[128,4096]{1,0:T(8,128)(2,1)} %refs_1_.7) | copy-start | bytes 3145732
  36.3 14.7 %collective-permute-start.13 = (f32[512,128]{1,0:T(8,128)S(1)}, f32[512,128]{1,0:T(8,128)S(1)}, u32[]{:S(2)}, u32[]{:S(2)}) collective-permute-start(f32[512,128]{1,0:T(8,128)S(1)} %add.71), channel_id=1, source_target_pairs={{0,1},{1,2},{2,3},{4,5},{5,6},{6,7},{8,9},{9,10},{10,11},{12,13},{... | collective-permute-start | bytes 786440 | tf_op jit(solution)/shard_map/ppermute | solution.py:162
  41.1 10.1 %collective-permute-start.15 = (f32[512,128]{1,0:T(8,128)}, f32[512,128]{1,0:T(8,128)S(1)}, u32[]{:S(2)}, u32[]{:S(2)}) collective-permute-start(f32[512,128]{1,0:T(8,128)} %add.72), channel_id=1, source_target_pairs={{3,2},{2,1},{1,0},{7,6},{6,5},{5,4},{11,10},{10,9},{9,8},{15,14},{... | collective-permute-start | bytes 786440 | tf_op jit(solution)/shard_map/ppermute | solution.py:163
  43.4 10.6 %collective-permute-start.4 = (f32[512,128]{1,0:T(8,128)S(1)}, f32[512,128]{1,0:T(8,128)S(1)}, u32[]{:S(2)}, u32[]{:S(2)}) collective-permute-start(f32[512,128]{1,0:T(8,128)S(1)} %add.66), channel_id=1, source_target_pairs={{3,2},{2,1},{1,0},{7,6},{6,5},{5,4},{11,10},{10,9},{9,8},{15,14},{... | collective-permute-start | bytes 786440 | tf_op jit(solution)/shard_map/ppermute | solution.py:163
  45.7 9.1 %collective-permute-start.2 = (f32[512,128]{1,0:T(8,128)S(1)}, f32[512,128]{1,0:T(8,128)S(1)}, u32[]{:S(2)}, u32[]{:S(2)}) collective-permute-start(f32[512,128]{1,0:T(8,128)S(1)} %add.65), channel_id=1, source_target_pairs={{0,1},{1,2},{2,3},{4,5},{5,6},{6,7},{8,9},{9,10},{10,11},{12,13},{... | collective-permute-start | bytes 786440 | tf_op jit(solution)/shard_map/ppermute | solution.py:162
  52.3 3.7 %collective-permute-start.16 = (bf16[640,128]{1,0:T(8,128)(2,1)S(1)}, bf16[640,128]{1,0:T(8,128)(2,1)S(1)}, u32[]{:S(2)}, u32[]{:S(2)}) collective-permute-start(bf16[640,128]{1,0:T(8,128)(2,1)S(1)} %get-tuple-element.40), channel_id=1, source_target_pairs={{0,4},{4,0},{8,12},{12,8},{16,20},{20,16},{24,28},{28,24},{1,5},{5... | collective-permute-start | bytes 491528 | tf_op jit(solution)/shard_map/ppermute | solution.py:29
  55.9 1.7 %collective-permute-start.5 = (bf16[640,128]{1,0:T(8,128)(2,1)S(1)}, bf16[640,128]{1,0:T(8,128)(2,1)S(1)}, u32[]{:S(2)}, u32[]{:S(2)}) collective-permute-start(bf16[640,128]{1,0:T(8,128)(2,1)S(1)} %get-tuple-element.33), channel_id=1, source_target_pairs={{0,4},{4,0},{8,12},{12,8},{16,20},{20,16},{24,28},{28,24},{1,5},{5... | collective-permute-start | bytes 491528 | tf_op jit(solution)/shard_map/ppermute | solution.py:29
  56.1 5.4 %collective-permute-start.17 = (bf16[640,128]{1,0:T(8,128)(2,1)S(1)}, bf16[640,128]{1,0:T(8,128)(2,1)S(1)}, u32[]{:S(2)}, u32[]{:S(2)}) collective-permute-start(bf16[640,128]{1,0:T(8,128)(2,1)S(1)} %add.73), channel_id=1, source_target_pairs={{0,8},{4,20},{8,0},{12,28},{16,24},{20,4},{24,16},{28,12},{1,9},{5... | collective-permute-start | bytes 491528 | tf_op jit(solution)/shard_map/ppermute | solution.py:372
  57.7 5.5 %collective-permute-start.6 = (bf16[640,128]{1,0:T(8,128)(2,1)S(1)}, bf16[640,128]{1,0:T(8,128)(2,1)S(1)}, u32[]{:S(2)}, u32[]{:S(2)}) collective-permute-start(bf16[640,128]{1,0:T(8,128)(2,1)S(1)} %add.67), channel_id=1, source_target_pairs={{0,8},{4,20},{8,0},{12,28},{16,24},{20,4},{24,16},{28,12},{1,9},{5... | collective-permute-start | bytes 491528 | tf_op jit(solution)/shard_map/ppermute | solution.py:372
  61.5 5.4 %collective-permute-start.18 = (bf16[640,128]{1,0:T(8,128)(2,1)S(1)}, bf16[640,128]{1,0:T(8,128)(2,1)S(1)}, u32[]{:S(2)}, u32[]{:S(2)}) collective-permute-start(bf16[640,128]{1,0:T(8,128)(2,1)S(1)} %add.74), channel_id=1, source_target_pairs={{0,16},{4,12},{8,24},{12,4},{16,0},{20,28},{24,8},{28,20},{1,17},{... | collective-permute-start | bytes 491528 | tf_op jit(solution)/shard_map/ppermute | solution.py:372
  63.3 5.4 %collective-permute-start.7 = (bf16[640,128]{1,0:T(8,128)(2,1)S(1)}, bf16[640,128]{1,0:T(8,128)(2,1)S(1)}, u32[]{:S(2)}, u32[]{:S(2)}) collective-permute-start(bf16[640,128]{1,0:T(8,128)(2,1)S(1)} %add.68), channel_id=1, source_target_pairs={{0,16},{4,12},{8,24},{12,4},{16,0},{20,28},{24,8},{28,20},{1,17},{... | collective-permute-start | bytes 491528 | tf_op jit(solution)/shard_map/ppermute | solution.py:372
  66.9 1.8 %collective-permute-start.19 = (bf16[640,128]{1,0:T(8,128)(2,1)S(1)}, bf16[640,128]{1,0:T(8,128)(2,1)S(1)}, u32[]{:S(2)}, u32[]{:S(2)}) collective-permute-start(bf16[640,128]{1,0:T(8,128)(2,1)S(1)} %add.75), channel_id=1, source_target_pairs={{0,4},{4,0},{8,12},{12,8},{16,20},{20,16},{24,28},{28,24},{1,5},{5... | collective-permute-start | bytes 491528 | tf_op jit(solution)/shard_map/ppermute | solution.py:29
  68.7 4.6 %collective-permute-start.8 = (bf16[640,128]{1,0:T(8,128)(2,1)S(1)}, bf16[640,128]{1,0:T(8,128)(2,1)S(1)}, u32[]{:S(2)}, u32[]{:S(2)}) collective-permute-start(bf16[640,128]{1,0:T(8,128)(2,1)S(1)} %add.69), channel_id=1, source_target_pairs={{0,4},{4,0},{8,12},{12,8},{16,20},{20,16},{24,28},{28,24},{1,5},{5... | collective-permute-start | bytes 491528 | tf_op jit(solution)/shard_map/ppermute | solution.py:29
  68.9 9.2 %collective-permute-start.20 = (bf16[1280,128]{1,0:T(8,128)(2,1)S(1)}, bf16[1280,128]{1,0:T(8,128)(2,1)S(1)}, u32[]{:S(2)}, u32[]{:S(2)}) collective-permute-start(bf16[1280,128]{1,0:T(8,128)(2,1)S(1)} %maximum_select_fusion.1.refs_5_), channel_id=1, source_target_pairs={{0,1},{1,2},{2,3},{7,6},{6,5},{5,4},{8,9},{9,10},{10,11},{15,14},{... | collective-permute-start | bytes 983048 | tf_op jit(solution)/shard_map/ppermute | solution.py:408
  73.4 8.5 %collective-permute-start.9 = (bf16[1280,128]{1,0:T(8,128)(2,1)S(1)}, bf16[1280,128]{1,0:T(8,128)(2,1)S(1)}, u32[]{:S(2)}, u32[]{:S(2)}) collective-permute-start(bf16[1280,128]{1,0:T(8,128)(2,1)S(1)} %maximum_select_fusion.refs_4_), channel_id=1, source_target_pairs={{0,1},{1,2},{2,3},{7,6},{6,5},{5,4},{8,9},{9,10},{10,11},{15,14},{... | collective-permute-start | bytes 983048 | tf_op jit(solution)/shard_map/ppermute | solution.py:408
  78.1 4.7 %collective-permute-start.21 = (bf16[1280,128]{1,0:T(8,128)(2,1)S(1)}, bf16[1280,128]{1,0:T(8,128)(2,1)S(1)}, u32[]{:S(2)}, u32[]{:S(2)}) collective-permute-start(bf16[1280,128]{1,0:T(8,128)(2,1)S(1)} %collective-permute-done.20.refs_5_), channel_id=1, source_target_pairs={{1,2},{2,3},{6,5},{5,4},{9,10},{10,11},{14,13},{13,12},{17,18},{18... | collective-permute-start | bytes 983048 | tf_op jit(solution)/shard_map/ppermute | solution.py:408
  81.9 2.3 %collective-permute-start.10 = (bf16[1280,128]{1,0:T(8,128)(2,1)S(1)}, bf16[1280,128]{1,0:T(8,128)(2,1)S(1)}, u32[]{:S(2)}, u32[]{:S(2)}) collective-permute-start(bf16[1280,128]{1,0:T(8,128)(2,1)S(1)} %collective-permute-done.9.refs_4_), channel_id=1, source_target_pairs={{1,2},{2,3},{6,5},{5,4},{9,10},{10,11},{14,13},{13,12},{17,18},{18... | collective-permute-start | bytes 983048 | tf_op jit(solution)/shard_map/ppermute | solution.py:408
  82.6 8.7 %collective-permute-start.29 = (bf16[1280,128]{1,0:T(8,128)(2,1)S(1)}, bf16[1280,128]{1,0:T(8,128)(2,1)S(1)}, u32[]{:S(2)}, u32[]{:S(2)}) collective-permute-start(bf16[1280,128]{1,0:T(8,128)(2,1)S(1)} %collective-permute-done.20.refs_5_), channel_id=1, source_target_pairs={{0,4},{4,0},{8,12},{12,8},{16,20},{20,16},{24,28},{28,24},{1,5},{5... | collective-permute-start | bytes 983048 | tf_op jit(solution)/shard_map/ppermute | solution.py:29
  82.8 8.9 %collective-permute-start.25 = (bf16[1280,128]{1,0:T(8,128)(2,1)S(1)}, bf16[1280,128]{1,0:T(8,128)(2,1)}, u32[]{:S(2)}, u32[]{:S(2)}) collective-permute-start(bf16[1280,128]{1,0:T(8,128)(2,1)S(1)} %collective-permute-done.21.refs_9_.refs_5_), channel_id=1, source_target_pairs={{2,3},{5,4},{10,11},{13,12},{18,19},{21,20},{26,27},{29,28}} | collective-permute-start | bytes 983048 | tf_op jit(solution)/shard_map/ppermute | solution.py:408
  84.2 10.0 %collective-permute-start.24 = (bf16[1280,128]{1,0:T(8,128)(2,1)S(1)}, bf16[1280,128]{1,0:T(8,128)(2,1)}, u32[]{:S(2)}, u32[]{:S(2)}) collective-permute-start(bf16[1280,128]{1,0:T(8,128)(2,1)S(1)} %collective-permute-done.10.refs_8_.refs_4_), channel_id=1, source_target_pairs={{2,3},{5,4},{10,11},{13,12},{18,19},{21,20},{26,27},{29,28}} | collective-permute-start | bytes 983048 | tf_op jit(solution)/shard_map/ppermute | solution.py:408
  85.6 18.2 %collective-permute-start.28 = (bf16[1280,128]{1,0:T(8,128)(2,1)S(1)}, bf16[1280,128]{1,0:T(8,128)(2,1)}, u32[]{:S(2)}, u32[]{:S(2)}) collective-permute-start(bf16[1280,128]{1,0:T(8,128)(2,1)S(1)} %collective-permute-done.9.refs_4_), channel_id=1, source_target_pairs={{0,4},{4,0},{8,12},{12,8},{16,20},{20,16},{24,28},{28,24},{1,5},{5... | collective-permute-start | bytes 983048 | tf_op jit(solution)/shard_map/ppermute | solution.py:29
  91.2 17.2 %collective-permute-start.23 = (bf16[1280,128]{1,0:T(8,128)(2,1)S(1)}, bf16[1280,128]{1,0:T(8,128)(2,1)S(1)}, u32[]{:S(2)}, u32[]{:S(2)}) collective-permute-start(bf16[1280,128]{1,0:T(8,128)(2,1)S(1)} %collective-permute-done.21.refs_9_.refs_5_), channel_id=1, source_target_pairs={{0,4},{4,0},{8,12},{12,8},{16,20},{20,16},{24,28},{28,24},{1,5},{5... | collective-permute-start | bytes 983048 | tf_op jit(solution)/shard_map/ppermute | solution.py:29
  91.3 17.2 %collective-permute-start.22 = (bf16[1280,128]{1,0:T(8,128)(2,1)S(1)}, bf16[1280,128]{1,0:T(8,128)(2,1)}, u32[]{:S(2)}, u32[]{:S(2)}) collective-permute-start(bf16[1280,128]{1,0:T(8,128)(2,1)S(1)} %collective-permute-done.10.refs_8_.refs_4_), channel_id=1, source_target_pairs={{0,4},{4,0},{8,12},{12,8},{16,20},{20,16},{24,28},{28,24},{1,5},{5... | collective-permute-start | bytes 983048 | tf_op jit(solution)/shard_map/ppermute | solution.py:29
  91.7 21.3 %collective-permute-start.27 = (bf16[1280,128]{1,0:T(8,128)(2,1)}, bf16[1280,128]{1,0:T(8,128)(2,1)S(1)}, u32[]{:S(2)}, u32[]{:S(2)}) collective-permute-start(bf16[1280,128]{1,0:T(8,128)(2,1)} %collective-permute-done.25.refs_9_), channel_id=1, source_target_pairs={{0,4},{4,0},{8,12},{12,8},{16,20},{20,16},{24,28},{28,24},{1,5},{5... | collective-permute-start | bytes 983048 | tf_op jit(solution)/shard_map/ppermute | solution.py:29
  94.2 18.8 %collective-permute-start.26 = (bf16[1280,128]{1,0:T(8,128)(2,1)}, bf16[1280,128]{1,0:T(8,128)(2,1)S(1)}, u32[]{:S(2)}, u32[]{:S(2)}) collective-permute-start(bf16[1280,128]{1,0:T(8,128)(2,1)} %collective-permute-done.24.refs_8_), channel_id=1, source_target_pairs={{0,4},{4,0},{8,12},{12,8},{16,20},{20,16},{24,28},{28,24},{1,5},{5... | collective-permute-start | bytes 983048 | tf_op jit(solution)/shard_map/ppermute | solution.py:29
  (9 other events, 61.3 us)

commit v4 on v3

v4 whole, which is shorter than its diff:
```python
import math

import jax
import jax.numpy as jnp
from jax import lax
from jax.experimental import pallas as pl
from jax.experimental.pallas import tpu as pltpu
from jax.sharding import PartitionSpec as P

EPSILON = 1e-05
FLOOR_SCORE = -1e30
KV_TOTAL = 1280
STACK = 2
MIB = 2**20

VMEM = pl.BlockSpec(memory_space=pltpu.VMEM)
SMEM = pl.BlockSpec(memory_space=pltpu.SMEM)
ANYWHERE = pl.BlockSpec(memory_space=pl.ANY)
HBM = pl.BlockSpec(memory_space=pltpu.HBM)


def params(mib):
    return pltpu.CompilerParams(vmem_limit_bytes=mib * MIB)


def swapped(value, axis, bit):
    mask = 2**bit
    pairs = [(source, source ^ mask) for source in range(lax.axis_size(axis))]
    return lax.ppermute(value, axis, pairs)


def project(chunk_of, wanted, vis_feats, kv_weight, pair):
    count = lax.axis_size("head")
    rows, width = vis_feats.shape
    per_kv = count // (kv_weight.shape[1] // pair)
    block_rows = rows // per_kv
    head_dim = pair // 2
    alone = wanted == 1
    steps = 4
    few, deep = rows // steps, width // steps

    def kernel(feats_ref, weight_ref, *refs):
        out_refs = refs[: 2 * wanted]
        chunks = [chunk_of(lax.axis_index("head"), n) for n in range(wanted)]
        columns = [pl.multiple_of((chunk // per_kv) * pair, pair) for chunk in chunks]
        if alone:
            feats_vmem, weight_vmem, sems = refs[2 * wanted :]
            copies = []
            for n in range(steps):
                span = pl.ds(n * few, few)
                copies.append((feats_ref.at[span], feats_vmem.at[span], sems.at[n]))
            for n in range(steps):
                span = pl.ds(n * deep, deep)
                source = weight_ref.at[span, pl.ds(columns[0], pair)]
                copies.append((source, weight_vmem.at[span], sems.at[steps + n]))
            copies = [pltpu.make_async_copy(*copy) for copy in copies]
            for copy in copies:
                copy.start()
            for copy in copies:
                copy.wait()
            feats_ref, weight_ref, columns = feats_vmem, weight_vmem, [0]
        for n in range(wanted):
            row = 0 if per_kv == 1 else pl.multiple_of((chunks[n] % per_kv) * block_rows, block_rows)
            out = jnp.dot(
                feats_ref[pl.ds(row, block_rows), :],
                weight_ref[:, pl.ds(columns[n], pair)],
                preferred_element_type=jnp.float32,
            )
            out_refs[2 * n][...] = out[:, :head_dim]
            out_refs[2 * n + 1][...] = out[:, head_dim:]

    scratch = [
        pltpu.VMEM((rows, width), vis_feats.dtype),
        pltpu.VMEM((width, pair), kv_weight.dtype),
        pltpu.SemaphoreType.DMA((2 * steps,)),
    ]
    if alone:
        vis_feats = pltpu.with_memory_space_constraint(vis_feats, pltpu.HBM)
        kv_weight = pltpu.with_memory_space_constraint(kv_weight, pltpu.HBM)
    flat = pl.pallas_call(
        kernel,
        in_specs=[HBM, HBM] if alone else [VMEM, VMEM],
        out_specs=[VMEM] * (2 * wanted),
        out_shape=[jax.ShapeDtypeStruct((block_rows, head_dim), jnp.float32)] * (2 * wanted),
        scratch_shapes=scratch if alone else [],
        compiler_params=params(10),
        cost_estimate=pl.CostEstimate(
            flops=2 * wanted * block_rows * width * pair,
            bytes_accessed=(wanted * pair + rows) * width * 2,
            transcendentals=0,
        ),
        name="project",
    )(vis_feats, kv_weight)
    return [flat[2 * n : 2 * n + 2] for n in range(wanted)]


def sum_over_head(vis_feats, kv_weight, pair, early):
    count = lax.axis_size("head")
    ends = project(lambda here, n: count - 1 - here, 1, vis_feats, kv_weight, pair)[0]
    offsets = []
    for hop in range(2, count):
        offsets += [o for o in dict.fromkeys((count - hop, hop)) if o not in offsets]
    offsets.append(0)

    def rest(here, n):
        chunk = here + offsets[n]
        return jnp.where(chunk >= count, chunk - count, chunk)

    parts = dict(zip(offsets, project(rest, len(offsets), vis_feats, kv_weight, pair)))
    held = lax.optimization_barrier((ends[1], parts[0][0], *early))
    ends = (ends[0], held[0])
    parts[0] = (held[1], parts[0][1])
    early = held[2:]

    to_right, to_left = [None] * 2, [None] * 2
    for hop in range(1, count):
        senders = range(min(hop, count - 1))
        right_pairs = [(i, i + 1) for i in senders]
        left_pairs = [(count - 1 - i, count - 2 - i) for i in senders]
        for piece in range(2):
            if hop == 1 and count > 3:
                arrived = lax.ppermute(ends[piece], "head", right_pairs + left_pairs)
                to_right[piece] = to_left[piece] = arrived
                continue
            if hop == 1:
                right = left = ends[piece]
            elif hop == 2 and count == 4:
                right = left = parts[2][piece] + to_right[piece]
            else:
                right = parts[count - hop][piece] + to_right[piece]
                left = parts[hop][piece] + to_left[piece]
            to_right[piece] = lax.ppermute(right, "head", right_pairs)
            to_left[piece] = lax.ppermute(left, "head", left_pairs)
    return [[parts[0][piece], to_right[piece], to_left[piece]] for piece in range(2)], early


def finish_chunk(partial_sums, key_gain, image_tokens, image_owner, per_kv, are_keys):
    rows, head_dim = partial_sums[0].shape
    half = KV_TOTAL // 2
    images = image_owner.shape[0]

    def kernel(tokens_ref, owner_ref, own_ref, left_ref, right_ref, gain_ref, mine_ref, other_ref):
        data = own_ref[...] + left_ref[...] + right_ref[...]
        if are_keys:
            mean = jnp.mean(data * data, axis=-1, keepdims=True)
            data = data * lax.rsqrt(mean + EPSILON) * gain_ref[...]
        data = data.astype(jnp.bfloat16)
        ctx = lax.axis_index("ctx")
        start, count, before = jnp.int32(0), jnp.int32(0), jnp.int32(0)
        for i in range(images):
            here = owner_ref[i] == ctx
            start = jnp.where(here, before, start)
            count = jnp.where(here, tokens_ref[i], count)
            before = before + tokens_ref[i]
        token = lax.broadcasted_iota(jnp.int32, (half, rows), 1) + (lax.axis_index("head") % per_kv) * rows
        token = jnp.where(token < count, token, -2 * KV_TOTAL)
        row = lax.broadcasted_iota(jnp.int32, (half, rows), 0)
        core = ctx % 2
        for ref, side in ((other_ref, 1 - core), (mine_ref, core)):
            match = (row + (side * half - start)) == token
            chosen = jnp.where(match, 1.0, 0.0).astype(jnp.bfloat16)
            ref[...] = jnp.dot(chosen, data, preferred_element_type=jnp.float32).astype(jnp.bfloat16)

    return pl.pallas_call(
        kernel,
        in_specs=[SMEM] * 2 + [VMEM] * 4,
        out_specs=[VMEM] * 2,
        out_shape=[jax.ShapeDtypeStruct((half, head_dim), jnp.bfloat16)] * 2,
        compiler_params=params(16),
        cost_estimate=pl.CostEstimate(
            flops=4 * half * rows * head_dim, bytes_accessed=12 * rows * head_dim, transcendentals=0
        ),
        name="finish",
    )(image_tokens, image_owner, *partial_sums, key_gain[None, :])


def mask_columns(cross_mask, image_tokens, head_dim, rows):
    images = image_tokens.shape[0]

    def kernel(tokens_ref, cross_ref, row_ref, bias_ref):
        here = pl.multiple_of(lax.axis_index("head") * rows, rows)
        cross = cross_ref[pl.ds(here, rows), :].astype(jnp.float32)
        column = lax.broadcasted_iota(jnp.int32, row_ref.shape, 1)
        closed = jnp.ones(row_ref.shape, jnp.float32)
        for i in range(images):
            closed = jnp.where(column == i, 1.0 - cross[:, i : i + 1], closed)
        row_ref[...] = closed.astype(jnp.bfloat16)
        row = lax.broadcasted_iota(jnp.int32, bias_ref.shape, 0)
        column = lax.broadcasted_iota(jnp.int32, bias_ref.shape, 1)
        before = jnp.int32(0)
        bias = jnp.zeros(bias_ref.shape, jnp.float32)
        for i in range(images + 1):
            after = before + tokens_ref[i] if i < images else jnp.int32(KV_TOTAL)
            inside = (column == i) & (row >= before) & (row < after)
            bias = jnp.where(inside, FLOOR_SCORE, bias)
            before = after
        bias_ref[...] = bias.astype(jnp.bfloat16)

    return pl.pallas_call(
        kernel,
        in_specs=[SMEM, VMEM],
        out_specs=[VMEM] * 2,
        out_shape=[
            jax.ShapeDtypeStruct((rows, head_dim), jnp.bfloat16),
            jax.ShapeDtypeStruct((KV_TOTAL, head_dim), jnp.bfloat16),
        ],
        compiler_params=params(8),
        name="masks",
    )(image_tokens, cross_mask)


def attend(call, own, arrivals, queries, row_mask, token_bias, kv_heads, images, previous, key_head=None):
    rows, width = queries.shape
    tokens, head_dim = own[0].shape
    half = tokens // 2
    block_width = width // kv_heads
    group = block_width // head_dim
    factor = head_dim ** (-0.5) * math.log2(math.e)
    stack = min(STACK, group)
    blocks = range(group // stack)
    first_hop = (call + 1) // 2
    sources = [own] if call == 0 else [pair for hop in arrivals[first_hop - 1 : call] for pair in hop]
    count = len(sources)
    line = lax.axis_size("head")

    def kernel(*refs):
        queries_ref, mask_ref, bias_ref = refs[:3]
        source_refs = refs[3 : 3 + 2 * count]
        out_ref, keys_ref, values_ref, result_ref, sem = refs[3 + 2 * count + (previous is not None) :]
        core = lax.axis_index("ctx") % 2
        head = lax.axis_index("head") if key_head is None else key_head

        def take(n, core):
            for side, at in ((0, core), (1, 1 - core)):
                span = pl.ds(pl.multiple_of(at * half, half), half)
                keys_ref[span, :head_dim] = source_refs[2 * n][side * half : (side + 1) * half, :]
                values_ref[span, :] = source_refs[2 * n + 1][side * half : (side + 1) * half, :]

        keys_ref[:, head_dim:] = bias_ref[...]
        if call == 0:
            take(0, core)
        else:
            here, step = head, 1 - 2 * core
            rank = jnp.int32(0)
            for hop in range(1, call + 1):
                for side in range(2):
                    candidate = here + (hop if side else -hop) * step
                    valid = (candidate >= 0) & (candidate < line)
                    rank = rank + jnp.where(valid, 1, 0)
                    chosen = valid & (rank == call)
                    head = jnp.where(chosen, candidate, head)
                    if hop >= first_hop:
                        n = 2 * (hop - first_hop) + side
                        source_core = 1 - core if side else core
                        pl.when(chosen)(lambda n=n, at=source_core: take(n, at))
        column = pl.multiple_of(head * block_width, block_width)
        some = jnp.min(mask_ref[:, :images].astype(jnp.float32), axis=1, keepdims=True) < 0.5

        def scores_of(n):
            left = []
            for j in range(n * stack, (n + 1) * stack):
                query = queries_ref[:, pl.ds(column + j * head_dim, head_dim)]
                left.append(jnp.concatenate([query, mask_ref[...]], axis=1))
            return lax.dot_general(
                jnp.concatenate(left, axis=0),
                keys_ref[...],
                (((1,), (1,)), ((), ())),
                preferred_element_type=jnp.float32,
            )

        scores = scores_of(0)
        for n in blocks:
            following = scores_of(n + 1) if n + 1 < len(blocks) else None
            largest = jnp.max(scores, axis=1, keepdims=True)
            weights = jnp.exp2((scores - largest) * factor)
            summed = jnp.sum(weights, axis=1, keepdims=True)
            mixed = jnp.dot(
                weights.astype(jnp.bfloat16), values_ref[...], preferred_element_type=jnp.float32
            )
            mixed = mixed / jnp.maximum(summed, 1.0)
            for j in range(stack):
                one = jnp.where(some, mixed[j * rows : (j + 1) * rows], 0.0)
                at = (n * stack + j) * head_dim
                result_ref[:, at : at + head_dim] = one.astype(jnp.bfloat16)
            scores = following
        store = pltpu.make_async_copy(result_ref, out_ref.at[:, pl.ds(column, block_width)], sem)
        store.start()
        store.wait()

    operands = [queries, row_mask, token_bias]
    for source in sources:
        operands += source
    in_specs = [VMEM] * len(operands)
    aliases = {}
    if previous is not None:
        aliases = {len(operands): 0}
        operands.append(previous)
        in_specs.append(ANYWHERE)
    return pl.pallas_call(
        kernel,
        in_specs=in_specs,
        out_specs=ANYWHERE,
        out_shape=jax.ShapeDtypeStruct((rows, width), jnp.bfloat16),
        scratch_shapes=[
            pltpu.VMEM((tokens, 2 * head_dim), jnp.bfloat16),
            pltpu.VMEM((tokens, head_dim), jnp.bfloat16),
            pltpu.VMEM((rows, block_width), jnp.bfloat16),
            pltpu.SemaphoreType.DMA,
        ],
        input_output_aliases=aliases,
        compiler_params=params(16),
        cost_estimate=pl.CostEstimate(
            flops=6 * rows * group * tokens * head_dim,
            bytes_accessed=rows * block_width * 4,
            transcendentals=rows * group * tokens,
        ),
        name="attend",
    )(*operands)


def shards(queries, vis_feats, kv_weight, key_gain, cross_mask, image_tokens, image_owner):
    head_count = lax.axis_size("head")
    ctx_count = lax.axis_size("ctx")
    ctx_bits = ctx_count.bit_length() - 1
    head_dim = key_gain.shape[0]
    kv_heads = kv_weight.shape[1] // (2 * head_dim)
    per_kv = head_count // kv_heads
    images = image_tokens.shape[0]

    masks = mask_columns(cross_mask, image_tokens, head_dim, queries.shape[0])
    partial_sums, (row_mask, token_bias) = sum_over_head(vis_feats, kv_weight, 2 * head_dim, masks)

    def spread(piece):
        block, other = finish_chunk(
            partial_sums[piece], key_gain, image_tokens, image_owner, per_kv, piece == 0
        )
        if per_kv > 1:
            groups = [[k * per_kv + j for j in range(per_kv)] for k in range(kv_heads)]
            block, other = lax.psum((block, other), "head", axis_index_groups=groups)
        block = block + swapped(other, "ctx", 0)
        for step in range(1, ctx_bits):
            pairs = [
                (c, c ^ (2**step if c % 2 == 0 else 2 ** (ctx_bits - step))) for c in range(ctx_count)
            ]
            block = block + lax.ppermute(block, "ctx", pairs)
        other = swapped(block, "ctx", 0)
        return jnp.concatenate([block, other], 0)

    keys, values = spread(0), spread(1)

    if per_kv > 1:
        groups = [[k * per_kv + j for k in range(kv_heads)] for j in range(per_kv)]
        keys = lax.all_gather(keys, "head", axis_index_groups=groups)
        values = lax.all_gather(values, "head", axis_index_groups=groups)
        out = None
        for k in range(kv_heads):
            own = (keys[k], values[k])
            out = attend(0, own, [], queries, row_mask, token_bias, kv_heads, images, out, k)
        return out

    def place(c, h):
        return c * head_count + h

    own = (keys, values)
    arrivals = []
    out = attend(0, own, arrivals, queries, row_mask, token_bias, kv_heads, images, None)
    passing = [keys, values]
    for hop in range(1, head_count):
        pairs = []
        for c in range(ctx_count):
            for i in range(hop - 1, head_count - 1):
                if c % 2 == 0:
                    pairs.append((place(c, i), place(c, i + 1)))
                else:
                    pairs.append((place(c, head_count - 1 - i), place(c, head_count - 2 - i)))
        crossing = [None, None]
        for piece in range(2):
            passing[piece] = lax.ppermute(passing[piece], ("ctx", "head"), pairs)
            crossing[piece] = swapped(passing[piece], "ctx", 0)
        arrivals.append([tuple(passing), tuple(crossing)])
        out = attend(hop, own, arrivals, queries, row_mask, token_bias, kv_heads, images, out)
    return out


def solution(mesh):
    return jax.shard_map(
        shards,
        mesh=mesh,
        in_specs=(
            P(("ctx", "head"), None),
            P("ctx", "head"),
            P("head", None),
            P(),
            P("ctx", None),
            P(),
            P(),
        ),
        out_specs=P(("ctx", "head"), None),
        check_vma=False,
    )
```

time: 120 us -> 107 us (0.89)
  Pallas kernels: 26.7 us -> 20.5 us
  other arithmetic: 4.8 us -> 0.52 us
  local copies, waits for them, and re-layouts: 7.3 us -> 3.95 us
  waiting for transfers between devices: 17.9 us -> 19.7 us
    pallas_call x4, Pallas kernels: 17.9 us -> 11.8 us  [attend(): pl.pallas_call(kernel, in_specs=in_specs, out_specs=ANYWHERE, out_shape=j...]
    unnamed x23 -> x15, local copies, waits for them, and re-layouts: 7.28 us -> 3.95 us
    ppermute x6, starting transfers between devices: 12.4 us -> 10 us  [shards(): passing[piece] = lax.ppermute(passing[piece], ('ctx', 'head'), pairs)]
    ppermute x4, waiting for transfers between devices: 1.9 us -> 3.66 us  [sum_over_head(): to_left[piece] = lax.ppermute(left, 'head', left_pairs)]
    add x2, other arithmetic: 1.74 us -> 0.06 us  [sum_over_head(): left = parts[hop][piece] + to_left[piece]]
    ppermute x10, starting transfers between devices: 12.7 us -> 14 us  [swapped(): return lax.ppermute(value, axis, pairs)]
  transfers between devices with their start and end apart: 30 -> 30, of which waited for: 10 -> 10; matrix products, arithmetic and copies ran while one was open for 3% -> 0% of each run, Pallas kernels for 13% -> 11%
where the time goes in v4:
time: 107 us; the launch traced here: 105 us
  starting transfers between devices  59.9 us (56%)
  Pallas kernels  20.5 us (19%)
  waiting for transfers between devices  19.7 us (18%)
  local copies, waits for them, and re-layouts  3.95 us (4%)
    ppermute x4, starting transfers between devices, sum_over_head(): to_right[piece] = lax.ppermute(right, 'head', right_pairs)  19.6 us
    ppermute x10, starting transfers between devices, swapped(): return lax.ppermute(value, axis, pairs)  14 us
    pallas_call x4, Pallas kernels, attend(): pl.pallas_call(kernel, in_specs=in_specs, out_specs=ANYWHERE, out_shape=j...  11.8 us
    ppermute x6, starting transfers between devices, shards(): passing[piece] = lax.ppermute(passing[piece], ('ctx', 'head'), pairs)  10 us
    ppermute x2, starting transfers between devices, sum_over_head(): arrived = lax.ppermute(ends[piece], 'head', right_pairs + left_pairs)  6.28 us
    ppermute x4, waiting for transfers between devices, spread(): block = block + lax.ppermute(block, 'ctx', pairs)  6.24 us
    ppermute x4, starting transfers between devices, spread(): block = block + lax.ppermute(block, 'ctx', pairs)  6.05 us
    ppermute x2, waiting for transfers between devices, sum_over_head(): arrived = lax.ppermute(ends[piece], 'head', right_pairs + left_pairs)  5.83 us
  transfers between devices with their start and end apart: 30, of which 10 were waited for; matrix products, arithmetic and copies ran while one was open for 0% of the time, Pallas kernels for 11%

profile of v4, /device:TPU:0, one launch (start us, length us, event | category | flops | bytes accessed | tf_op | source)
XLA Modules:
  0.0 105.2 jit_solution(5060306724884364197)
XLA Ops:
  0.0 2.2 %copy-done.1 = bf16[2048,1024]{1,0:T(8,128)(2,1)S(1)} copy-done((bf16[2048,1024]{1,0:T(8,128)(2,1)S(1)}, bf16[2048,1024]{1,0:T(8,128)(2,1)}, u32[]{:S(2)}) %copy-start.1) | copy-done | bytes 4194328
  2.2 1.6 %copy-done.2 = bf16[512,2048]{1,0:T(8,128)(2,1)S(1)} copy-done((bf16[512,2048]{1,0:T(8,128)(2,1)S(1)}, bf16[512,2048]{1,0:T(8,128)(2,1)}, u32[]{:S(2)}) %copy-start.2) | copy-done | bytes 2097176
  3.8 2.4 %project.3 = (f32[512,128]{1,0:T(8,128)S(1)}, f32[512,128]{1,0:T(8,128)S(1)}, f32[512,128]{1,0:T(8,128)S(1)}, f32[512,128]{1,0:T(8,128)S(1)}, f32[512,128]{1,0:T...) custom-call(bf16[512,2048]{1,0:T(8,128)(2,1)S(1)} %copy-done.2, ...), custom_call_target="tpu_custom_call" | custom-call | flops 2147483648 | bytes 6291456 | tf_op jit(solution)/shard_map/project/pallas_call | solution.py:80
  6.2 2.6 %project.2 = (f32[512,128]{1,0:T(8,128)S(1)}, f32[512,128]{1,0:T(8,128)S(1)}) custom-call(bf16[512,2048]{1,0:T(8,128)(2,1)} %feats_ref.3, bf16[2048,1024]{1,0:T(8,128)(2,1)} %weight_ref.3), custom_call_target="tpu_custom_call" | custom-call | flops 536870912 | bytes 3145728 | tf_op jit(solution)/shard_map/project/pallas_call | solution.py:80
  9.0 1.6 %masks.1 = (bf16[128,128]{1,0:T(8,128)(2,1)S(1)}, bf16[1280,128]{1,0:T(8,128)(2,1)S(1)}) custom-call(s32[4]{0:T(128)S(1)} %copy-done.3, s32[512,4]{1,0:T(8,128)S(1)} %copy.11.cross_ref), custom_call_target="tpu_custom_call" | custom-call | tf_op jit(solution)/shard_map/masks/pallas_call | solution.py:199
  10.6 5.0 %collective-permute-start.11 = (f32[512,128]{1,0:T(8,128)S(1)}, f32[512,128]{1,0:T(8,128)S(1)}, u32[]{:S(2)}, u32[]{:S(2)}) collective-permute-start(f32[512,128]{1,0:T(8,128)S(1)} %get-tuple-element.41), channel_id=1, source_target_pairs={{0,1},{3,2},{4,5},{7,6},{8,9},{11,10},{12,13},{15,14},{16,17},{19,... | collective-permute-start | bytes 786440 | tf_op jit(solution)/shard_map/ppermute | solution.py:122
  15.5 1.3 %collective-permute-start = (f32[512,128]{1,0:T(8,128)S(1)}, f32[512,128]{1,0:T(8,128)S(1)}, u32[]{:S(2)}, u32[]{:S(2)}) collective-permute-start(f32[512,128]{1,0:T(8,128)S(1)} %get-tuple-element.34), channel_id=1, source_target_pairs={{0,1},{3,2},{4,5},{7,6},{8,9},{11,10},{12,13},{15,14},{16,17},{19,... | collective-permute-start | bytes 786440 | tf_op jit(solution)/shard_map/ppermute | solution.py:122
  16.9 5.3 %collective-permute-done.11 = f32[512,128]{1,0:T(8,128)S(1)} collective-permute-done((f32[512,128]{1,0:T(8,128)S(1)}, f32[512,128]{1,0:T(8,128)S(1)}, u32[]{:S(2)}, u32[]{:S(2)}) %collective-permute-start.11) | collective-permute-done | bytes 262176 | tf_op jit(solution)/shard_map/ppermute | solution.py:122
  22.2 4.4 %collective-permute-start.12 = (f32[512,128]{1,0:T(8,128)S(1)}, f32[512,128]{1,0:T(8,128)S(1)}, u32[]{:S(2)}, u32[]{:S(2)}) collective-permute-start(f32[512,128]{1,0:T(8,128)S(1)} %add.42), channel_id=1, source_target_pairs={{0,1},{1,2},{4,5},{5,6},{8,9},{9,10},{12,13},{13,14},{16,17},{17,1... | collective-permute-start | bytes 786440 | tf_op jit(solution)/shard_map/ppermute | solution.py:132
  28.5 5.0 %collective-permute-start.1 = (f32[512,128]{1,0:T(8,128)S(1)}, f32[512,128]{1,0:T(8,128)S(1)}, u32[]{:S(2)}, u32[]{:S(2)}) collective-permute-start(f32[512,128]{1,0:T(8,128)S(1)} %add.36), channel_id=1, source_target_pairs={{0,1},{1,2},{4,5},{5,6},{8,9},{9,10},{12,13},{13,14},{16,17},{17,1... | collective-permute-start | bytes 786440 | tf_op jit(solution)/shard_map/ppermute | solution.py:132
  33.6 4.7 %collective-permute-start.13 = (f32[512,128]{1,0:T(8,128)S(1)}, f32[512,128]{1,0:T(8,128)S(1)}, u32[]{:S(2)}, u32[]{:S(2)}) collective-permute-start(f32[512,128]{1,0:T(8,128)S(1)} %add.43), channel_id=1, source_target_pairs={{0,1},{1,2},{2,3},{4,5},{5,6},{6,7},{8,9},{9,10},{10,11},{12,13},{... | collective-permute-start | bytes 786440 | tf_op jit(solution)/shard_map/ppermute | solution.py:132
  38.4 1.3 %collective-permute-start.15 = (f32[512,128]{1,0:T(8,128)S(1)}, f32[512,128]{1,0:T(8,128)S(1)}, u32[]{:S(2)}, u32[]{:S(2)}) collective-permute-start(f32[512,128]{1,0:T(8,128)S(1)} %add.44), channel_id=1, source_target_pairs={{3,2},{2,1},{1,0},{7,6},{6,5},{5,4},{11,10},{10,9},{9,8},{15,14},{... | collective-permute-start | bytes 786440 | tf_op jit(solution)/shard_map/ppermute | solution.py:133
  41.1 5.5 %collective-permute-start.2 = (f32[512,128]{1,0:T(8,128)S(1)}, f32[512,128]{1,0:T(8,128)S(1)}, u32[]{:S(2)}, u32[]{:S(2)}) collective-permute-start(f32[512,128]{1,0:T(8,128)S(1)} %add.37), channel_id=1, source_target_pairs={{0,1},{1,2},{2,3},{4,5},{5,6},{6,7},{8,9},{9,10},{10,11},{12,13},{... | collective-permute-start | bytes 786440 | tf_op jit(solution)/shard_map/ppermute | solution.py:132
  46.5 2.0 %collective-permute-done.15.right_ref = f32[512,128]{1,0:T(8,128)S(1)} collective-permute-done((f32[512,128]{1,0:T(8,128)S(1)}, f32[512,128]{1,0:T(8,128)S(1)}, u32[]{:S(2)}, u32[]{:S(2)}) %collective-permute-start.15) | collective-permute-done | bytes 262176 | tf_op jit(solution)/shard_map/ppermute | solution.py:133
  49.7 1.6 %collective-permute-done.4.right_ref = f32[512,128]{1,0:T(8,128)S(1)} collective-permute-done((f32[512,128]{1,0:T(8,128)S(1)}, f32[512,128]{1,0:T(8,128)S(1)}, u32[]{:S(2)}, u32[]{:S(2)}) %collective-permute-start.4) | collective-permute-done | bytes 262176 | tf_op jit(solution)/shard_map/ppermute | solution.py:133
  52.7 1.6 %collective-permute-start.17 = (bf16[640,128]{1,0:T(8,128)(2,1)S(1)}, bf16[640,128]{1,0:T(8,128)(2,1)S(1)}, u32[]{:S(2)}, u32[]{:S(2)}) collective-permute-start(bf16[640,128]{1,0:T(8,128)(2,1)S(1)} %add.45), channel_id=1, source_target_pairs={{0,8},{4,20},{8,0},{12,28},{16,24},{20,4},{24,16},{28,12},{1,9},{5... | collective-permute-start | bytes 491528 | tf_op jit(solution)/shard_map/ppermute | solution.py:345
  54.3 1.3 %collective-permute-start.6 = (bf16[640,128]{1,0:T(8,128)(2,1)S(1)}, bf16[640,128]{1,0:T(8,128)(2,1)S(1)}, u32[]{:S(2)}, u32[]{:S(2)}) collective-permute-start(bf16[640,128]{1,0:T(8,128)(2,1)S(1)} %add.39), channel_id=1, source_target_pairs={{0,8},{4,20},{8,0},{12,28},{16,24},{20,4},{24,16},{28,12},{1,9},{5... | collective-permute-start | bytes 491528 | tf_op jit(solution)/shard_map/ppermute | solution.py:345
  55.6 2.5 %collective-permute-done.17 = bf16[640,128]{1,0:T(8,128)(2,1)S(1)} collective-permute-done((bf16[640,128]{1,0:T(8,128)(2,1)S(1)}, bf16[640,128]{1,0:T(8,128)(2,1)S(1)}, u32[]{:S(2)}, u32[]{:S(2)}) %collective-permute-start.17) | collective-permute-done | bytes 163872 | tf_op jit(solution)/shard_map/ppermute | solution.py:345
  58.1 1.6 %collective-permute-start.18 = (bf16[640,128]{1,0:T(8,128)(2,1)S(1)}, bf16[640,128]{1,0:T(8,128)(2,1)S(1)}, u32[]{:S(2)}, u32[]{:S(2)}) collective-permute-start(bf16[640,128]{1,0:T(8,128)(2,1)S(1)} %add.46), channel_id=1, source_target_pairs={{0,16},{4,12},{8,24},{12,4},{16,0},{20,28},{24,8},{28,20},{1,17},{... | collective-permute-start | bytes 491528 | tf_op jit(solution)/shard_map/ppermute | solution.py:345
  59.8 1.6 %collective-permute-start.7 = (bf16[640,128]{1,0:T(8,128)(2,1)S(1)}, bf16[640,128]{1,0:T(8,128)(2,1)S(1)}, u32[]{:S(2)}, u32[]{:S(2)}) collective-permute-start(bf16[640,128]{1,0:T(8,128)(2,1)S(1)} %add.40), channel_id=1, source_target_pairs={{0,16},{4,12},{8,24},{12,4},{16,0},{20,28},{24,8},{28,20},{1,17},{... | collective-permute-start | bytes 491528 | tf_op jit(solution)/shard_map/ppermute | solution.py:345
  61.4 2.0 %collective-permute-done.18 = bf16[640,128]{1,0:T(8,128)(2,1)S(1)} collective-permute-done((bf16[640,128]{1,0:T(8,128)(2,1)S(1)}, bf16[640,128]{1,0:T(8,128)(2,1)S(1)}, u32[]{:S(2)}, u32[]{:S(2)}) %collective-permute-start.18) | collective-permute-done | bytes 163872 | tf_op jit(solution)/shard_map/ppermute | solution.py:345
  63.6 1.6 %collective-permute-done.7 = bf16[640,128]{1,0:T(8,128)(2,1)S(1)} collective-permute-done((bf16[640,128]{1,0:T(8,128)(2,1)S(1)}, bf16[640,128]{1,0:T(8,128)(2,1)S(1)}, u32[]{:S(2)}, u32[]{:S(2)}) %collective-permute-start.7) | collective-permute-done | bytes 163872 | tf_op jit(solution)/shard_map/ppermute | solution.py:345
  65.4 3.4 %collective-permute-start.20 = (bf16[1280,128]{1,0:T(8,128)(2,1)S(1)}, bf16[1280,128]{1,0:T(8,128)(2,1)S(1)}, u32[]{:S(2)}, u32[]{:S(2)}) collective-permute-start(bf16[1280,128]{1,0:T(8,128)(2,1)S(1)} %pad_maximum_fusion.1.refs_4_), channel_id=1, source_target_pairs={{0,1},{1,2},{2,3},{7,6},{6,5},{5,4},{8,9},{9,10},{10,11},{15,14},{... | collective-permute-start | bytes 983048 | tf_op jit(solution)/shard_map/ppermute | solution.py:378
  68.9 3.9 %collective-permute-start.9 = (bf16[1280,128]{1,0:T(8,128)(2,1)S(1)}, bf16[1280,128]{1,0:T(8,128)(2,1)S(1)}, u32[]{:S(2)}, u32[]{:S(2)}) collective-permute-start(bf16[1280,128]{1,0:T(8,128)(2,1)S(1)} %pad_maximum_fusion.refs_3_), channel_id=1, source_target_pairs={{0,1},{1,2},{2,3},{7,6},{6,5},{5,4},{8,9},{9,10},{10,11},{15,14},{... | collective-permute-start | bytes 983048 | tf_op jit(solution)/shard_map/ppermute | solution.py:378
  74.1 3.3 %collective-permute-done.9.refs_3_ = bf16[1280,128]{1,0:T(8,128)(2,1)S(1)} collective-permute-done((bf16[1280,128]{1,0:T(8,128)(2,1)S(1)}, bf16[1280,128]{1,0:T(8,128)(2,1)S(1)}, u32[]{:S(2)}, u32[]{:S(2)}) %collective-permute-start.9) | collective-permute-done | bytes 327712 | tf_op jit(solution)/shard_map/ppermute | solution.py:378
  80.0 6.8 %collective-permute-start.28 = (bf16[1280,128]{1,0:T(8,128)(2,1)S(1)}, bf16[1280,128]{1,0:T(8,128)(2,1)S(1)}, u32[]{:S(2)}, u32[]{:S(2)}) collective-permute-start(bf16[1280,128]{1,0:T(8,128)(2,1)S(1)} %collective-permute-done.9.refs_3_), channel_id=1, source_target_pairs={{0,4},{4,0},{8,12},{12,8},{16,20},{20,16},{24,28},{28,24},{1,5},{5... | collective-permute-start | bytes 983048 | tf_op jit(solution)/shard_map/ppermute | solution.py:29
  87.2 2.4 %collective-permute-start.27 = (bf16[1280,128]{1,0:T(8,128)(2,1)S(1)}, bf16[1280,128]{1,0:T(8,128)(2,1)S(1)}, u32[]{:S(2)}, u32[]{:S(2)}) collective-permute-start(bf16[1280,128]{1,0:T(8,128)(2,1)S(1)} %collective-permute-done.25.refs_8_), channel_id=1, source_target_pairs={{0,4},{4,0},{8,12},{12,8},{16,20},{20,16},{24,28},{28,24},{1,5},{5... | collective-permute-start | bytes 983048 | tf_op jit(solution)/shard_map/ppermute | solution.py:29
  89.7 3.5 %collective-permute-start.26 = (bf16[1280,128]{1,0:T(8,128)(2,1)S(1)}, bf16[1280,128]{1,0:T(8,128)(2,1)S(1)}, u32[]{:S(2)}, u32[]{:S(2)}) collective-permute-start(bf16[1280,128]{1,0:T(8,128)(2,1)S(1)} %collective-permute-done.24.refs_7_), channel_id=1, source_target_pairs={{0,4},{4,0},{8,12},{12,8},{16,20},{20,16},{24,28},{28,24},{1,5},{5... | collective-permute-start | bytes 983048 | tf_op jit(solution)/shard_map/ppermute | solution.py:29
  93.2 2.8 %attend.4.refs_7_ = bf16[128,4096]{1,0:T(8,128)(2,1)} custom-call(bf16[128,4096]{1,0:T(8,128)(2,1)S(1)} %copy-done, bf16[128,128]{1,0:T(8,128)(2,1)S(1)} %get-tuple-element.29.refs_1_, bf16[1280,128]{1,0:T(8,128)(2,1)S(1)} %get-tuple-element.30.refs_2_, bf16[1280,128]{1,0:T(8,128)(2,1)S(1)} %pad_maximum_fusion.refs_3_, ...), custom_call_target="tpu_custom_call" | custom-call | flops 1006632960 | bytes 524288 | tf_op jit(solution)/shard_map/attend/pallas_call | solution.py:299
  96.0 2.9 %attend.5.refs_11_ = bf16[128,4096]{1,0:T(8,128)(2,1)} custom-call(bf16[128,4096]{1,0:T(8,128)(2,1)S(1)} %copy-done, bf16[128,128]{1,0:T(8,128)(2,1)S(1)} %get-tuple-element.29.refs_1_, bf16[1280,128]{1,0:T(8,128)(2,1)S(1)} %get-tuple-element.30.refs_2_, bf16[1280,128]{1,0:T(8,128)(2,1)S(1)} %collective-permute-done.9.refs_3_, ...), custom_call_target="tpu_custom_call", output_to_operand_aliasing={{}: (7, {})} | custom-call | flops 1006632960 | bytes 524288 | tf_op jit(solution)/shard_map/attend/pallas_call | solution.py:299
  99.0 3.1 %attend.6.refs_11_ = bf16[128,4096]{1,0:T(8,128)(2,1)} custom-call(bf16[128,4096]{1,0:T(8,128)(2,1)S(1)} %copy-done, bf16[128,128]{1,0:T(8,128)(2,1)S(1)} %get-tuple-element.29.refs_1_, bf16[1280,128]{1,0:T(8,128)(2,1)S(1)} %get-tuple-element.30.refs_2_, bf16[1280,128]{1,0:T(8,128)(2,1)S(1)} %collective-permute-done.9.refs_3_, ...), custom_call_target="tpu_custom_call", output_to_operand_aliasing={{}: (11, {})} | custom-call | flops 1006632960 | bytes 524288 | tf_op jit(solution)/shard_map/attend/pallas_call | solution.py:299
  102.1 2.9 %attend.7 = bf16[128,4096]{1,0:T(8,128)(2,1)} custom-call(bf16[128,4096]{1,0:T(8,128)(2,1)S(1)} %copy-done, bf16[128,128]{1,0:T(8,128)(2,1)S(1)} %get-tuple-element.29.refs_1_, bf16[1280,128]{1,0:T(8,128)(2,1)S(1)} %get-tuple-element.30.refs_2_, bf16[1280,128]{1,0:T(8,128)(2,1)S(1)} %collective-permute-done.10.refs_7_.refs_3_, ...), custom_call_target="tpu_custom_call", output_to_operand_aliasing={{}: (11, {})} | custom-call | flops 1006632960 | bytes 524288 | tf_op jit(solution)/shard_map/attend/pallas_call | solution.py:299
  (66 shorter events, 10.8 us)
Async XLA Ops:
  8.8 39.7 %copy-start.4 = (s32[4]{0:T(128)S(1)}, s32[4]{0:T(128)}, u32[]{:S(2)}) copy-start(s32[4]{0:T(128)} %owner_ref.3) | copy-start | bytes 52
  10.6 11.6 %collective-permute-start.11 = (f32[512,128]{1,0:T(8,128)S(1)}, f32[512,128]{1,0:T(8,128)S(1)}, u32[]{:S(2)}, u32[]{:S(2)}) collective-permute-start(f32[512,128]{1,0:T(8,128)S(1)} %get-tuple-element.41), channel_id=1, source_target_pairs={{0,1},{3,2},{4,5},{7,6},{8,9},{11,10},{12,13},{15,14},{16,17},{19,... | collective-permute-start | bytes 786440 | tf_op jit(solution)/shard_map/ppermute | solution.py:122
  15.5 12.3 %collective-permute-start = (f32[512,128]{1,0:T(8,128)S(1)}, f32[512,128]{1,0:T(8,128)S(1)}, u32[]{:S(2)}, u32[]{:S(2)}) collective-permute-start(f32[512,128]{1,0:T(8,128)S(1)} %get-tuple-element.34), channel_id=1, source_target_pairs={{0,1},{3,2},{4,5},{7,6},{8,9},{11,10},{12,13},{15,14},{16,17},{19,... | collective-permute-start | bytes 786440 | tf_op jit(solution)/shard_map/ppermute | solution.py:122
  22.2 11.3 %collective-permute-start.12 = (f32[512,128]{1,0:T(8,128)S(1)}, f32[512,128]{1,0:T(8,128)S(1)}, u32[]{:S(2)}, u32[]{:S(2)}) collective-permute-start(f32[512,128]{1,0:T(8,128)S(1)} %add.42), channel_id=1, source_target_pairs={{0,1},{1,2},{4,5},{5,6},{8,9},{9,10},{12,13},{13,14},{16,17},{17,1... | collective-permute-start | bytes 786440 | tf_op jit(solution)/shard_map/ppermute | solution.py:132
  26.6 11.7 %collective-permute-start.14 = (f32[512,128]{1,0:T(8,128)S(1)}, f32[512,128]{1,0:T(8,128)S(1)}, u32[]{:S(2)}, u32[]{:S(2)}) collective-permute-start(f32[512,128]{1,0:T(8,128)S(1)} %add.42), channel_id=1, source_target_pairs={{3,2},{2,1},{7,6},{6,5},{11,10},{10,9},{15,14},{14,13},{19,18},{18... | collective-permute-start | bytes 786440 | tf_op jit(solution)/shard_map/ppermute | solution.py:133
  27.9 11.8 %collective-permute-start.3 = (f32[512,128]{1,0:T(8,128)S(1)}, f32[512,128]{1,0:T(8,128)S(1)}, u32[]{:S(2)}, u32[]{:S(2)}) collective-permute-start(f32[512,128]{1,0:T(8,128)S(1)} %add.36), channel_id=1, source_target_pairs={{3,2},{2,1},{7,6},{6,5},{11,10},{10,9},{15,14},{14,13},{19,18},{18... | collective-permute-start | bytes 786440 | tf_op jit(solution)/shard_map/ppermute | solution.py:133
  28.5 12.5 %collective-permute-start.1 = (f32[512,128]{1,0:T(8,128)S(1)}, f32[512,128]{1,0:T(8,128)S(1)}, u32[]{:S(2)}, u32[]{:S(2)}) collective-permute-start(f32[512,128]{1,0:T(8,128)S(1)} %add.36), channel_id=1, source_target_pairs={{0,1},{1,2},{4,5},{5,6},{8,9},{9,10},{12,13},{13,14},{16,17},{17,1... | collective-permute-start | bytes 786440 | tf_op jit(solution)/shard_map/ppermute | solution.py:132
  33.6 59.6 %copy-start = (bf16[128,4096]{1,0:T(8,128)(2,1)S(1)}, bf16[128,4096]{1,0:T(8,128)(2,1)}, u32[]{:S(2)}) copy-start(bf16[128,4096]{1,0:T(8,128)(2,1)} %refs_0_.7) | copy-start | bytes 3145732
  33.6 12.9 %collective-permute-start.13 = (f32[512,128]{1,0:T(8,128)S(1)}, f32[512,128]{1,0:T(8,128)S(1)}, u32[]{:S(2)}, u32[]{:S(2)}) collective-permute-start(f32[512,128]{1,0:T(8,128)S(1)} %add.43), channel_id=1, source_target_pairs={{0,1},{1,2},{2,3},{4,5},{5,6},{6,7},{8,9},{9,10},{10,11},{12,13},{... | collective-permute-start | bytes 786440 | tf_op jit(solution)/shard_map/ppermute | solution.py:132
  38.4 10.2 %collective-permute-start.15 = (f32[512,128]{1,0:T(8,128)S(1)}, f32[512,128]{1,0:T(8,128)S(1)}, u32[]{:S(2)}, u32[]{:S(2)}) collective-permute-start(f32[512,128]{1,0:T(8,128)S(1)} %add.44), channel_id=1, source_target_pairs={{3,2},{2,1},{1,0},{7,6},{6,5},{5,4},{11,10},{10,9},{9,8},{15,14},{... | collective-permute-start | bytes 786440 | tf_op jit(solution)/shard_map/ppermute | solution.py:133
  39.7 11.6 %collective-permute-start.4 = (f32[512,128]{1,0:T(8,128)S(1)}, f32[512,128]{1,0:T(8,128)S(1)}, u32[]{:S(2)}, u32[]{:S(2)}) collective-permute-start(f32[512,128]{1,0:T(8,128)S(1)} %add.38), channel_id=1, source_target_pairs={{3,2},{2,1},{1,0},{7,6},{6,5},{5,4},{11,10},{10,9},{9,8},{15,14},{... | collective-permute-start | bytes 786440 | tf_op jit(solution)/shard_map/ppermute | solution.py:133
  41.1 10.3 %collective-permute-start.2 = (f32[512,128]{1,0:T(8,128)S(1)}, f32[512,128]{1,0:T(8,128)S(1)}, u32[]{:S(2)}, u32[]{:S(2)}) collective-permute-start(f32[512,128]{1,0:T(8,128)S(1)} %add.37), channel_id=1, source_target_pairs={{0,1},{1,2},{2,3},{4,5},{5,6},{6,7},{8,9},{9,10},{10,11},{12,13},{... | collective-permute-start | bytes 786440 | tf_op jit(solution)/shard_map/ppermute | solution.py:132
  49.6 3.0 %collective-permute-start.16 = (bf16[640,128]{1,0:T(8,128)(2,1)S(1)}, bf16[640,128]{1,0:T(8,128)(2,1)S(1)}, u32[]{:S(2)}, u32[]{:S(2)}) collective-permute-start(bf16[640,128]{1,0:T(8,128)(2,1)S(1)} %get-tuple-element.44), channel_id=1, source_target_pairs={{0,4},{4,0},{8,12},{12,8},{16,20},{20,16},{24,28},{28,24},{1,5},{5... | collective-permute-start | bytes 491528 | tf_op jit(solution)/shard_map/ppermute | solution.py:29
  52.5 1.7 %collective-permute-start.5 = (bf16[640,128]{1,0:T(8,128)(2,1)S(1)}, bf16[640,128]{1,0:T(8,128)(2,1)S(1)}, u32[]{:S(2)}, u32[]{:S(2)}) collective-permute-start(bf16[640,128]{1,0:T(8,128)(2,1)S(1)} %get-tuple-element.37), channel_id=1, source_target_pairs={{0,4},{4,0},{8,12},{12,8},{16,20},{20,16},{24,28},{28,24},{1,5},{5... | collective-permute-start | bytes 491528 | tf_op jit(solution)/shard_map/ppermute | solution.py:29
  52.7 5.4 %collective-permute-start.17 = (bf16[640,128]{1,0:T(8,128)(2,1)S(1)}, bf16[640,128]{1,0:T(8,128)(2,1)S(1)}, u32[]{:S(2)}, u32[]{:S(2)}) collective-permute-start(bf16[640,128]{1,0:T(8,128)(2,1)S(1)} %add.45), channel_id=1, source_target_pairs={{0,8},{4,20},{8,0},{12,28},{16,24},{20,4},{24,16},{28,12},{1,9},{5... | collective-permute-start | bytes 491528 | tf_op jit(solution)/shard_map/ppermute | solution.py:345
  54.3 5.5 %collective-permute-start.6 = (bf16[640,128]{1,0:T(8,128)(2,1)S(1)}, bf16[640,128]{1,0:T(8,128)(2,1)S(1)}, u32[]{:S(2)}, u32[]{:S(2)}) collective-permute-start(bf16[640,128]{1,0:T(8,128)(2,1)S(1)} %add.39), channel_id=1, source_target_pairs={{0,8},{4,20},{8,0},{12,28},{16,24},{20,4},{24,16},{28,12},{1,9},{5... | collective-permute-start | bytes 491528 | tf_op jit(solution)/shard_map/ppermute | solution.py:345
  58.1 5.4 %collective-permute-start.18 = (bf16[640,128]{1,0:T(8,128)(2,1)S(1)}, bf16[640,128]{1,0:T(8,128)(2,1)S(1)}, u32[]{:S(2)}, u32[]{:S(2)}) collective-permute-start(bf16[640,128]{1,0:T(8,128)(2,1)S(1)} %add.46), channel_id=1, source_target_pairs={{0,16},{4,12},{8,24},{12,4},{16,0},{20,28},{24,8},{28,20},{1,17},{... | collective-permute-start | bytes 491528 | tf_op jit(solution)/shard_map/ppermute | solution.py:345
  59.8 5.4 %collective-permute-start.7 = (bf16[640,128]{1,0:T(8,128)(2,1)S(1)}, bf16[640,128]{1,0:T(8,128)(2,1)S(1)}, u32[]{:S(2)}, u32[]{:S(2)}) collective-permute-start(bf16[640,128]{1,0:T(8,128)(2,1)S(1)} %add.40), channel_id=1, source_target_pairs={{0,16},{4,12},{8,24},{12,4},{16,0},{20,28},{24,8},{28,20},{1,17},{... | collective-permute-start | bytes 491528 | tf_op jit(solution)/shard_map/ppermute | solution.py:345
  63.5 1.8 %collective-permute-start.19 = (bf16[640,128]{1,0:T(8,128)(2,1)S(1)}, bf16[640,128]{1,0:T(8,128)(2,1)S(1)}, u32[]{:S(2)}, u32[]{:S(2)}) collective-permute-start(bf16[640,128]{1,0:T(8,128)(2,1)S(1)} %add.47), channel_id=1, source_target_pairs={{0,4},{4,0},{8,12},{12,8},{16,20},{20,16},{24,28},{28,24},{1,5},{5... | collective-permute-start | bytes 491528 | tf_op jit(solution)/shard_map/ppermute | solution.py:29
  65.3 3.6 %collective-permute-start.8 = (bf16[640,128]{1,0:T(8,128)(2,1)S(1)}, bf16[640,128]{1,0:T(8,128)(2,1)S(1)}, u32[]{:S(2)}, u32[]{:S(2)}) collective-permute-start(bf16[640,128]{1,0:T(8,128)(2,1)S(1)} %add.41), channel_id=1, source_target_pairs={{0,4},{4,0},{8,12},{12,8},{16,20},{20,16},{24,28},{28,24},{1,5},{5... | collective-permute-start | bytes 491528 | tf_op jit(solution)/shard_map/ppermute | solution.py:29
  65.4 8.0 %collective-permute-start.20 = (bf16[1280,128]{1,0:T(8,128)(2,1)S(1)}, bf16[1280,128]{1,0:T(8,128)(2,1)S(1)}, u32[]{:S(2)}, u32[]{:S(2)}) collective-permute-start(bf16[1280,128]{1,0:T(8,128)(2,1)S(1)} %pad_maximum_fusion.1.refs_4_), channel_id=1, source_target_pairs={{0,1},{1,2},{2,3},{7,6},{6,5},{5,4},{8,9},{9,10},{10,11},{15,14},{... | collective-permute-start | bytes 983048 | tf_op jit(solution)/shard_map/ppermute | solution.py:378
  68.9 8.5 %collective-permute-start.9 = (bf16[1280,128]{1,0:T(8,128)(2,1)S(1)}, bf16[1280,128]{1,0:T(8,128)(2,1)S(1)}, u32[]{:S(2)}, u32[]{:S(2)}) collective-permute-start(bf16[1280,128]{1,0:T(8,128)(2,1)S(1)} %pad_maximum_fusion.refs_3_), channel_id=1, source_target_pairs={{0,1},{1,2},{2,3},{7,6},{6,5},{5,4},{8,9},{9,10},{10,11},{15,14},{... | collective-permute-start | bytes 983048 | tf_op jit(solution)/shard_map/ppermute | solution.py:378
  73.4 5.2 %collective-permute-start.21 = (bf16[1280,128]{1,0:T(8,128)(2,1)S(1)}, bf16[1280,128]{1,0:T(8,128)(2,1)S(1)}, u32[]{:S(2)}, u32[]{:S(2)}) collective-permute-start(bf16[1280,128]{1,0:T(8,128)(2,1)S(1)} %collective-permute-done.20.refs_4_), channel_id=1, source_target_pairs={{1,2},{2,3},{6,5},{5,4},{9,10},{10,11},{14,13},{13,12},{17,18},{18... | collective-permute-start | bytes 983048 | tf_op jit(solution)/shard_map/ppermute | solution.py:378
  77.4 1.9 %collective-permute-start.10 = (bf16[1280,128]{1,0:T(8,128)(2,1)S(1)}, bf16[1280,128]{1,0:T(8,128)(2,1)S(1)}, u32[]{:S(2)}, u32[]{:S(2)}) collective-permute-start(bf16[1280,128]{1,0:T(8,128)(2,1)S(1)} %collective-permute-done.9.refs_3_), channel_id=1, source_target_pairs={{1,2},{2,3},{6,5},{5,4},{9,10},{10,11},{14,13},{13,12},{17,18},{18... | collective-permute-start | bytes 983048 | tf_op jit(solution)/shard_map/ppermute | solution.py:378
  78.0 8.8 %collective-permute-start.29 = (bf16[1280,128]{1,0:T(8,128)(2,1)S(1)}, bf16[1280,128]{1,0:T(8,128)(2,1)S(1)}, u32[]{:S(2)}, u32[]{:S(2)}) collective-permute-start(bf16[1280,128]{1,0:T(8,128)(2,1)S(1)} %collective-permute-done.20.refs_4_), channel_id=1, source_target_pairs={{0,4},{4,0},{8,12},{12,8},{16,20},{20,16},{24,28},{28,24},{1,5},{5... | collective-permute-start | bytes 983048 | tf_op jit(solution)/shard_map/ppermute | solution.py:29
  78.6 8.7 %collective-permute-start.25 = (bf16[1280,128]{1,0:T(8,128)(2,1)S(1)}, bf16[1280,128]{1,0:T(8,128)(2,1)S(1)}, u32[]{:S(2)}, u32[]{:S(2)}) collective-permute-start(bf16[1280,128]{1,0:T(8,128)(2,1)S(1)} %collective-permute-done.21.refs_8_.refs_4_), channel_id=1, source_target_pairs={{2,3},{5,4},{10,11},{13,12},{18,19},{21,20},{26,27},{29,28}} | collective-permute-start | bytes 983048 | tf_op jit(solution)/shard_map/ppermute | solution.py:378
  79.3 10.4 %collective-permute-start.24 = (bf16[1280,128]{1,0:T(8,128)(2,1)S(1)}, bf16[1280,128]{1,0:T(8,128)(2,1)S(1)}, u32[]{:S(2)}, u32[]{:S(2)}) collective-permute-start(bf16[1280,128]{1,0:T(8,128)(2,1)S(1)} %collective-permute-done.10.refs_7_.refs_3_), channel_id=1, source_target_pairs={{2,3},{5,4},{10,11},{13,12},{18,19},{21,20},{26,27},{29,28}} | collective-permute-start | bytes 983048 | tf_op jit(solution)/shard_map/ppermute | solution.py:378
  80.0 16.1 %collective-permute-start.28 = (bf16[1280,128]{1,0:T(8,128)(2,1)S(1)}, bf16[1280,128]{1,0:T(8,128)(2,1)S(1)}, u32[]{:S(2)}, u32[]{:S(2)}) collective-permute-start(bf16[1280,128]{1,0:T(8,128)(2,1)S(1)} %collective-permute-done.9.refs_3_), channel_id=1, source_target_pairs={{0,4},{4,0},{8,12},{12,8},{16,20},{20,16},{24,28},{28,24},{1,5},{5... | collective-permute-start | bytes 983048 | tf_op jit(solution)/shard_map/ppermute | solution.py:29
  86.7 12.2 %collective-permute-start.23 = (bf16[1280,128]{1,0:T(8,128)(2,1)S(1)}, bf16[1280,128]{1,0:T(8,128)(2,1)S(1)}, u32[]{:S(2)}, u32[]{:S(2)}) collective-permute-start(bf16[1280,128]{1,0:T(8,128)(2,1)S(1)} %collective-permute-done.21.refs_8_.refs_4_), channel_id=1, source_target_pairs={{0,4},{4,0},{8,12},{12,8},{16,20},{20,16},{24,28},{28,24},{1,5},{5... | collective-permute-start | bytes 983048 | tf_op jit(solution)/shard_map/ppermute | solution.py:29
  86.8 12.1 %collective-permute-start.22 = (bf16[1280,128]{1,0:T(8,128)(2,1)S(1)}, bf16[1280,128]{1,0:T(8,128)(2,1)S(1)}, u32[]{:S(2)}, u32[]{:S(2)}) collective-permute-start(bf16[1280,128]{1,0:T(8,128)(2,1)S(1)} %collective-permute-done.10.refs_7_.refs_3_), channel_id=1, source_target_pairs={{0,4},{4,0},{8,12},{12,8},{16,20},{20,16},{24,28},{28,24},{1,5},{5... | collective-permute-start | bytes 983048 | tf_op jit(solution)/shard_map/ppermute | solution.py:29
  87.2 14.8 %collective-permute-start.27 = (bf16[1280,128]{1,0:T(8,128)(2,1)S(1)}, bf16[1280,128]{1,0:T(8,128)(2,1)S(1)}, u32[]{:S(2)}, u32[]{:S(2)}) collective-permute-start(bf16[1280,128]{1,0:T(8,128)(2,1)S(1)} %collective-permute-done.25.refs_8_), channel_id=1, source_target_pairs={{0,4},{4,0},{8,12},{12,8},{16,20},{20,16},{24,28},{28,24},{1,5},{5... | collective-permute-start | bytes 983048 | tf_op jit(solution)/shard_map/ppermute | solution.py:29
  89.7 12.4 %collective-permute-start.26 = (bf16[1280,128]{1,0:T(8,128)(2,1)S(1)}, bf16[1280,128]{1,0:T(8,128)(2,1)S(1)}, u32[]{:S(2)}, u32[]{:S(2)}) collective-permute-start(bf16[1280,128]{1,0:T(8,128)(2,1)S(1)} %collective-permute-done.24.refs_7_), channel_id=1, source_target_pairs={{0,4},{4,0},{8,12},{12,8},{16,20},{20,16},{24,28},{28,24},{1,5},{5... | collective-permute-start | bytes 983048 | tf_op jit(solution)/shard_map/ppermute | solution.py:29
  (5 other events, 49.0 us)

commit v5 on v4

--- a/solution.py
+++ b/solution.py
@@ -12,6 +12,9 @@
 KV_TOTAL = 1280
 STACK = 2
 MIB = 2**20
+EDGES = [(0, 1), (1, 0), (2, 3), (3, 2)]
+MIDDLE = [(1, 2), (2, 1)]
+OUTWARD = [(1, 0), (2, 3)]
 
 VMEM = pl.BlockSpec(memory_space=pltpu.VMEM)
 SMEM = pl.BlockSpec(memory_space=pltpu.SMEM)
@@ -134,6 +137,35 @@
     return [[parts[0][piece], to_right[piece], to_left[piece]] for piece in range(2)], early
 
 
+def swap_sums(vis_feats, kv_weight, pair, early):
+    def first(here, n):
+        return jnp.where(here < 2, 3, 0)
+
+    def later(here, n):
+        return (jnp.where(here < 2, 2, 1), jnp.where(here < 2, 1 - here, 5 - here), here)[n]
+
+    far = project(first, 1, vis_feats, kv_weight, pair)[0]
+    near, last, own = project(later, 3, vis_feats, kv_weight, pair)
+    held = lax.optimization_barrier((far[1], own[0], *early))
+    far, own, early = (far[0], held[0]), (held[1], own[1]), held[2:]
+
+    def swap(value, pairs):
+        return lax.ppermute(value, "head", pairs)
+
+    def add(left, right):
+        return left + right
+
+    sums = []
+    for piece in range(2):
+        for_far = swap(far[piece], EDGES)
+        for_near = swap(near[piece], EDGES)
+        for_far = swap(add(far[piece], for_far), MIDDLE)
+        for_near = swap(add(near[piece], for_near), MIDDLE)
+        final = swap(add(last[piece], for_far), EDGES)
+        sums.append([own[piece], final, for_near])
+    return sums, early
+
+
 def finish_chunk(partial_sums, key_gain, image_tokens, image_owner, per_kv, are_keys):
     rows, head_dim = partial_sums[0].shape
     half = KV_TOTAL // 2
@@ -209,51 +241,41 @@
     )(image_tokens, cross_mask)
 
 
-def attend(call, own, arrivals, queries, row_mask, token_bias, kv_heads, images, previous, key_head=None):
+def put_halves(mine_ref, other_ref, first, put):
+    half = KV_TOTAL // 2
+    core = lax.axis_index("ctx") % 2
+    for at, ref in ((core, mine_ref), (1 - core, other_ref)):
+        put(pl.ds(pl.multiple_of(at * half, half), half), ref[first : first + half, :])
+
+
+def attend(head_of, first, keys, values, queries, row_mask, token_bias, kv_heads, images):
     rows, width = queries.shape
-    tokens, head_dim = own[0].shape
-    half = tokens // 2
+    tokens, head_dim = KV_TOTAL, keys[0].shape[1]
     block_width = width // kv_heads
     group = block_width // head_dim
     factor = head_dim ** (-0.5) * math.log2(math.e)
     stack = min(STACK, group)
     blocks = range(group // stack)
-    first_hop = (call + 1) // 2
-    sources = [own] if call == 0 else [pair for hop in arrivals[first_hop - 1 : call] for pair in hop]
-    count = len(sources)
-    line = lax.axis_size("head")
+    whole = values is not None
 
     def kernel(*refs):
-        queries_ref, mask_ref, bias_ref = refs[:3]
-        source_refs = refs[3 : 3 + 2 * count]
-        out_ref, keys_ref, values_ref, result_ref, sem = refs[3 + 2 * count + (previous is not None) :]
-        core = lax.axis_index("ctx") % 2
-        head = lax.axis_index("head") if key_head is None else key_head
-
-        def take(n, core):
-            for side, at in ((0, core), (1, 1 - core)):
-                span = pl.ds(pl.multiple_of(at * half, half), half)
-                keys_ref[span, :head_dim] = source_refs[2 * n][side * half : (side + 1) * half, :]
-                values_ref[span, :] = source_refs[2 * n + 1][side * half : (side + 1) * half, :]
-
+        queries_ref, mask_ref, bias_ref, *key_refs = refs[:5]
+        if whole:
+            *value_refs, result_ref, keys_ref, values_ref = refs[5:]
+
+            def put_values(span, half):
+                values_ref[span, :] = half
+
+            put_halves(*value_refs, first, put_values)
+        else:
+            weights_ref, sums_ref, keys_ref = refs[5:]
+
+        def put_keys(span, half):
+            keys_ref[span, :head_dim] = half
+
+        put_halves(*key_refs, first, put_keys)
         keys_ref[:, head_dim:] = bias_ref[...]
-        if call == 0:
-            take(0, core)
-        else:
-            here, step = head, 1 - 2 * core
-            rank = jnp.int32(0)
-            for hop in range(1, call + 1):
-                for side in range(2):
-                    candidate = here + (hop if side else -hop) * step
-                    valid = (candidate >= 0) & (candidate < line)
-                    rank = rank + jnp.where(valid, 1, 0)
-                    chosen = valid & (rank == call)
-                    head = jnp.where(chosen, candidate, head)
-                    if hop >= first_hop:
-                        n = 2 * (hop - first_hop) + side
-                        source_core = 1 - core if side else core
-                        pl.when(chosen)(lambda n=n, at=source_core: take(n, at))
-        column = pl.multiple_of(head * block_width, block_width)
+        column = pl.multiple_of(head_of(lax.axis_index("head")) * block_width, block_width)
         some = jnp.min(mask_ref[:, :images].astype(jnp.float32), axis=1, keepdims=True) < 0.5
 
         def scores_of(n):
@@ -273,48 +295,105 @@
             following = scores_of(n + 1) if n + 1 < len(blocks) else None
             largest = jnp.max(scores, axis=1, keepdims=True)
             weights = jnp.exp2((scores - largest) * factor)
-            summed = jnp.sum(weights, axis=1, keepdims=True)
-            mixed = jnp.dot(
-                weights.astype(jnp.bfloat16), values_ref[...], preferred_element_type=jnp.float32
-            )
-            mixed = mixed / jnp.maximum(summed, 1.0)
+            summed = jnp.maximum(jnp.sum(weights, axis=1, keepdims=True), 1.0)
+            weights = weights.astype(jnp.bfloat16)
+            scores = following
+            if not whole:
+                span = slice(n * stack * rows, (n + 1) * stack * rows)
+                weights_ref[span, :] = weights
+                sums_ref[span, :] = jnp.broadcast_to(summed, (stack * rows, head_dim))
+                continue
+            mixed = jnp.dot(weights, values_ref[...], preferred_element_type=jnp.float32) / summed
             for j in range(stack):
                 one = jnp.where(some, mixed[j * rows : (j + 1) * rows], 0.0)
                 at = (n * stack + j) * head_dim
                 result_ref[:, at : at + head_dim] = one.astype(jnp.bfloat16)
-            scores = following
-        store = pltpu.make_async_copy(result_ref, out_ref.at[:, pl.ds(column, block_width)], sem)
-        store.start()
-        store.wait()
-
-    operands = [queries, row_mask, token_bias]
-    for source in sources:
-        operands += source
-    in_specs = [VMEM] * len(operands)
-    aliases = {}
-    if previous is not None:
-        aliases = {len(operands): 0}
-        operands.append(previous)
-        in_specs.append(ANYWHERE)
+
+    operands = [queries, row_mask, token_bias, *keys, *(values or ())]
+    if whole:
+        out_shape = [jax.ShapeDtypeStruct((rows, block_width), jnp.bfloat16)]
+    else:
+        out_shape = [
+            jax.ShapeDtypeStruct((group * rows, tokens), jnp.bfloat16),
+            jax.ShapeDtypeStruct((group * rows, head_dim), jnp.float32),
+        ]
+    scratch = [pltpu.VMEM((tokens, 2 * head_dim), jnp.bfloat16)]
+    if whole:
+        scratch.append(pltpu.VMEM((tokens, head_dim), jnp.bfloat16))
     return pl.pallas_call(
         kernel,
-        in_specs=in_specs,
-        out_specs=ANYWHERE,
-        out_shape=jax.ShapeDtypeStruct((rows, width), jnp.bfloat16),
-        scratch_shapes=[
-            pltpu.VMEM((tokens, 2 * head_dim), jnp.bfloat16),
-            pltpu.VMEM((tokens, head_dim), jnp.bfloat16),
-            pltpu.VMEM((rows, block_width), jnp.bfloat16),
-            pltpu.SemaphoreType.DMA,
-        ],
-        input_output_aliases=aliases,
-        compiler_params=params(16),
+        in_specs=[VMEM] * len(operands),
+        out_specs=[VMEM] * len(out_shape),
+        out_shape=out_shape,
+        scratch_shapes=scratch,
+        compiler_params=params(14),
         cost_estimate=pl.CostEstimate(
-            flops=6 * rows * group * tokens * head_dim,
-            bytes_accessed=rows * block_width * 4,
+            flops=(6 if whole else 4) * rows * group * tokens * head_dim,
+            bytes_accessed=rows * block_width * 2,
             transcendentals=rows * group * tokens,
         ),
-        name="attend",
+        name="attend" if whole else "weigh",
+    )(*operands)
+
+
+def mix_far(heads_of, values, weighed, row_mask, earlier, images):
+    head_dim = values[0].shape[1]
+    rows = row_mask.shape[0]
+    block_width = earlier[0].shape[1]
+    group = block_width // head_dim
+    before, count = len(earlier), len(weighed)
+    half = KV_TOTAL // 2
+
+    def kernel(*refs):
+        weighed_refs, refs = refs[: 2 * count], refs[2 * count :]
+        mask_ref, mine_ref, other_ref = refs[:3]
+        earlier_refs = refs[3 : 3 + before]
+        out_ref, values_ref, result_ref, sems = refs[3 + before :]
+        here = lax.axis_index("head")
+
+        def store(n, ref):
+            column = pl.multiple_of(heads_of[n](here) * block_width, block_width)
+            return pltpu.make_async_copy(ref, out_ref.at[:, pl.ds(column, block_width)], sems.at[n])
+
+        for n, ref in enumerate(earlier_refs):
+            store(n, ref).start()
+        some = jnp.min(mask_ref[:, :images].astype(jnp.float32), axis=1, keepdims=True) < 0.5
+        for n in range(count):
+
+            def put(span, block):
+                values_ref[n, span, :] = block
+
+            put_halves(mine_ref, other_ref, n * half, put)
+        for n in range(count):
+            mixed = jnp.dot(weighed_refs[2 * n][...], values_ref[n], preferred_element_type=jnp.float32)
+            mixed = mixed / weighed_refs[2 * n + 1][...]
+            for j in range(group):
+                one = jnp.where(some, mixed[j * rows : (j + 1) * rows], 0.0)
+                result_ref[n, :, j * head_dim : (j + 1) * head_dim] = one.astype(jnp.bfloat16)
+            store(before + n, result_ref.at[n]).start()
+        for n, ref in enumerate(earlier_refs):
+            store(n, ref).wait()
+        for n in range(count):
+            store(before + n, result_ref.at[n]).wait()
+
+    operands = [array for pair in weighed for array in pair] + [row_mask, *values, *earlier]
+    return pl.pallas_call(
+        kernel,
+        in_specs=[VMEM] * len(operands),
+        out_specs=HBM,
+        out_shape=jax.ShapeDtypeStruct((rows, (before + count) * block_width), jnp.bfloat16),
+        scratch_shapes=[
+            pltpu.VMEM((count, KV_TOTAL, head_dim), jnp.bfloat16),
+            pltpu.VMEM((count, rows, block_width), jnp.bfloat16),
+            pltpu.SemaphoreType.DMA((before + count,)),
+        ],
+        compiler_params=params(12),
+        cost_estimate=pl.CostEstimate(
+            flops=2 * count * rows * group * KV_TOTAL * head_dim,
+            bytes_accessed=rows * block_width * 2 * (before + count),
+            transcendentals=0,
+        ),
+        name="mix_far",
     )(*operands)
 
 
@@ -328,7 +407,8 @@
     images = image_tokens.shape[0]
 
     masks = mask_columns(cross_mask, image_tokens, head_dim, queries.shape[0])
-    partial_sums, (row_mask, token_bias) = sum_over_head(vis_feats, kv_weight, 2 * head_dim, masks)
+    add_up = swap_sums if head_count == 4 else sum_over_head
+    partial_sums, (row_mask, token_bias) = add_up(vis_feats, kv_weight, 2 * head_dim, masks)
 
     def spread(piece):
         block, other = finish_chunk(
@@ -343,43 +423,52 @@
                 (c, c ^ (2**step if c % 2 == 0 else 2 ** (ctx_bits - step))) for c in range(ctx_count)
             ]
             block = block + lax.ppermute(block, "ctx", pairs)
-        other = swapped(block, "ctx", 0)
-        return jnp.concatenate([block, other], 0)
+        return block
 
     keys, values = spread(0), spread(1)
 
-    if per_kv > 1:
+    def run(head_of, first, keys, values):
+        return attend(head_of, first, keys, values, queries, row_mask, token_bias, kv_heads, images)
+
+    def join(block):
+        return block, swapped(block, "ctx", 0)
+
+    if head_count != 4 or per_kv > 1:
         groups = [[k * per_kv + j for k in range(kv_heads)] for j in range(per_kv)]
-        keys = lax.all_gather(keys, "head", axis_index_groups=groups)
-        values = lax.all_gather(values, "head", axis_index_groups=groups)
-        out = None
+        keys, values = (
+            join(lax.all_gather(block, "head", axis_index_groups=groups))
+            for block in (keys, values)
+        )
+        parts = []
         for k in range(kv_heads):
-            own = (keys[k], values[k])
-            out = attend(0, own, [], queries, row_mask, token_bias, kv_heads, images, out, k)
-        return out
-
-    def place(c, h):
-        return c * head_count + h
-
-    own = (keys, values)
-    arrivals = []
-    out = attend(0, own, arrivals, queries, row_mask, token_bias, kv_heads, images, None)
-    passing = [keys, values]
-    for hop in range(1, head_count):
-        pairs = []
-        for c in range(ctx_count):
-            for i in range(hop - 1, head_count - 1):
-                if c % 2 == 0:
-                    pairs.append((place(c, i), place(c, i + 1)))
-                else:
-                    pairs.append((place(c, head_count - 1 - i), place(c, head_count - 2 - i)))
-        crossing = [None, None]
-        for piece in range(2):
-            passing[piece] = lax.ppermute(passing[piece], ("ctx", "head"), pairs)
-            crossing[piece] = swapped(passing[piece], "ctx", 0)
-        arrivals.append([tuple(passing), tuple(crossing)])
-        out = attend(hop, own, arrivals, queries, row_mask, token_bias, kv_heads, images, out)
-    return out
+            halves = ([mine[k], other[k]] for mine, other in (keys, values))
+            parts += run(lambda here, k=k: k, 0, *halves)
+        return jnp.concatenate(parts, axis=1)
+
+    held = [[], [], [], []]
+    for block in (keys, values):
+
+        def swap(value, pairs):
+            return lax.ppermute(value, "head", pairs)
+
+        near = swap(block, EDGES)
+        inner = swap(block, MIDDLE)
+        outer = swap(near, MIDDLE)
+        inner = inner + swap(inner, OUTWARD)
+        outer = outer + swap(outer, OUTWARD)
+        for n, half in enumerate((block, near, inner, outer)):
+            held[n].append(join(half))
+    heads_of = [
+        lambda here: here,
+        lambda here: jnp.where(here % 2 == 0, here + 1, here - 1),
+        lambda here: jnp.where(here < 2, 2, 1),
+        lambda here: jnp.where(here < 2, 3, 0),
+    ]
+    parts = []
+    for n in range(3):
+        parts += run(heads_of[n], 0, *held[n])
+    weighed = [run(heads_of[3], 0, held[3][0], None)]
+    return mix_far(heads_of, held[3][1], weighed, row_mask, parts, images)
 
 
 def solution(mesh):

time: 107 us -> 94.8 us (0.89); the launches traced: 105 us -> 94.4 us
  starting transfers between devices: 59.9 us -> 40.7 us
  waiting for transfers between devices: 19.7 us -> 32.1 us
  Pallas kernels: 20.5 us -> 18 us
  local copies, waits for them, and re-layouts: 3.95 us -> 2.35 us
    ppermute x16 -> x20, waiting for transfers between devices: 13.4 us -> 27.4 us  [swap(): return lax.ppermute(value, 'head', pairs)]
    ppermute x10, starting transfers between devices: 14 us -> 1.44 us  [swapped(): return lax.ppermute(value, axis, pairs)]
    ppermute x16 -> x20, starting transfers between devices: 39.8 us -> 33.2 us  [swap(): return lax.ppermute(value, 'head', pairs)]
    pallas_call x4 -> x5, Pallas kernels: 11.8 us -> 9.67 us  [the longest x4 8.05 us: attend(): pl.pallas_call(kernel, in_specs=[VMEM] * len(operands), out_specs=[VMEM]...]
    ppermute x4, waiting for transfers between devices: 6.24 us -> 4.61 us  [spread(): block = block + lax.ppermute(block, 'ctx', pairs)]
    unnamed x15, local copies, waits for them, and re-layouts: 3.95 us -> 2.35 us
  transfers between devices with their start and end apart: 30 -> 34, of which waited for: 10 -> 14; matrix products, arithmetic and copies ran while one was open for 0% -> 1% of each run, Pallas kernels for 11% -> 14%
where the time goes in v5:
time: 94.8 us; the launch traced here: 94.4 us
  starting transfers between devices  40.7 us (43%)
  waiting for transfers between devices  32.1 us (34%)
  Pallas kernels  18 us (19%)
  local copies, waits for them, and re-layouts  2.35 us (2%)
    ppermute x20, starting transfers between devices, swap(): return lax.ppermute(value, 'head', pairs)  33.2 us
    ppermute x20, waiting for transfers between devices, swap(): return lax.ppermute(value, 'head', pairs)  27.4 us
    pallas_call x4, Pallas kernels, attend(): pl.pallas_call(kernel, in_specs=[VMEM] * len(operands), out_specs=[VMEM]...  8.05 us
    ppermute x4, starting transfers between devices, spread(): block = block + lax.ppermute(block, 'ctx', pairs)  6.06 us
    ppermute x4, waiting for transfers between devices, spread(): block = block + lax.ppermute(block, 'ctx', pairs)  4.61 us
    pallas_call x2, Pallas kernels, project(): pl.pallas_call(kernel, in_specs=[HBM, HBM] if alone else [VMEM, VMEM], ou...  4.59 us
    unnamed x15, local copies, waits for them, and re-layouts  2.35 us
    pallas_call x2, Pallas kernels, finish_chunk(): pl.pallas_call(kernel, in_specs=[SMEM] * 2 + [VMEM] * 4, out_specs=[VMEM]...  2.19 us
  transfers between devices with their start and end apart: 34, of which 14 were waited for; matrix products, arithmetic and copies ran while one was open for 1% of the time, Pallas kernels for 14%

profile of v5, /device:TPU:0, one launch (start us, length us, event | category | flops | bytes accessed | tf_op | source)
XLA Modules:
  0.0 94.4 jit_solution(5227686984970773965)
XLA Ops:
  0.0 2.8 %project.2 = (f32[512,128]{1,0:T(8,128)S(1)}, f32[512,128]{1,0:T(8,128)S(1)}) custom-call(bf16[512,2048]{1,0:T(8,128)(2,1)} %feats_ref.3, bf16[2048,1024]{1,0:T(8,128)(2,1)} %weight_ref.3), custom_call_target="tpu_custom_call" | custom-call | flops 536870912 | bytes 3145728 | tf_op jit(solution)/shard_map/project/pallas_call | solution.py:83
  2.8 3.1 %collective-permute-start = (f32[512,128]{1,0:T(8,128)S(1)}, f32[512,128]{1,0:T(8,128)S(1)}, u32[]{:S(2)}, u32[]{:S(2)}) collective-permute-start(f32[512,128]{1,0:T(8,128)S(1)} %get-tuple-element.33), channel_id=1, source_target_pairs={{0,1},{1,0},{2,3},{3,2},{4,5},{5,4},{6,7},{7,6},{8,9},{9,8},{10,11... | collective-permute-start | bytes 786440 | tf_op jit(solution)/shard_map/ppermute | solution.py:153
  6.1 1.6 %masks.1 = (bf16[128,128]{1,0:T(8,128)(2,1)S(1)}, bf16[1280,128]{1,0:T(8,128)(2,1)S(1)}) custom-call(s32[4]{0:T(128)S(1)} %copy-done.2, s32[512,4]{1,0:T(8,128)S(1)} %copy.8.cross_ref), custom_call_target="tpu_custom_call" | custom-call | tf_op jit(solution)/shard_map/masks/pallas_call | solution.py:231
  7.6 2.2 %copy-done = bf16[2048,1024]{1,0:T(8,128)(2,1)S(1)} copy-done((bf16[2048,1024]{1,0:T(8,128)(2,1)S(1)}, bf16[2048,1024]{1,0:T(8,128)(2,1)}, u32[]{:S(2)}) %copy-start) | copy-done | bytes 4194328
  9.8 1.8 %project.3 = (f32[512,128]{1,0:T(8,128)S(1)}, f32[512,128]{1,0:T(8,128)S(1)}, f32[512,128]{1,0:T(8,128)S(1)}, f32[512,128]{1,0:T(8,128)S(1)}, f32[512,128]{1,0:T(8,128)S(1)}, /*index=5*/f32[512,128]{1,0:T(8,128)S(1)}) custom-call(bf16[512,2048]{1,0:T(8,128)(2,1)S(1)} %copy-done.1, bf16[2048,1024]{1,0:T(8,128)(2,1)S(1)} %copy-done), custom_call_target="tpu_custom_call" | custom-call | flops 1610612736 | bytes 5242880 | tf_op jit(solution)/shard_map/project/pallas_call | solution.py:83
  11.8 2.0 %collective-permute-start.3 = (f32[512,128]{1,0:T(8,128)S(1)}, f32[512,128]{1,0:T(8,128)S(1)}, u32[]{:S(2)}, u32[]{:S(2)}) collective-permute-start(f32[512,128]{1,0:T(8,128)S(1)} %get-tuple-element.34), channel_id=1, source_target_pairs={{0,1},{1,0},{2,3},{3,2},{4,5},{5,4},{6,7},{7,6},{8,9},{9,8},{10,11... | collective-permute-start | bytes 786440 | tf_op jit(solution)/shard_map/ppermute | solution.py:153
  14.5 4.5 %collective-permute-start.15 = (f32[512,128]{1,0:T(8,128)S(1)}, f32[512,128]{1,0:T(8,128)S(1)}, u32[]{:S(2)}, u32[]{:S(2)}) collective-permute-start(f32[512,128]{1,0:T(8,128)S(1)} %get-tuple-element.42), channel_id=1, source_target_pairs={{0,1},{1,0},{2,3},{3,2},{4,5},{5,4},{6,7},{7,6},{8,9},{9,8},{10,11... | collective-permute-start | bytes 786440 | tf_op jit(solution)/shard_map/ppermute | solution.py:153
  19.0 2.0 %collective-permute-done.12 = f32[512,128]{1,0:T(8,128)S(1)} collective-permute-done((f32[512,128]{1,0:T(8,128)S(1)}, f32[512,128]{1,0:T(8,128)S(1)}, u32[]{:S(2)}, u32[]{:S(2)}) %collective-permute-start.12) | collective-permute-done | bytes 262176 | tf_op jit(solution)/shard_map/ppermute | solution.py:153
  21.6 4.9 %collective-permute-done.3 = f32[512,128]{1,0:T(8,128)S(1)} collective-permute-done((f32[512,128]{1,0:T(8,128)S(1)}, f32[512,128]{1,0:T(8,128)S(1)}, u32[]{:S(2)}, u32[]{:S(2)}) %collective-permute-start.3) | collective-permute-done | bytes 262176 | tf_op jit(solution)/shard_map/ppermute | solution.py:153
  27.3 4.5 %collective-permute-start.2 = (f32[512,128]{1,0:T(8,128)S(1)}, f32[512,128]{1,0:T(8,128)S(1)}, u32[]{:S(2)}, u32[]{:S(2)}) collective-permute-start(f32[512,128]{1,0:T(8,128)S(1)} %add.49), channel_id=1, source_target_pairs={{0,1},{1,0},{2,3},{3,2},{4,5},{5,4},{6,7},{7,6},{8,9},{9,8},{10,11... | collective-permute-start | bytes 786440 | tf_op jit(solution)/shard_map/ppermute | solution.py:153
  32.7 4.7 %collective-permute-start.14 = (f32[512,128]{1,0:T(8,128)S(1)}, f32[512,128]{1,0:T(8,128)S(1)}, u32[]{:S(2)}, u32[]{:S(2)}) collective-permute-start(f32[512,128]{1,0:T(8,128)S(1)} %add.56), channel_id=1, source_target_pairs={{0,1},{1,0},{2,3},{3,2},{4,5},{5,4},{6,7},{7,6},{8,9},{9,8},{10,11... | collective-permute-start | bytes 786440 | tf_op jit(solution)/shard_map/ppermute | solution.py:153
  38.7 3.2 %collective-permute-done.14.left_ref = f32[512,128]{1,0:T(8,128)S(1)} collective-permute-done((f32[512,128]{1,0:T(8,128)S(1)}, f32[512,128]{1,0:T(8,128)S(1)}, u32[]{:S(2)}, u32[]{:S(2)}) %collective-permute-start.14) | collective-permute-done | bytes 262176 | tf_op jit(solution)/shard_map/ppermute | solution.py:153
  43.2 1.6 %collective-permute-start.6 = (bf16[640,128]{1,0:T(8,128)(2,1)S(1)}, bf16[640,128]{1,0:T(8,128)(2,1)S(1)}, u32[]{:S(2)}, u32[]{:S(2)}) collective-permute-start(bf16[640,128]{1,0:T(8,128)(2,1)S(1)} %add.51), channel_id=1, source_target_pairs={{0,8},{4,20},{8,0},{12,28},{16,24},{20,4},{24,16},{28,12},{1,9},{5... | collective-permute-start | bytes 491528 | tf_op jit(solution)/shard_map/ppermute | solution.py:425
  44.8 1.3 %collective-permute-start.18 = (bf16[640,128]{1,0:T(8,128)(2,1)S(1)}, bf16[640,128]{1,0:T(8,128)(2,1)S(1)}, u32[]{:S(2)}, u32[]{:S(2)}) collective-permute-start(bf16[640,128]{1,0:T(8,128)(2,1)S(1)} %add.58), channel_id=1, source_target_pairs={{0,8},{4,20},{8,0},{12,28},{16,24},{20,4},{24,16},{28,12},{1,9},{5... | collective-permute-start | bytes 491528 | tf_op jit(solution)/shard_map/ppermute | solution.py:425
  46.1 2.5 %collective-permute-done.6 = bf16[640,128]{1,0:T(8,128)(2,1)S(1)} collective-permute-done((bf16[640,128]{1,0:T(8,128)(2,1)S(1)}, bf16[640,128]{1,0:T(8,128)(2,1)S(1)}, u32[]{:S(2)}, u32[]{:S(2)}) %collective-permute-start.6) | collective-permute-done | bytes 163872 | tf_op jit(solution)/shard_map/ppermute | solution.py:425
  48.6 1.6 %collective-permute-start.7 = (bf16[640,128]{1,0:T(8,128)(2,1)S(1)}, bf16[640,128]{1,0:T(8,128)(2,1)S(1)}, u32[]{:S(2)}, u32[]{:S(2)}) collective-permute-start(bf16[640,128]{1,0:T(8,128)(2,1)S(1)} %add.52), channel_id=1, source_target_pairs={{0,16},{4,12},{8,24},{12,4},{16,0},{20,28},{24,8},{28,20},{1,17},{... | collective-permute-start | bytes 491528 | tf_op jit(solution)/shard_map/ppermute | solution.py:425
  50.4 1.6 %collective-permute-start.19 = (bf16[640,128]{1,0:T(8,128)(2,1)S(1)}, bf16[640,128]{1,0:T(8,128)(2,1)S(1)}, u32[]{:S(2)}, u32[]{:S(2)}) collective-permute-start(bf16[640,128]{1,0:T(8,128)(2,1)S(1)} %add.59), channel_id=1, source_target_pairs={{0,16},{4,12},{8,24},{12,4},{16,0},{20,28},{24,8},{28,20},{1,17},{... | collective-permute-start | bytes 491528 | tf_op jit(solution)/shard_map/ppermute | solution.py:425
  52.0 2.0 %collective-permute-done.7 = bf16[640,128]{1,0:T(8,128)(2,1)S(1)} collective-permute-done((bf16[640,128]{1,0:T(8,128)(2,1)S(1)}, bf16[640,128]{1,0:T(8,128)(2,1)S(1)}, u32[]{:S(2)}, u32[]{:S(2)}) %collective-permute-start.7) | collective-permute-done | bytes 163872 | tf_op jit(solution)/shard_map/ppermute | solution.py:425
  54.1 1.9 %collective-permute-start.8 = (bf16[640,128]{1,0:T(8,128)(2,1)S(1)}, bf16[640,128]{1,0:T(8,128)(2,1)S(1)}, u32[]{:S(2)}, u32[]{:S(2)}) collective-permute-start(bf16[640,128]{1,0:T(8,128)(2,1)S(1)} %add.53.refs_3_), channel_id=1, source_target_pairs={{0,1},{1,0},{2,3},{3,2},{4,5},{5,4},{6,7},{7,6},{8,9},{9,8},{10,11... | collective-permute-start | bytes 491528 | tf_op jit(solution)/shard_map/ppermute | solution.py:452
  56.0 1.7 %collective-permute-start.20 = (bf16[640,128]{1,0:T(8,128)(2,1)S(1)}, bf16[640,128]{1,0:T(8,128)(2,1)S(1)}, u32[]{:S(2)}, u32[]{:S(2)}) collective-permute-start(bf16[640,128]{1,0:T(8,128)(2,1)S(1)} %add.60.refs_5_), channel_id=1, source_target_pairs={{0,1},{1,0},{2,3},{3,2},{4,5},{5,4},{6,7},{7,6},{8,9},{9,8},{10,11... | collective-permute-start | bytes 491528 | tf_op jit(solution)/shard_map/ppermute | solution.py:452
  59.1 1.7 %collective-permute-done.8.refs_3_ = bf16[640,128]{1,0:T(8,128)(2,1)S(1)} collective-permute-done((bf16[640,128]{1,0:T(8,128)(2,1)S(1)}, bf16[640,128]{1,0:T(8,128)(2,1)S(1)}, u32[]{:S(2)}, u32[]{:S(2)}) %collective-permute-start.8) | collective-permute-done | bytes 163872 | tf_op jit(solution)/shard_map/ppermute | solution.py:452
  64.6 1.3 %collective-permute-start.32 = (bf16[640,128]{1,0:T(8,128)(2,1)S(1)}, bf16[640,128]{1,0:T(8,128)(2,1)S(1)}, u32[]{:S(2)}, u32[]{:S(2)}) collective-permute-start(bf16[640,128]{1,0:T(8,128)(2,1)S(1)} %collective-permute-done.31), channel_id=1, source_target_pairs={{1,0},{2,3},{5,4},{6,7},{9,8},{10,11},{13,12},{14,15},{17,16},{18,... | collective-permute-start | bytes 491528 | tf_op jit(solution)/shard_map/ppermute | solution.py:452
  66.0 1.3 %collective-permute-start.10 = (bf16[640,128]{1,0:T(8,128)(2,1)S(1)}, bf16[640,128]{1,0:T(8,128)(2,1)S(1)}, u32[]{:S(2)}, u32[]{:S(2)}) collective-permute-start(bf16[640,128]{1,0:T(8,128)(2,1)S(1)} %collective-permute-done.9), channel_id=1, source_target_pairs={{1,0},{2,3},{5,4},{6,7},{9,8},{10,11},{13,12},{14,15},{17,16},{18,... | collective-permute-start | bytes 491528 | tf_op jit(solution)/shard_map/ppermute | solution.py:452
  67.3 1.5 %collective-permute-start.22 = (bf16[640,128]{1,0:T(8,128)(2,1)S(1)}, bf16[640,128]{1,0:T(8,128)(2,1)S(1)}, u32[]{:S(2)}, u32[]{:S(2)}) collective-permute-start(bf16[640,128]{1,0:T(8,128)(2,1)S(1)} %collective-permute-done.21), channel_id=1, source_target_pairs={{1,0},{2,3},{5,4},{6,7},{9,8},{10,11},{13,12},{14,15},{17,16},{18,... | collective-permute-start | bytes 491528 | tf_op jit(solution)/shard_map/ppermute | solution.py:452
  68.7 7.5 %collective-permute-done.29 = bf16[640,128]{1,0:T(8,128)(2,1)S(1)} collective-permute-done((bf16[640,128]{1,0:T(8,128)(2,1)S(1)}, bf16[640,128]{1,0:T(8,128)(2,1)S(1)}, u32[]{:S(2)}, u32[]{:S(2)}) %collective-permute-start.29) | collective-permute-done | bytes 163872 | tf_op jit(solution)/shard_map/ppermute | solution.py:452
  76.2 3.5 %collective-permute-done.32 = bf16[640,128]{1,0:T(8,128)(2,1)S(1)} collective-permute-done((bf16[640,128]{1,0:T(8,128)(2,1)S(1)}, bf16[640,128]{1,0:T(8,128)(2,1)S(1)}, u32[]{:S(2)}, u32[]{:S(2)}) %collective-permute-start.32) | collective-permute-done | bytes 163872 | tf_op jit(solution)/shard_map/ppermute | solution.py:452
  80.4 2.8 %collective-permute-done.10 = bf16[640,128]{1,0:T(8,128)(2,1)S(1)} collective-permute-done((bf16[640,128]{1,0:T(8,128)(2,1)S(1)}, bf16[640,128]{1,0:T(8,128)(2,1)S(1)}, u32[]{:S(2)}, u32[]{:S(2)}) %collective-permute-start.10) | collective-permute-done | bytes 163872 | tf_op jit(solution)/shard_map/ppermute | solution.py:452
  83.2 2.1 %attend.3.refs_5_ = bf16[128,1024]{1,0:T(8,128)(2,1)S(1)} custom-call(bf16[128,4096]{1,0:T(8,128)(2,1)S(1)} %copy-done.5, bf16[128,128]{1,0:T(8,128)(2,1)S(1)} %get-tuple-element.29.refs_1_.refs_2_, bf16[1280,128]{1,0:T(8,128)(2,1)S(1)} %get-tuple-element.30.refs_2_, bf16[640,128]{1,0:T(8,128)(2,1)S(1)} %add.53.refs_3_, ...), custom_call_target="tpu_custom_call" | custom-call | flops 1006632960 | bytes 262144 | tf_op jit(solution)/shard_map/attend/pallas_call | solution.py:323
  86.6 2.1 %attend.4.refs_6_ = bf16[128,1024]{1,0:T(8,128)(2,1)S(1)} custom-call(bf16[128,4096]{1,0:T(8,128)(2,1)S(1)} %copy-done.5, bf16[128,128]{1,0:T(8,128)(2,1)S(1)} %get-tuple-element.29.refs_1_.refs_2_, bf16[1280,128]{1,0:T(8,128)(2,1)S(1)} %get-tuple-element.30.refs_2_, bf16[640,128]{1,0:T(8,128)(2,1)S(1)} %collective-permute-done.8.refs_3_, ...), custom_call_target="tpu_custom_call" | custom-call | flops 1006632960 | bytes 262144 | tf_op jit(solution)/shard_map/attend/pallas_call | solution.py:323
  88.8 2.1 %attend.5.refs_7_ = bf16[128,1024]{1,0:T(8,128)(2,1)S(1)} custom-call(bf16[128,4096]{1,0:T(8,128)(2,1)S(1)} %copy-done.5, bf16[128,128]{1,0:T(8,128)(2,1)S(1)} %get-tuple-element.29.refs_1_.refs_2_, bf16[1280,128]{1,0:T(8,128)(2,1)S(1)} %get-tuple-element.30.refs_2_, bf16[640,128]{1,0:T(8,128)(2,1)S(1)} %add.62.refs_3_, ...), custom_call_target="tpu_custom_call" | custom-call | flops 1006632960 | bytes 262144 | tf_op jit(solution)/shard_map/attend/pallas_call | solution.py:323
  90.9 1.7 %weigh.1 = (bf16[1024,1280]{1,0:T(8,128)(2,1)S(1)}, f32[1024,128]{1,0:T(8,128)S(1)}) custom-call(bf16[128,4096]{1,0:T(8,128)(2,1)S(1)} %copy-done.5, bf16[128,128]{1,0:T(8,128)(2,1)S(1)} %get-tuple-element.29.refs_1_.refs_2_, bf16[1280,128]{1,0:T(8,128)(2,1)S(1)} %get-tuple-element.30.refs_2_, bf16[640,128]{1,0:T(8,128)(2,1)S(1)} %add.54.refs_3_, ...), custom_call_target="tpu_custom_call" | custom-call | flops 671088640 | bytes 262144 | tf_op jit(solution)/shard_map/weigh/pallas_call | solution.py:323
  92.6 1.6 %mix_far.1 = bf16[128,4096]{1,0:T(8,128)(2,1)} custom-call(bf16[1024,1280]{1,0:T(8,128)(2,1)S(1)} %get-tuple-element.37.refs_0_, f32[1024,128]{1,0:T(8,128)S(1)} %get-tuple-element.38.refs_1_, bf16[128,128]{1,0:T(8,128)(2,1)S(1)} %get-tuple-element.29.refs_1_.refs_2_, bf16[640,128]{1,0:T(8,128)(2,1)S(1)} %add.61.refs_3_, ...), custom_call_target="tpu_custom_call" | custom-call | flops 335544320 | bytes 1048576 | tf_op jit(solution)/shard_map/mix_far/pallas_call | solution.py:380
  (77 shorter events, 13.2 us)
Async XLA Ops:
  2.8 11.0 %collective-permute-start = (f32[512,128]{1,0:T(8,128)S(1)}, f32[512,128]{1,0:T(8,128)S(1)}, u32[]{:S(2)}, u32[]{:S(2)}) collective-permute-start(f32[512,128]{1,0:T(8,128)S(1)} %get-tuple-element.33), channel_id=1, source_target_pairs={{0,1},{1,0},{2,3},{3,2},{4,5},{5,4},{6,7},{7,6},{8,9},{9,8},{10,11... | collective-permute-start | bytes 786440 | tf_op jit(solution)/shard_map/ppermute | solution.py:153
  11.7 9.2 %collective-permute-start.12 = (f32[512,128]{1,0:T(8,128)S(1)}, f32[512,128]{1,0:T(8,128)S(1)}, u32[]{:S(2)}, u32[]{:S(2)}) collective-permute-start(f32[512,128]{1,0:T(8,128)S(1)} %get-tuple-element.41), channel_id=1, source_target_pairs={{0,1},{1,0},{2,3},{3,2},{4,5},{5,4},{6,7},{7,6},{8,9},{9,8},{10,11... | collective-permute-start | bytes 786440 | tf_op jit(solution)/shard_map/ppermute | solution.py:153
  11.8 14.8 %collective-permute-start.3 = (f32[512,128]{1,0:T(8,128)S(1)}, f32[512,128]{1,0:T(8,128)S(1)}, u32[]{:S(2)}, u32[]{:S(2)}) collective-permute-start(f32[512,128]{1,0:T(8,128)S(1)} %get-tuple-element.34), channel_id=1, source_target_pairs={{0,1},{1,0},{2,3},{3,2},{4,5},{5,4},{6,7},{7,6},{8,9},{9,8},{10,11... | collective-permute-start | bytes 786440 | tf_op jit(solution)/shard_map/ppermute | solution.py:153
  13.8 13.5 %collective-permute-start.1 = (f32[512,128]{1,0:T(8,128)S(1)}, f32[512,128]{1,0:T(8,128)S(1)}, u32[]{:S(2)}, u32[]{:S(2)}) collective-permute-start(f32[512,128]{1,0:T(8,128)S(1)} %add.48), channel_id=1, source_target_pairs={{1,2},{2,1},{5,6},{6,5},{9,10},{10,9},{13,14},{14,13},{17,18},{18,... | collective-permute-start | bytes 786440 | tf_op jit(solution)/shard_map/ppermute | solution.py:153
  14.5 17.4 %collective-permute-start.15 = (f32[512,128]{1,0:T(8,128)S(1)}, f32[512,128]{1,0:T(8,128)S(1)}, u32[]{:S(2)}, u32[]{:S(2)}) collective-permute-start(f32[512,128]{1,0:T(8,128)S(1)} %get-tuple-element.42), channel_id=1, source_target_pairs={{0,1},{1,0},{2,3},{3,2},{4,5},{5,4},{6,7},{7,6},{8,9},{9,8},{10,11... | collective-permute-start | bytes 786440 | tf_op jit(solution)/shard_map/ppermute | solution.py:153
  21.0 11.7 %collective-permute-start.13 = (f32[512,128]{1,0:T(8,128)S(1)}, f32[512,128]{1,0:T(8,128)S(1)}, u32[]{:S(2)}, u32[]{:S(2)}) collective-permute-start(f32[512,128]{1,0:T(8,128)S(1)} %add.55), channel_id=1, source_target_pairs={{1,2},{2,1},{5,6},{6,5},{9,10},{10,9},{13,14},{14,13},{17,18},{18,... | collective-permute-start | bytes 786440 | tf_op jit(solution)/shard_map/ppermute | solution.py:153
  26.6 10.8 %collective-permute-start.4 = (f32[512,128]{1,0:T(8,128)S(1)}, f32[512,128]{1,0:T(8,128)S(1)}, u32[]{:S(2)}, u32[]{:S(2)}) collective-permute-start(f32[512,128]{1,0:T(8,128)S(1)} %add.50), channel_id=1, source_target_pairs={{1,2},{2,1},{5,6},{6,5},{9,10},{10,9},{13,14},{14,13},{17,18},{18,... | collective-permute-start | bytes 786440 | tf_op jit(solution)/shard_map/ppermute | solution.py:153
  27.3 10.2 %collective-permute-start.2 = (f32[512,128]{1,0:T(8,128)S(1)}, f32[512,128]{1,0:T(8,128)S(1)}, u32[]{:S(2)}, u32[]{:S(2)}) collective-permute-start(f32[512,128]{1,0:T(8,128)S(1)} %add.49), channel_id=1, source_target_pairs={{0,1},{1,0},{2,3},{3,2},{4,5},{5,4},{6,7},{7,6},{8,9},{9,8},{10,11... | collective-permute-start | bytes 786440 | tf_op jit(solution)/shard_map/ppermute | solution.py:153
  31.9 6.8 %collective-permute-start.16 = (f32[512,128]{1,0:T(8,128)S(1)}, f32[512,128]{1,0:T(8,128)S(1)}, u32[]{:S(2)}, u32[]{:S(2)}) collective-permute-start(f32[512,128]{1,0:T(8,128)S(1)} %add.57), channel_id=1, source_target_pairs={{1,2},{2,1},{5,6},{6,5},{9,10},{10,9},{13,14},{14,13},{17,18},{18,... | collective-permute-start | bytes 786440 | tf_op jit(solution)/shard_map/ppermute | solution.py:153
  32.7 9.3 %collective-permute-start.14 = (f32[512,128]{1,0:T(8,128)S(1)}, f32[512,128]{1,0:T(8,128)S(1)}, u32[]{:S(2)}, u32[]{:S(2)}) collective-permute-start(f32[512,128]{1,0:T(8,128)S(1)} %add.56), channel_id=1, source_target_pairs={{0,1},{1,0},{2,3},{3,2},{4,5},{5,4},{6,7},{7,6},{8,9},{9,8},{10,11... | collective-permute-start | bytes 786440 | tf_op jit(solution)/shard_map/ppermute | solution.py:153
  43.2 5.4 %collective-permute-start.6 = (bf16[640,128]{1,0:T(8,128)(2,1)S(1)}, bf16[640,128]{1,0:T(8,128)(2,1)S(1)}, u32[]{:S(2)}, u32[]{:S(2)}) collective-permute-start(bf16[640,128]{1,0:T(8,128)(2,1)S(1)} %add.51), channel_id=1, source_target_pairs={{0,8},{4,20},{8,0},{12,28},{16,24},{20,4},{24,16},{28,12},{1,9},{5... | collective-permute-start | bytes 491528 | tf_op jit(solution)/shard_map/ppermute | solution.py:425
  44.8 5.5 %collective-permute-start.18 = (bf16[640,128]{1,0:T(8,128)(2,1)S(1)}, bf16[640,128]{1,0:T(8,128)(2,1)S(1)}, u32[]{:S(2)}, u32[]{:S(2)}) collective-permute-start(bf16[640,128]{1,0:T(8,128)(2,1)S(1)} %add.58), channel_id=1, source_target_pairs={{0,8},{4,20},{8,0},{12,28},{16,24},{20,4},{24,16},{28,12},{1,9},{5... | collective-permute-start | bytes 491528 | tf_op jit(solution)/shard_map/ppermute | solution.py:425
  48.6 5.4 %collective-permute-start.7 = (bf16[640,128]{1,0:T(8,128)(2,1)S(1)}, bf16[640,128]{1,0:T(8,128)(2,1)S(1)}, u32[]{:S(2)}, u32[]{:S(2)}) collective-permute-start(bf16[640,128]{1,0:T(8,128)(2,1)S(1)} %add.52), channel_id=1, source_target_pairs={{0,16},{4,12},{8,24},{12,4},{16,0},{20,28},{24,8},{28,20},{1,17},{... | collective-permute-start | bytes 491528 | tf_op jit(solution)/shard_map/ppermute | solution.py:425
  50.4 5.5 %collective-permute-start.19 = (bf16[640,128]{1,0:T(8,128)(2,1)S(1)}, bf16[640,128]{1,0:T(8,128)(2,1)S(1)}, u32[]{:S(2)}, u32[]{:S(2)}) collective-permute-start(bf16[640,128]{1,0:T(8,128)(2,1)S(1)} %add.59), channel_id=1, source_target_pairs={{0,16},{4,12},{8,24},{12,4},{16,0},{20,28},{24,8},{28,20},{1,17},{... | collective-permute-start | bytes 491528 | tf_op jit(solution)/shard_map/ppermute | solution.py:425
  54.1 6.8 %collective-permute-start.8 = (bf16[640,128]{1,0:T(8,128)(2,1)S(1)}, bf16[640,128]{1,0:T(8,128)(2,1)S(1)}, u32[]{:S(2)}, u32[]{:S(2)}) collective-permute-start(bf16[640,128]{1,0:T(8,128)(2,1)S(1)} %add.53.refs_3_), channel_id=1, source_target_pairs={{0,1},{1,0},{2,3},{3,2},{4,5},{5,4},{6,7},{7,6},{8,9},{9,8},{10,11... | collective-permute-start | bytes 491528 | tf_op jit(solution)/shard_map/ppermute | solution.py:452
  56.0 6.6 %collective-permute-start.20 = (bf16[640,128]{1,0:T(8,128)(2,1)S(1)}, bf16[640,128]{1,0:T(8,128)(2,1)S(1)}, u32[]{:S(2)}, u32[]{:S(2)}) collective-permute-start(bf16[640,128]{1,0:T(8,128)(2,1)S(1)} %add.60.refs_5_), channel_id=1, source_target_pairs={{0,1},{1,0},{2,3},{3,2},{4,5},{5,4},{6,7},{7,6},{8,9},{9,8},{10,11... | collective-permute-start | bytes 491528 | tf_op jit(solution)/shard_map/ppermute | solution.py:452
  57.7 5.6 %collective-permute-start.28 = (bf16[640,128]{1,0:T(8,128)(2,1)S(1)}, bf16[640,128]{1,0:T(8,128)(2,1)S(1)}, u32[]{:S(2)}, u32[]{:S(2)}) collective-permute-start(bf16[640,128]{1,0:T(8,128)(2,1)S(1)} %add.53.refs_3_), channel_id=1, source_target_pairs={{1,2},{2,1},{5,6},{6,5},{9,10},{10,9},{13,14},{14,13},{17,18},{18,... | collective-permute-start | bytes 491528 | tf_op jit(solution)/shard_map/ppermute | solution.py:452
  58.3 6.2 %collective-permute-start.31 = (bf16[640,128]{1,0:T(8,128)(2,1)S(1)}, bf16[640,128]{1,0:T(8,128)(2,1)S(1)}, u32[]{:S(2)}, u32[]{:S(2)}) collective-permute-start(bf16[640,128]{1,0:T(8,128)(2,1)S(1)} %add.60.refs_5_), channel_id=1, source_target_pairs={{1,2},{2,1},{5,6},{6,5},{9,10},{10,9},{13,14},{14,13},{17,18},{18,... | collective-permute-start | bytes 491528 | tf_op jit(solution)/shard_map/ppermute | solution.py:452
  59.0 6.8 %collective-permute-start.24 = (bf16[640,128]{1,0:T(8,128)(2,1)S(1)}, bf16[640,128]{1,0:T(8,128)(2,1)S(1)}, u32[]{:S(2)}, u32[]{:S(2)}) collective-permute-start(bf16[640,128]{1,0:T(8,128)(2,1)S(1)} %add.53.refs_3_), channel_id=1, source_target_pairs={{0,4},{4,0},{8,12},{12,8},{16,20},{20,16},{24,28},{28,24},{1,5},{5... | collective-permute-start | bytes 491528 | tf_op jit(solution)/shard_map/ppermute | solution.py:32
  60.8 5.1 %collective-permute-start.9 = (bf16[640,128]{1,0:T(8,128)(2,1)S(1)}, bf16[640,128]{1,0:T(8,128)(2,1)S(1)}, u32[]{:S(2)}, u32[]{:S(2)}) collective-permute-start(bf16[640,128]{1,0:T(8,128)(2,1)S(1)} %collective-permute-done.8.refs_3_), channel_id=1, source_target_pairs={{1,2},{2,1},{5,6},{6,5},{9,10},{10,9},{13,14},{14,13},{17,18},{18,... | collective-permute-start | bytes 491528 | tf_op jit(solution)/shard_map/ppermute | solution.py:452
  62.6 4.7 %collective-permute-start.21 = (bf16[640,128]{1,0:T(8,128)(2,1)S(1)}, bf16[640,128]{1,0:T(8,128)(2,1)S(1)}, u32[]{:S(2)}, u32[]{:S(2)}) collective-permute-start(bf16[640,128]{1,0:T(8,128)(2,1)S(1)} %collective-permute-done.20.refs_5_), channel_id=1, source_target_pairs={{1,2},{2,1},{5,6},{6,5},{9,10},{10,9},{13,14},{14,13},{17,18},{18,... | collective-permute-start | bytes 491528 | tf_op jit(solution)/shard_map/ppermute | solution.py:452
  63.2 13.0 %collective-permute-start.29 = (bf16[640,128]{1,0:T(8,128)(2,1)S(1)}, bf16[640,128]{1,0:T(8,128)(2,1)S(1)}, u32[]{:S(2)}, u32[]{:S(2)}) collective-permute-start(bf16[640,128]{1,0:T(8,128)(2,1)S(1)} %collective-permute-done.28), channel_id=1, source_target_pairs={{1,0},{2,3},{5,4},{6,7},{9,8},{10,11},{13,12},{14,15},{17,16},{18,... | collective-permute-start | bytes 491528 | tf_op jit(solution)/shard_map/ppermute | solution.py:452
  64.6 15.2 %collective-permute-start.32 = (bf16[640,128]{1,0:T(8,128)(2,1)S(1)}, bf16[640,128]{1,0:T(8,128)(2,1)S(1)}, u32[]{:S(2)}, u32[]{:S(2)}) collective-permute-start(bf16[640,128]{1,0:T(8,128)(2,1)S(1)} %collective-permute-done.31), channel_id=1, source_target_pairs={{1,0},{2,3},{5,4},{6,7},{9,8},{10,11},{13,12},{14,15},{17,16},{18,... | collective-permute-start | bytes 491528 | tf_op jit(solution)/shard_map/ppermute | solution.py:452
  65.9 14.0 %collective-permute-start.25 = (bf16[640,128]{1,0:T(8,128)(2,1)S(1)}, bf16[640,128]{1,0:T(8,128)(2,1)S(1)}, u32[]{:S(2)}, u32[]{:S(2)}) collective-permute-start(bf16[640,128]{1,0:T(8,128)(2,1)S(1)} %add.60.refs_5_), channel_id=1, source_target_pairs={{0,4},{4,0},{8,12},{12,8},{16,20},{20,16},{24,28},{28,24},{1,5},{5... | collective-permute-start | bytes 491528 | tf_op jit(solution)/shard_map/ppermute | solution.py:32
  66.0 17.3 %collective-permute-start.10 = (bf16[640,128]{1,0:T(8,128)(2,1)S(1)}, bf16[640,128]{1,0:T(8,128)(2,1)S(1)}, u32[]{:S(2)}, u32[]{:S(2)}) collective-permute-start(bf16[640,128]{1,0:T(8,128)(2,1)S(1)} %collective-permute-done.9), channel_id=1, source_target_pairs={{1,0},{2,3},{5,4},{6,7},{9,8},{10,11},{13,12},{14,15},{17,16},{18,... | collective-permute-start | bytes 491528 | tf_op jit(solution)/shard_map/ppermute | solution.py:452
  67.3 18.7 %collective-permute-start.22 = (bf16[640,128]{1,0:T(8,128)(2,1)S(1)}, bf16[640,128]{1,0:T(8,128)(2,1)S(1)}, u32[]{:S(2)}, u32[]{:S(2)}) collective-permute-start(bf16[640,128]{1,0:T(8,128)(2,1)S(1)} %collective-permute-done.21), channel_id=1, source_target_pairs={{1,0},{2,3},{5,4},{6,7},{9,8},{10,11},{13,12},{14,15},{17,16},{18,... | collective-permute-start | bytes 491528 | tf_op jit(solution)/shard_map/ppermute | solution.py:452
  76.2 9.8 %collective-permute-start.26 = (bf16[640,128]{1,0:T(8,128)(2,1)S(1)}, bf16[640,128]{1,0:T(8,128)(2,1)S(1)}, u32[]{:S(2)}, u32[]{:S(2)}) collective-permute-start(bf16[640,128]{1,0:T(8,128)(2,1)S(1)} %collective-permute-done.8.refs_3_), channel_id=1, source_target_pairs={{0,4},{4,0},{8,12},{12,8},{16,20},{20,16},{24,28},{28,24},{1,5},{5... | collective-permute-start | bytes 491528 | tf_op jit(solution)/shard_map/ppermute | solution.py:32
  79.7 6.9 %collective-permute-start.27 = (bf16[640,128]{1,0:T(8,128)(2,1)S(1)}, bf16[640,128]{1,0:T(8,128)(2,1)S(1)}, u32[]{:S(2)}, u32[]{:S(2)}) collective-permute-start(bf16[640,128]{1,0:T(8,128)(2,1)S(1)} %collective-permute-done.20.refs_5_), channel_id=1, source_target_pairs={{0,4},{4,0},{8,12},{12,8},{16,20},{20,16},{24,28},{28,24},{1,5},{5... | collective-permute-start | bytes 491528 | tf_op jit(solution)/shard_map/ppermute | solution.py:32
  79.8 8.9 %collective-permute-start.30 = (bf16[640,128]{1,0:T(8,128)(2,1)S(1)}, bf16[640,128]{1,0:T(8,128)(2,1)S(1)}, u32[]{:S(2)}, u32[]{:S(2)}) collective-permute-start(bf16[640,128]{1,0:T(8,128)(2,1)S(1)} %add.62.refs_3_), channel_id=1, source_target_pairs={{0,4},{4,0},{8,12},{12,8},{16,20},{20,16},{24,28},{28,24},{1,5},{5... | collective-permute-start | bytes 491528 | tf_op jit(solution)/shard_map/ppermute | solution.py:32
  83.2 5.5 %collective-permute-start.33 = (bf16[640,128]{1,0:T(8,128)(2,1)S(1)}, bf16[640,128]{1,0:T(8,128)(2,1)S(1)}, u32[]{:S(2)}, u32[]{:S(2)}) collective-permute-start(bf16[640,128]{1,0:T(8,128)(2,1)S(1)} %add.63.refs_5_), channel_id=1, source_target_pairs={{0,4},{4,0},{8,12},{12,8},{16,20},{20,16},{24,28},{28,24},{1,5},{5... | collective-permute-start | bytes 491528 | tf_op jit(solution)/shard_map/ppermute | solution.py:32
  86.0 4.9 %collective-permute-start.11 = (bf16[640,128]{1,0:T(8,128)(2,1)S(1)}, bf16[640,128]{1,0:T(8,128)(2,1)S(1)}, u32[]{:S(2)}, u32[]{:S(2)}) collective-permute-start(bf16[640,128]{1,0:T(8,128)(2,1)S(1)} %add.54.refs_3_), channel_id=1, source_target_pairs={{0,4},{4,0},{8,12},{12,8},{16,20},{20,16},{24,28},{28,24},{1,5},{5... | collective-permute-start | bytes 491528 | tf_op jit(solution)/shard_map/ppermute | solution.py:32
  86.1 6.5 %collective-permute-start.23 = (bf16[640,128]{1,0:T(8,128)(2,1)S(1)}, bf16[640,128]{1,0:T(8,128)(2,1)S(1)}, u32[]{:S(2)}, u32[]{:S(2)}) collective-permute-start(bf16[640,128]{1,0:T(8,128)(2,1)S(1)} %add.61.refs_3_), channel_id=1, source_target_pairs={{0,4},{4,0},{8,12},{12,8},{16,20},{20,16},{24,28},{28,24},{1,5},{5... | collective-permute-start | bytes 491528 | tf_op jit(solution)/shard_map/ppermute | solution.py:32
  (9 other events, 125.3 us)

commit v6 on v5

--- a/solution.py
+++ b/solution.py
@@ -137,6 +137,59 @@
     return [[parts[0][piece], to_right[piece], to_left[piece]] for piece in range(2)], early
 
 
+def swap_middle(value):
+    pairs = []
+    for c in range(lax.axis_size("ctx")):
+        pairs += [((c, 1), (c, 2)), ((c, 2), (c, 1)), ((c, 0), (c ^ 1, 0)), ((c, 3), (c ^ 1, 3))]
+    pairs = [tuple(c * 4 + h for c, h in pair) for pair in pairs]
+    return lax.ppermute(value, ("ctx", "head"), pairs)
+
+
+def in_middle():
+    here = lax.axis_index("head")
+    return (here == 1) | (here == 2)
+
+
+def add_in_middle(left, right):
+    def kernel(left_ref, right_ref, out_ref):
+        @pl.when(in_middle())
+        def _():
+            out_ref[...] = left_ref[...] + right_ref[...]
+
+        @pl.when(jnp.logical_not(in_middle()))
+        def _():
+            out_ref[...] = left_ref[...]
+
+    return pl.pallas_call(
+        kernel,
+        in_specs=[VMEM] * 2,
+        out_specs=VMEM,
+        out_shape=jax.ShapeDtypeStruct(left.shape, left.dtype),
+        compiler_params=params(4),
+        name="add_in_middle",
+    )(left, right)
+
+
+def pick_by_place(middle, end):
+    def kernel(middle_ref, end_ref, out_ref):
+        @pl.when(in_middle())
+        def _():
+            out_ref[...] = middle_ref[...]
+
+        @pl.when(jnp.logical_not(in_middle()))
+        def _():
+            out_ref[...] = end_ref[...]
+
+    return pl.pallas_call(
+        kernel,
+        in_specs=[VMEM] * 2,
+        out_specs=VMEM,
+        out_shape=jax.ShapeDtypeStruct(middle.shape, middle.dtype),
+        compiler_params=params(4),
+        name="pick_by_place",
+    )(middle, end)
+
+
 def swap_sums(vis_feats, kv_weight, pair, early):
     def first(here, n):
         return jnp.where(here < 2, 3, 0)
@@ -150,7 +203,7 @@
     far, own, early = (far[0], held[0]), (held[1], own[1]), held[2:]
 
     def swap(value, pairs):
-        return lax.ppermute(value, "head", pairs)
+        return swap_middle(value) if pairs is MIDDLE else lax.ppermute(value, "head", pairs)
 
     def add(left, right):
         return left + right
@@ -161,18 +214,21 @@
         for_near = swap(near[piece], EDGES)
         for_far = swap(add(far[piece], for_far), MIDDLE)
         for_near = swap(add(near[piece], for_near), MIDDLE)
-        final = swap(add(last[piece], for_far), EDGES)
+        for_far = add_in_middle(last[piece], for_far)
+        final = swap(for_far, EDGES)
         sums.append([own[piece], final, for_near])
     return sums, early
 
 
-def finish_chunk(partial_sums, key_gain, image_tokens, image_owner, per_kv, are_keys):
+def finish_chunk(partial_sums, key_gain, image_tokens, image_owner, per_kv, are_keys, by_swaps):
     rows, head_dim = partial_sums[0].shape
     half = KV_TOTAL // 2
     images = image_owner.shape[0]
 
     def kernel(tokens_ref, owner_ref, own_ref, left_ref, right_ref, gain_ref, mine_ref, other_ref):
-        data = own_ref[...] + left_ref[...] + right_ref[...]
+        data = own_ref[...] + left_ref[...]
+        last = right_ref[...]
+        data = data + (jnp.where(in_middle(), last, 0.0) if by_swaps else last)
         if are_keys:
             mean = jnp.mean(data * data, axis=-1, keepdims=True)
             data = data * lax.rsqrt(mean + EPSILON) * gain_ref[...]
@@ -412,7 +468,7 @@
 
     def spread(piece):
         block, other = finish_chunk(
-            partial_sums[piece], key_gain, image_tokens, image_owner, per_kv, piece == 0
+            partial_sums[piece], key_gain, image_tokens, image_owner, per_kv, piece == 0, head_count == 4
         )
         if per_kv > 1:
             groups = [[k * per_kv + j for j in range(per_kv)] for k in range(kv_heads)]
@@ -449,13 +505,13 @@
     for block in (keys, values):
 
         def swap(value, pairs):
-            return lax.ppermute(value, "head", pairs)
+            return swap_middle(value) if pairs is MIDDLE else lax.ppermute(value, "head", pairs)
 
         near = swap(block, EDGES)
         inner = swap(block, MIDDLE)
         outer = swap(near, MIDDLE)
-        inner = inner + swap(inner, OUTWARD)
-        outer = outer + swap(outer, OUTWARD)
+        inner = pick_by_place(inner, swap(inner, OUTWARD))
+        outer = pick_by_place(outer, swap(outer, OUTWARD))
         for n, half in enumerate((block, near, inner, outer)):
             held[n].append(join(half))
     heads_of = [

time: 94.8 us -> 90.3 us (0.953)
  starting transfers between devices: 40.7 us -> 30 us
  waiting for transfers between devices: 32.1 us -> 38.5 us
    ppermute x20, starting transfers between devices: 33.2 us -> 22.1 us  [the longest x12 21.3 us: swap(): lax.ppermute(value, 'head', pairs)]
    ppermute x20, waiting for transfers between devices: 27.4 us -> 32.5 us  [the longest x12 32.5 us: swap(): lax.ppermute(value, 'head', pairs)]
    ppermute x4, waiting for transfers between devices: 4.61 us -> 5.95 us  [spread(): block = block + lax.ppermute(block, 'ctx', pairs)]
  transfers between devices with their start and end apart: 34 -> 34, of which waited for: 14 -> 15; matrix products, arithmetic and copies ran while one was open for 1% -> 1% of each run, Pallas kernels for 14% -> 15%
where the time goes in v6:
time: 90.3 us; the launch traced here: 90.1 us
  waiting for transfers between devices  38.5 us (43%)
  starting transfers between devices  30 us (33%)
  Pallas kernels  18.3 us (20%)
  local copies, waits for them, and re-layouts  2.35 us (3%)
    ppermute x12, waiting for transfers between devices, swap(): lax.ppermute(value, 'head', pairs)  32.5 us
    ppermute x12, starting transfers between devices, swap(): lax.ppermute(value, 'head', pairs)  21.3 us
    pallas_call x4, Pallas kernels, attend(): pl.pallas_call(kernel, in_specs=[VMEM] * len(operands), out_specs=[VMEM]...  8.03 us
    ppermute x4, starting transfers between devices, spread(): block = block + lax.ppermute(block, 'ctx', pairs)  6.04 us
    ppermute x4, waiting for transfers between devices, spread(): block = block + lax.ppermute(block, 'ctx', pairs)  5.95 us
    pallas_call x2, Pallas kernels, project(): pl.pallas_call(kernel, in_specs=[HBM, HBM] if alone else [VMEM, VMEM], ou...  4.59 us
    unnamed x15, local copies, waits for them, and re-layouts  2.35 us
    pallas_call x2, Pallas kernels, finish_chunk(): pl.pallas_call(kernel, in_specs=[SMEM] * 2 + [VMEM] * 4, out_specs=[VMEM]...  2.22 us
  transfers between devices with their start and end apart: 34, of which 15 were waited for; matrix products, arithmetic and copies ran while one was open for 1% of the time, Pallas kernels for 15%

profile of v6, /device:TPU:0, one launch (start us, length us, event | category | flops | bytes accessed | tf_op | source)
XLA Modules:
  0.0 90.1 jit_solution(9026104793134377183)
XLA Ops:
  0.0 2.8 %project.2 = (f32[512,128]{1,0:T(8,128)S(1)}, f32[512,128]{1,0:T(8,128)S(1)}) custom-call(bf16[512,2048]{1,0:T(8,128)(2,1)} %feats_ref.3, bf16[2048,1024]{1,0:T(8,128)(2,1)} %weight_ref.3), custom_call_target="tpu_custom_call" | custom-call | flops 536870912 | bytes 3145728 | tf_op jit(solution)/shard_map/project/pallas_call | solution.py:83
  2.8 3.1 %collective-permute-start = (f32[512,128]{1,0:T(8,128)S(1)}, f32[512,128]{1,0:T(8,128)S(1)}, u32[]{:S(2)}, u32[]{:S(2)}) collective-permute-start(f32[512,128]{1,0:T(8,128)S(1)} %get-tuple-element.33), channel_id=1, source_target_pairs={{0,1},{1,0},{2,3},{3,2},{4,5},{5,4},{6,7},{7,6},{8,9},{9,8},{10,11... | collective-permute-start | bytes 786440 | tf_op jit(solution)/shard_map/ppermute | solution.py:206
  6.1 1.6 %masks.1 = (bf16[128,128]{1,0:T(8,128)(2,1)S(1)}, bf16[1280,128]{1,0:T(8,128)(2,1)S(1)}) custom-call(s32[4]{0:T(128)S(1)} %copy-done.2, s32[512,4]{1,0:T(8,128)S(1)} %copy.8.cross_ref), custom_call_target="tpu_custom_call" | custom-call | tf_op jit(solution)/shard_map/masks/pallas_call | solution.py:287
  7.6 2.2 %copy-done = bf16[2048,1024]{1,0:T(8,128)(2,1)S(1)} copy-done((bf16[2048,1024]{1,0:T(8,128)(2,1)S(1)}, bf16[2048,1024]{1,0:T(8,128)(2,1)}, u32[]{:S(2)}) %copy-start) | copy-done | bytes 4194328
  9.8 1.8 %project.3 = (f32[512,128]{1,0:T(8,128)S(1)}, f32[512,128]{1,0:T(8,128)S(1)}, f32[512,128]{1,0:T(8,128)S(1)}, f32[512,128]{1,0:T(8,128)S(1)}, f32[512,128]{1,0:T(8,128)S(1)}, /*index=5*/f32[512,128]{1,0:T(8,128)S(1)}) custom-call(bf16[512,2048]{1,0:T(8,128)(2,1)S(1)} %copy-done.1, bf16[2048,1024]{1,0:T(8,128)(2,1)S(1)} %copy-done), custom_call_target="tpu_custom_call" | custom-call | flops 1610612736 | bytes 5242880 | tf_op jit(solution)/shard_map/project/pallas_call | solution.py:83
  11.8 2.0 %collective-permute-start.3 = (f32[512,128]{1,0:T(8,128)S(1)}, f32[512,128]{1,0:T(8,128)S(1)}, u32[]{:S(2)}, u32[]{:S(2)}) collective-permute-start(f32[512,128]{1,0:T(8,128)S(1)} %get-tuple-element.34), channel_id=1, source_target_pairs={{0,1},{1,0},{2,3},{3,2},{4,5},{5,4},{6,7},{7,6},{8,9},{9,8},{10,11... | collective-permute-start | bytes 786440 | tf_op jit(solution)/shard_map/ppermute | solution.py:206
  13.9 3.2 %collective-permute-start.15 = (f32[512,128]{1,0:T(8,128)S(1)}, f32[512,128]{1,0:T(8,128)S(1)}, u32[]{:S(2)}, u32[]{:S(2)}) collective-permute-start(f32[512,128]{1,0:T(8,128)S(1)} %get-tuple-element.42), channel_id=1, source_target_pairs={{0,1},{1,0},{2,3},{3,2},{4,5},{5,4},{6,7},{7,6},{8,9},{9,8},{10,11... | collective-permute-start | bytes 786440 | tf_op jit(solution)/shard_map/ppermute | solution.py:206
  17.1 3.9 %collective-permute-done.12 = f32[512,128]{1,0:T(8,128)S(1)} collective-permute-done((f32[512,128]{1,0:T(8,128)S(1)}, f32[512,128]{1,0:T(8,128)S(1)}, u32[]{:S(2)}, u32[]{:S(2)}) %collective-permute-start.12) | collective-permute-done | bytes 262176 | tf_op jit(solution)/shard_map/ppermute | solution.py:206
  21.0 5.5 %collective-permute-done.3 = f32[512,128]{1,0:T(8,128)S(1)} collective-permute-done((f32[512,128]{1,0:T(8,128)S(1)}, f32[512,128]{1,0:T(8,128)S(1)}, u32[]{:S(2)}, u32[]{:S(2)}) %collective-permute-start.3) | collective-permute-done | bytes 262176 | tf_op jit(solution)/shard_map/ppermute | solution.py:206
  26.7 3.2 %collective-permute-start.2 = (f32[512,128]{1,0:T(8,128)S(1)}, f32[512,128]{1,0:T(8,128)S(1)}, u32[]{:S(2)}, u32[]{:S(2)}) collective-permute-start(f32[512,128]{1,0:T(8,128)S(1)} %add_in_middle.2), channel_id=1, source_target_pairs={{0,1},{1,0},{2,3},{3,2},{4,5},{5,4},{6,7},{7,6},{8,9},{9,8},{10,11... | collective-permute-start | bytes 786440 | tf_op jit(solution)/shard_map/ppermute | solution.py:206
  29.9 1.7 %collective-permute-done.15 = f32[512,128]{1,0:T(8,128)S(1)} collective-permute-done((f32[512,128]{1,0:T(8,128)S(1)}, f32[512,128]{1,0:T(8,128)S(1)}, u32[]{:S(2)}, u32[]{:S(2)}) %collective-permute-start.15) | collective-permute-done | bytes 262176 | tf_op jit(solution)/shard_map/ppermute | solution.py:206
  31.8 3.7 %collective-permute-start.14 = (f32[512,128]{1,0:T(8,128)S(1)}, f32[512,128]{1,0:T(8,128)S(1)}, u32[]{:S(2)}, u32[]{:S(2)}) collective-permute-start(f32[512,128]{1,0:T(8,128)S(1)} %add_in_middle.3), channel_id=1, source_target_pairs={{0,1},{1,0},{2,3},{3,2},{4,5},{5,4},{6,7},{7,6},{8,9},{9,8},{10,11... | collective-permute-start | bytes 786440 | tf_op jit(solution)/shard_map/ppermute | solution.py:206
  35.5 1.7 %collective-permute-done.2.left_ref = f32[512,128]{1,0:T(8,128)S(1)} collective-permute-done((f32[512,128]{1,0:T(8,128)S(1)}, f32[512,128]{1,0:T(8,128)S(1)}, u32[]{:S(2)}, u32[]{:S(2)}) %collective-permute-start.2) | collective-permute-done | bytes 262176 | tf_op jit(solution)/shard_map/ppermute | solution.py:206
  38.5 3.4 %collective-permute-done.14.left_ref = f32[512,128]{1,0:T(8,128)S(1)} collective-permute-done((f32[512,128]{1,0:T(8,128)S(1)}, f32[512,128]{1,0:T(8,128)S(1)}, u32[]{:S(2)}, u32[]{:S(2)}) %collective-permute-start.14) | collective-permute-done | bytes 262176 | tf_op jit(solution)/shard_map/ppermute | solution.py:206
  43.2 1.6 %collective-permute-start.6 = (bf16[640,128]{1,0:T(8,128)(2,1)S(1)}, bf16[640,128]{1,0:T(8,128)(2,1)S(1)}, u32[]{:S(2)}, u32[]{:S(2)}) collective-permute-start(bf16[640,128]{1,0:T(8,128)(2,1)S(1)} %add.32), channel_id=1, source_target_pairs={{0,8},{4,20},{8,0},{12,28},{16,24},{20,4},{24,16},{28,12},{1,9},{5... | collective-permute-start | bytes 491528 | tf_op jit(solution)/shard_map/ppermute | solution.py:481
  44.8 1.3 %collective-permute-start.18 = (bf16[640,128]{1,0:T(8,128)(2,1)S(1)}, bf16[640,128]{1,0:T(8,128)(2,1)S(1)}, u32[]{:S(2)}, u32[]{:S(2)}) collective-permute-start(bf16[640,128]{1,0:T(8,128)(2,1)S(1)} %add.37), channel_id=1, source_target_pairs={{0,8},{4,20},{8,0},{12,28},{16,24},{20,4},{24,16},{28,12},{1,9},{5... | collective-permute-start | bytes 491528 | tf_op jit(solution)/shard_map/ppermute | solution.py:481
  46.1 2.5 %collective-permute-done.6 = bf16[640,128]{1,0:T(8,128)(2,1)S(1)} collective-permute-done((bf16[640,128]{1,0:T(8,128)(2,1)S(1)}, bf16[640,128]{1,0:T(8,128)(2,1)S(1)}, u32[]{:S(2)}, u32[]{:S(2)}) %collective-permute-start.6) | collective-permute-done | bytes 163872 | tf_op jit(solution)/shard_map/ppermute | solution.py:481
  48.6 1.6 %collective-permute-start.7 = (bf16[640,128]{1,0:T(8,128)(2,1)S(1)}, bf16[640,128]{1,0:T(8,128)(2,1)S(1)}, u32[]{:S(2)}, u32[]{:S(2)}) collective-permute-start(bf16[640,128]{1,0:T(8,128)(2,1)S(1)} %add.33), channel_id=1, source_target_pairs={{0,16},{4,12},{8,24},{12,4},{16,0},{20,28},{24,8},{28,20},{1,17},{... | collective-permute-start | bytes 491528 | tf_op jit(solution)/shard_map/ppermute | solution.py:481
  50.4 1.6 %collective-permute-start.19 = (bf16[640,128]{1,0:T(8,128)(2,1)S(1)}, bf16[640,128]{1,0:T(8,128)(2,1)S(1)}, u32[]{:S(2)}, u32[]{:S(2)}) collective-permute-start(bf16[640,128]{1,0:T(8,128)(2,1)S(1)} %add.38), channel_id=1, source_target_pairs={{0,16},{4,12},{8,24},{12,4},{16,0},{20,28},{24,8},{28,20},{1,17},{... | collective-permute-start | bytes 491528 | tf_op jit(solution)/shard_map/ppermute | solution.py:481
  52.0 2.0 %collective-permute-done.7 = bf16[640,128]{1,0:T(8,128)(2,1)S(1)} collective-permute-done((bf16[640,128]{1,0:T(8,128)(2,1)S(1)}, bf16[640,128]{1,0:T(8,128)(2,1)S(1)}, u32[]{:S(2)}, u32[]{:S(2)}) %collective-permute-start.7) | collective-permute-done | bytes 163872 | tf_op jit(solution)/shard_map/ppermute | solution.py:481
  54.4 1.3 %collective-permute-done.19 = bf16[640,128]{1,0:T(8,128)(2,1)S(1)} collective-permute-done((bf16[640,128]{1,0:T(8,128)(2,1)S(1)}, bf16[640,128]{1,0:T(8,128)(2,1)S(1)}, u32[]{:S(2)}, u32[]{:S(2)}) %collective-permute-start.19) | collective-permute-done | bytes 163872 | tf_op jit(solution)/shard_map/ppermute | solution.py:481
  56.8 4.0 %collective-permute-done.8.refs_3_ = bf16[640,128]{1,0:T(8,128)(2,1)S(1)} collective-permute-done((bf16[640,128]{1,0:T(8,128)(2,1)S(1)}, bf16[640,128]{1,0:T(8,128)(2,1)S(1)}, u32[]{:S(2)}, u32[]{:S(2)}) %collective-permute-start.8) | collective-permute-done | bytes 163872 | tf_op jit(solution)/shard_map/ppermute | solution.py:508
  60.8 1.8 %collective-permute-done.20.refs_5_ = bf16[640,128]{1,0:T(8,128)(2,1)S(1)} collective-permute-done((bf16[640,128]{1,0:T(8,128)(2,1)S(1)}, bf16[640,128]{1,0:T(8,128)(2,1)S(1)}, u32[]{:S(2)}, u32[]{:S(2)}) %collective-permute-start.20) | collective-permute-done | bytes 163872 | tf_op jit(solution)/shard_map/ppermute | solution.py:508
  63.8 1.3 %collective-permute-start.32 = (bf16[640,128]{1,0:T(8,128)(2,1)S(1)}, bf16[640,128]{1,0:T(8,128)(2,1)S(1)}, u32[]{:S(2)}, u32[]{:S(2)}) collective-permute-start(bf16[640,128]{1,0:T(8,128)(2,1)S(1)} %collective-permute-done.31.middle_ref), channel_id=1, source_target_pairs={{1,0},{2,3},{5,4},{6,7},{9,8},{10,11},{13,12},{14,15},{17,16},{18,... | collective-permute-start | bytes 491528 | tf_op jit(solution)/shard_map/ppermute | solution.py:508
  68.3 3.7 %collective-permute-done.29.end_ref = bf16[640,128]{1,0:T(8,128)(2,1)S(1)} collective-permute-done((bf16[640,128]{1,0:T(8,128)(2,1)S(1)}, bf16[640,128]{1,0:T(8,128)(2,1)S(1)}, u32[]{:S(2)}, u32[]{:S(2)}) %collective-permute-start.29) | collective-permute-done | bytes 163872 | tf_op jit(solution)/shard_map/ppermute | solution.py:508
  72.0 3.5 %collective-permute-done.32.end_ref = bf16[640,128]{1,0:T(8,128)(2,1)S(1)} collective-permute-done((bf16[640,128]{1,0:T(8,128)(2,1)S(1)}, bf16[640,128]{1,0:T(8,128)(2,1)S(1)}, u32[]{:S(2)}, u32[]{:S(2)}) %collective-permute-start.32) | collective-permute-done | bytes 163872 | tf_op jit(solution)/shard_map/ppermute | solution.py:508
  76.2 2.9 %collective-permute-done.10.end_ref = bf16[640,128]{1,0:T(8,128)(2,1)S(1)} collective-permute-done((bf16[640,128]{1,0:T(8,128)(2,1)S(1)}, bf16[640,128]{1,0:T(8,128)(2,1)S(1)}, u32[]{:S(2)}, u32[]{:S(2)}) %collective-permute-start.10) | collective-permute-done | bytes 163872 | tf_op jit(solution)/shard_map/ppermute | solution.py:508
  79.0 2.1 %attend.3.refs_5_ = bf16[128,1024]{1,0:T(8,128)(2,1)S(1)} custom-call(bf16[128,4096]{1,0:T(8,128)(2,1)S(1)} %copy-done.5, bf16[128,128]{1,0:T(8,128)(2,1)S(1)} %get-tuple-element.29.refs_1_.refs_2_, bf16[1280,128]{1,0:T(8,128)(2,1)S(1)} %get-tuple-element.30.refs_2_, bf16[640,128]{1,0:T(8,128)(2,1)S(1)} %add.34.refs_3_, ...), custom_call_target="tpu_custom_call" | custom-call | flops 1006632960 | bytes 262144 | tf_op jit(solution)/shard_map/attend/pallas_call | solution.py:379
  82.3 2.1 %attend.4.refs_6_ = bf16[128,1024]{1,0:T(8,128)(2,1)S(1)} custom-call(bf16[128,4096]{1,0:T(8,128)(2,1)S(1)} %copy-done.5, bf16[128,128]{1,0:T(8,128)(2,1)S(1)} %get-tuple-element.29.refs_1_.refs_2_, bf16[1280,128]{1,0:T(8,128)(2,1)S(1)} %get-tuple-element.30.refs_2_, bf16[640,128]{1,0:T(8,128)(2,1)S(1)} %collective-permute-done.8.refs_3_, ...), custom_call_target="tpu_custom_call" | custom-call | flops 1006632960 | bytes 262144 | tf_op jit(solution)/shard_map/attend/pallas_call | solution.py:379
  84.5 2.1 %attend.5.refs_7_ = bf16[128,1024]{1,0:T(8,128)(2,1)S(1)} custom-call(bf16[128,4096]{1,0:T(8,128)(2,1)S(1)} %copy-done.5, bf16[128,128]{1,0:T(8,128)(2,1)S(1)} %get-tuple-element.29.refs_1_.refs_2_, bf16[1280,128]{1,0:T(8,128)(2,1)S(1)} %get-tuple-element.30.refs_2_, bf16[640,128]{1,0:T(8,128)(2,1)S(1)} %pick_by_place.6.refs_3_, ...), custom_call_target="tpu_custom_call" | custom-call | flops 1006632960 | bytes 262144 | tf_op jit(solution)/shard_map/attend/pallas_call | solution.py:379
  86.6 1.7 %weigh.1 = (bf16[1024,1280]{1,0:T(8,128)(2,1)S(1)}, f32[1024,128]{1,0:T(8,128)S(1)}) custom-call(bf16[128,4096]{1,0:T(8,128)(2,1)S(1)} %copy-done.5, bf16[128,128]{1,0:T(8,128)(2,1)S(1)} %get-tuple-element.29.refs_1_.refs_2_, bf16[1280,128]{1,0:T(8,128)(2,1)S(1)} %get-tuple-element.30.refs_2_, bf16[640,128]{1,0:T(8,128)(2,1)S(1)} %pick_by_place.4.refs_3_, ...), custom_call_target="tpu_custom_call" | custom-call | flops 671088640 | bytes 262144 | tf_op jit(solution)/shard_map/weigh/pallas_call | solution.py:379
  88.3 1.6 %mix_far.1 = bf16[128,4096]{1,0:T(8,128)(2,1)} custom-call(bf16[1024,1280]{1,0:T(8,128)(2,1)S(1)} %get-tuple-element.37.refs_0_, f32[1024,128]{1,0:T(8,128)S(1)} %get-tuple-element.38.refs_1_, bf16[128,128]{1,0:T(8,128)(2,1)S(1)} %get-tuple-element.29.refs_1_.refs_2_, bf16[640,128]{1,0:T(8,128)(2,1)S(1)} %pick_by_place.5.refs_3_, ...), custom_call_target="tpu_custom_call" | custom-call | flops 335544320 | bytes 1048576 | tf_op jit(solution)/shard_map/mix_far/pallas_call | solution.py:436
  (77 shorter events, 11.1 us)
Async XLA Ops:
  2.8 11.0 %collective-permute-start = (f32[512,128]{1,0:T(8,128)S(1)}, f32[512,128]{1,0:T(8,128)S(1)}, u32[]{:S(2)}, u32[]{:S(2)}) collective-permute-start(f32[512,128]{1,0:T(8,128)S(1)} %get-tuple-element.33), channel_id=1, source_target_pairs={{0,1},{1,0},{2,3},{3,2},{4,5},{5,4},{6,7},{7,6},{8,9},{9,8},{10,11... | collective-permute-start | bytes 786440 | tf_op jit(solution)/shard_map/ppermute | solution.py:206
  11.7 9.2 %collective-permute-start.12 = (f32[512,128]{1,0:T(8,128)S(1)}, f32[512,128]{1,0:T(8,128)S(1)}, u32[]{:S(2)}, u32[]{:S(2)}) collective-permute-start(f32[512,128]{1,0:T(8,128)S(1)} %get-tuple-element.41), channel_id=1, source_target_pairs={{0,1},{1,0},{2,3},{3,2},{4,5},{5,4},{6,7},{7,6},{8,9},{9,8},{10,11... | collective-permute-start | bytes 786440 | tf_op jit(solution)/shard_map/ppermute | solution.py:206
  11.8 14.8 %collective-permute-start.3 = (f32[512,128]{1,0:T(8,128)S(1)}, f32[512,128]{1,0:T(8,128)S(1)}, u32[]{:S(2)}, u32[]{:S(2)}) collective-permute-start(f32[512,128]{1,0:T(8,128)S(1)} %get-tuple-element.34), channel_id=1, source_target_pairs={{0,1},{1,0},{2,3},{3,2},{4,5},{5,4},{6,7},{7,6},{8,9},{9,8},{10,11... | collective-permute-start | bytes 786440 | tf_op jit(solution)/shard_map/ppermute | solution.py:206
  13.8 12.8 %collective-permute-start.1 = (f32[512,128]{1,0:T(8,128)S(1)}, f32[512,128]{1,0:T(8,128)S(1)}, u32[]{:S(2)}, u32[]{:S(2)}) collective-permute-start(f32[512,128]{1,0:T(8,128)S(1)} %add.30), channel_id=1, source_target_pairs={{1,2},{2,1},{0,4},{3,7},{5,6},{6,5},{4,0},{7,3},{9,10},{10,9},{8,1... | collective-permute-start | bytes 786440 | tf_op jit(solution)/shard_map/ppermute | solution.py:145
  13.9 17.8 %collective-permute-start.15 = (f32[512,128]{1,0:T(8,128)S(1)}, f32[512,128]{1,0:T(8,128)S(1)}, u32[]{:S(2)}, u32[]{:S(2)}) collective-permute-start(f32[512,128]{1,0:T(8,128)S(1)} %get-tuple-element.42), channel_id=1, source_target_pairs={{0,1},{1,0},{2,3},{3,2},{4,5},{5,4},{6,7},{7,6},{8,9},{9,8},{10,11... | collective-permute-start | bytes 786440 | tf_op jit(solution)/shard_map/ppermute | solution.py:206
  21.0 10.8 %collective-permute-start.13 = (f32[512,128]{1,0:T(8,128)S(1)}, f32[512,128]{1,0:T(8,128)S(1)}, u32[]{:S(2)}, u32[]{:S(2)}) collective-permute-start(f32[512,128]{1,0:T(8,128)S(1)} %add.35), channel_id=1, source_target_pairs={{1,2},{2,1},{0,4},{3,7},{5,6},{6,5},{4,0},{7,3},{9,10},{10,9},{8,1... | collective-permute-start | bytes 786440 | tf_op jit(solution)/shard_map/ppermute | solution.py:145
  26.6 9.0 %collective-permute-start.4 = (f32[512,128]{1,0:T(8,128)S(1)}, f32[512,128]{1,0:T(8,128)S(1)}, u32[]{:S(2)}, u32[]{:S(2)}) collective-permute-start(f32[512,128]{1,0:T(8,128)S(1)} %add.31), channel_id=1, source_target_pairs={{1,2},{2,1},{0,4},{3,7},{5,6},{6,5},{4,0},{7,3},{9,10},{10,9},{8,1... | collective-permute-start | bytes 786440 | tf_op jit(solution)/shard_map/ppermute | solution.py:145
  26.7 10.6 %collective-permute-start.2 = (f32[512,128]{1,0:T(8,128)S(1)}, f32[512,128]{1,0:T(8,128)S(1)}, u32[]{:S(2)}, u32[]{:S(2)}) collective-permute-start(f32[512,128]{1,0:T(8,128)S(1)} %add_in_middle.2), channel_id=1, source_target_pairs={{0,1},{1,0},{2,3},{3,2},{4,5},{5,4},{6,7},{7,6},{8,9},{9,8},{10,11... | collective-permute-start | bytes 786440 | tf_op jit(solution)/shard_map/ppermute | solution.py:206
  31.7 6.8 %collective-permute-start.16 = (f32[512,128]{1,0:T(8,128)S(1)}, f32[512,128]{1,0:T(8,128)S(1)}, u32[]{:S(2)}, u32[]{:S(2)}) collective-permute-start(f32[512,128]{1,0:T(8,128)S(1)} %add.36), channel_id=1, source_target_pairs={{1,2},{2,1},{0,4},{3,7},{5,6},{6,5},{4,0},{7,3},{9,10},{10,9},{8,1... | collective-permute-start | bytes 786440 | tf_op jit(solution)/shard_map/ppermute | solution.py:145
  31.8 10.2 %collective-permute-start.14 = (f32[512,128]{1,0:T(8,128)S(1)}, f32[512,128]{1,0:T(8,128)S(1)}, u32[]{:S(2)}, u32[]{:S(2)}) collective-permute-start(f32[512,128]{1,0:T(8,128)S(1)} %add_in_middle.3), channel_id=1, source_target_pairs={{0,1},{1,0},{2,3},{3,2},{4,5},{5,4},{6,7},{7,6},{8,9},{9,8},{10,11... | collective-permute-start | bytes 786440 | tf_op jit(solution)/shard_map/ppermute | solution.py:206
  38.5 4.7 %collective-permute-start.5 = (bf16[640,128]{1,0:T(8,128)(2,1)S(1)}, bf16[640,128]{1,0:T(8,128)(2,1)S(1)}, u32[]{:S(2)}, u32[]{:S(2)}) collective-permute-start(bf16[640,128]{1,0:T(8,128)(2,1)S(1)} %get-tuple-element.36), channel_id=1, source_target_pairs={{0,4},{4,0},{8,12},{12,8},{16,20},{20,16},{24,28},{28,24},{1,5},{5... | collective-permute-start | bytes 491528 | tf_op jit(solution)/shard_map/ppermute | solution.py:32
  43.2 5.4 %collective-permute-start.6 = (bf16[640,128]{1,0:T(8,128)(2,1)S(1)}, bf16[640,128]{1,0:T(8,128)(2,1)S(1)}, u32[]{:S(2)}, u32[]{:S(2)}) collective-permute-start(bf16[640,128]{1,0:T(8,128)(2,1)S(1)} %add.32), channel_id=1, source_target_pairs={{0,8},{4,20},{8,0},{12,28},{16,24},{20,4},{24,16},{28,12},{1,9},{5... | collective-permute-start | bytes 491528 | tf_op jit(solution)/shard_map/ppermute | solution.py:481
  44.8 5.5 %collective-permute-start.18 = (bf16[640,128]{1,0:T(8,128)(2,1)S(1)}, bf16[640,128]{1,0:T(8,128)(2,1)S(1)}, u32[]{:S(2)}, u32[]{:S(2)}) collective-permute-start(bf16[640,128]{1,0:T(8,128)(2,1)S(1)} %add.37), channel_id=1, source_target_pairs={{0,8},{4,20},{8,0},{12,28},{16,24},{20,4},{24,16},{28,12},{1,9},{5... | collective-permute-start | bytes 491528 | tf_op jit(solution)/shard_map/ppermute | solution.py:481
  48.6 5.4 %collective-permute-start.7 = (bf16[640,128]{1,0:T(8,128)(2,1)S(1)}, bf16[640,128]{1,0:T(8,128)(2,1)S(1)}, u32[]{:S(2)}, u32[]{:S(2)}) collective-permute-start(bf16[640,128]{1,0:T(8,128)(2,1)S(1)} %add.33), channel_id=1, source_target_pairs={{0,16},{4,12},{8,24},{12,4},{16,0},{20,28},{24,8},{28,20},{1,17},{... | collective-permute-start | bytes 491528 | tf_op jit(solution)/shard_map/ppermute | solution.py:481
  50.4 5.4 %collective-permute-start.19 = (bf16[640,128]{1,0:T(8,128)(2,1)S(1)}, bf16[640,128]{1,0:T(8,128)(2,1)S(1)}, u32[]{:S(2)}, u32[]{:S(2)}) collective-permute-start(bf16[640,128]{1,0:T(8,128)(2,1)S(1)} %add.38), channel_id=1, source_target_pairs={{0,16},{4,12},{8,24},{12,4},{16,0},{20,28},{24,8},{28,20},{1,17},{... | collective-permute-start | bytes 491528 | tf_op jit(solution)/shard_map/ppermute | solution.py:481
  54.1 6.7 %collective-permute-start.8 = (bf16[640,128]{1,0:T(8,128)(2,1)S(1)}, bf16[640,128]{1,0:T(8,128)(2,1)S(1)}, u32[]{:S(2)}, u32[]{:S(2)}) collective-permute-start(bf16[640,128]{1,0:T(8,128)(2,1)S(1)} %add.34.refs_3_), channel_id=1, source_target_pairs={{0,1},{1,0},{2,3},{3,2},{4,5},{5,4},{6,7},{7,6},{8,9},{9,8},{10,11... | collective-permute-start | bytes 491528 | tf_op jit(solution)/shard_map/ppermute | solution.py:508
  55.8 6.7 %collective-permute-start.20 = (bf16[640,128]{1,0:T(8,128)(2,1)S(1)}, bf16[640,128]{1,0:T(8,128)(2,1)S(1)}, u32[]{:S(2)}, u32[]{:S(2)}) collective-permute-start(bf16[640,128]{1,0:T(8,128)(2,1)S(1)} %add.39.refs_5_), channel_id=1, source_target_pairs={{0,1},{1,0},{2,3},{3,2},{4,5},{5,4},{6,7},{7,6},{8,9},{9,8},{10,11... | collective-permute-start | bytes 491528 | tf_op jit(solution)/shard_map/ppermute | solution.py:508
  56.3 6.3 %collective-permute-start.28 = (bf16[640,128]{1,0:T(8,128)(2,1)S(1)}, bf16[640,128]{1,0:T(8,128)(2,1)S(1)}, u32[]{:S(2)}, u32[]{:S(2)}) collective-permute-start(bf16[640,128]{1,0:T(8,128)(2,1)S(1)} %add.34.refs_3_), channel_id=1, source_target_pairs={{1,2},{2,1},{0,4},{3,7},{5,6},{6,5},{4,0},{7,3},{9,10},{10,9},{8,1... | collective-permute-start | bytes 491528 | tf_op jit(solution)/shard_map/ppermute | solution.py:145
  56.3 7.5 %collective-permute-start.31 = (bf16[640,128]{1,0:T(8,128)(2,1)S(1)}, bf16[640,128]{1,0:T(8,128)(2,1)S(1)}, u32[]{:S(2)}, u32[]{:S(2)}) collective-permute-start(bf16[640,128]{1,0:T(8,128)(2,1)S(1)} %add.39.refs_5_), channel_id=1, source_target_pairs={{1,2},{2,1},{0,4},{3,7},{5,6},{6,5},{4,0},{7,3},{9,10},{10,9},{8,1... | collective-permute-start | bytes 491528 | tf_op jit(solution)/shard_map/ppermute | solution.py:145
  56.8 8.3 %collective-permute-start.24 = (bf16[640,128]{1,0:T(8,128)(2,1)S(1)}, bf16[640,128]{1,0:T(8,128)(2,1)S(1)}, u32[]{:S(2)}, u32[]{:S(2)}) collective-permute-start(bf16[640,128]{1,0:T(8,128)(2,1)S(1)} %add.34.refs_3_), channel_id=1, source_target_pairs={{0,4},{4,0},{8,12},{12,8},{16,20},{20,16},{24,28},{28,24},{1,5},{5... | collective-permute-start | bytes 491528 | tf_op jit(solution)/shard_map/ppermute | solution.py:32
  60.8 4.9 %collective-permute-start.9 = (bf16[640,128]{1,0:T(8,128)(2,1)S(1)}, bf16[640,128]{1,0:T(8,128)(2,1)S(1)}, u32[]{:S(2)}, u32[]{:S(2)}) collective-permute-start(bf16[640,128]{1,0:T(8,128)(2,1)S(1)} %collective-permute-done.8.refs_3_), channel_id=1, source_target_pairs={{1,2},{2,1},{0,4},{3,7},{5,6},{6,5},{4,0},{7,3},{9,10},{10,9},{8,1... | collective-permute-start | bytes 491528 | tf_op jit(solution)/shard_map/ppermute | solution.py:145
  62.5 9.5 %collective-permute-start.29 = (bf16[640,128]{1,0:T(8,128)(2,1)S(1)}, bf16[640,128]{1,0:T(8,128)(2,1)S(1)}, u32[]{:S(2)}, u32[]{:S(2)}) collective-permute-start(bf16[640,128]{1,0:T(8,128)(2,1)S(1)} %collective-permute-done.28.middle_ref), channel_id=1, source_target_pairs={{1,0},{2,3},{5,4},{6,7},{9,8},{10,11},{13,12},{14,15},{17,16},{18,... | collective-permute-start | bytes 491528 | tf_op jit(solution)/shard_map/ppermute | solution.py:508
  63.8 11.7 %collective-permute-start.32 = (bf16[640,128]{1,0:T(8,128)(2,1)S(1)}, bf16[640,128]{1,0:T(8,128)(2,1)S(1)}, u32[]{:S(2)}, u32[]{:S(2)}) collective-permute-start(bf16[640,128]{1,0:T(8,128)(2,1)S(1)} %collective-permute-done.31.middle_ref), channel_id=1, source_target_pairs={{1,0},{2,3},{5,4},{6,7},{9,8},{10,11},{13,12},{14,15},{17,16},{18,... | collective-permute-start | bytes 491528 | tf_op jit(solution)/shard_map/ppermute | solution.py:508
  65.1 10.4 %collective-permute-start.25 = (bf16[640,128]{1,0:T(8,128)(2,1)S(1)}, bf16[640,128]{1,0:T(8,128)(2,1)S(1)}, u32[]{:S(2)}, u32[]{:S(2)}) collective-permute-start(bf16[640,128]{1,0:T(8,128)(2,1)S(1)} %add.39.refs_5_), channel_id=1, source_target_pairs={{0,4},{4,0},{8,12},{12,8},{16,20},{20,16},{24,28},{28,24},{1,5},{5... | collective-permute-start | bytes 491528 | tf_op jit(solution)/shard_map/ppermute | solution.py:32
  65.7 13.3 %collective-permute-start.10 = (bf16[640,128]{1,0:T(8,128)(2,1)S(1)}, bf16[640,128]{1,0:T(8,128)(2,1)S(1)}, u32[]{:S(2)}, u32[]{:S(2)}) collective-permute-start(bf16[640,128]{1,0:T(8,128)(2,1)S(1)} %collective-permute-done.9.middle_ref), channel_id=1, source_target_pairs={{1,0},{2,3},{5,4},{6,7},{9,8},{10,11},{13,12},{14,15},{17,16},{18,... | collective-permute-start | bytes 491528 | tf_op jit(solution)/shard_map/ppermute | solution.py:508
  67.0 14.5 %collective-permute-start.22 = (bf16[640,128]{1,0:T(8,128)(2,1)S(1)}, bf16[640,128]{1,0:T(8,128)(2,1)S(1)}, u32[]{:S(2)}, u32[]{:S(2)}) collective-permute-start(bf16[640,128]{1,0:T(8,128)(2,1)S(1)} %collective-permute-done.21.middle_ref), channel_id=1, source_target_pairs={{1,0},{2,3},{5,4},{6,7},{9,8},{10,11},{13,12},{14,15},{17,16},{18,... | collective-permute-start | bytes 491528 | tf_op jit(solution)/shard_map/ppermute | solution.py:508
  72.0 10.0 %collective-permute-start.26 = (bf16[640,128]{1,0:T(8,128)(2,1)S(1)}, bf16[640,128]{1,0:T(8,128)(2,1)S(1)}, u32[]{:S(2)}, u32[]{:S(2)}) collective-permute-start(bf16[640,128]{1,0:T(8,128)(2,1)S(1)} %collective-permute-done.8.refs_3_), channel_id=1, source_target_pairs={{0,4},{4,0},{8,12},{12,8},{16,20},{20,16},{24,28},{28,24},{1,5},{5... | collective-permute-start | bytes 491528 | tf_op jit(solution)/shard_map/ppermute | solution.py:32
  75.5 6.8 %collective-permute-start.27 = (bf16[640,128]{1,0:T(8,128)(2,1)S(1)}, bf16[640,128]{1,0:T(8,128)(2,1)S(1)}, u32[]{:S(2)}, u32[]{:S(2)}) collective-permute-start(bf16[640,128]{1,0:T(8,128)(2,1)S(1)} %collective-permute-done.20.refs_5_), channel_id=1, source_target_pairs={{0,4},{4,0},{8,12},{12,8},{16,20},{20,16},{24,28},{28,24},{1,5},{5... | collective-permute-start | bytes 491528 | tf_op jit(solution)/shard_map/ppermute | solution.py:32
  75.6 8.9 %collective-permute-start.30 = (bf16[640,128]{1,0:T(8,128)(2,1)S(1)}, bf16[640,128]{1,0:T(8,128)(2,1)S(1)}, u32[]{:S(2)}, u32[]{:S(2)}) collective-permute-start(bf16[640,128]{1,0:T(8,128)(2,1)S(1)} %pick_by_place.6.refs_3_), channel_id=1, source_target_pairs={{0,4},{4,0},{8,12},{12,8},{16,20},{20,16},{24,28},{28,24},{1,5},{5... | collective-permute-start | bytes 491528 | tf_op jit(solution)/shard_map/ppermute | solution.py:32
  79.0 5.5 %collective-permute-start.33 = (bf16[640,128]{1,0:T(8,128)(2,1)S(1)}, bf16[640,128]{1,0:T(8,128)(2,1)S(1)}, u32[]{:S(2)}, u32[]{:S(2)}) collective-permute-start(bf16[640,128]{1,0:T(8,128)(2,1)S(1)} %pick_by_place.7.refs_5_), channel_id=1, source_target_pairs={{0,4},{4,0},{8,12},{12,8},{16,20},{20,16},{24,28},{28,24},{1,5},{5... | collective-permute-start | bytes 491528 | tf_op jit(solution)/shard_map/ppermute | solution.py:32
  81.6 5.1 %collective-permute-start.11 = (bf16[640,128]{1,0:T(8,128)(2,1)S(1)}, bf16[640,128]{1,0:T(8,128)(2,1)S(1)}, u32[]{:S(2)}, u32[]{:S(2)}) collective-permute-start(bf16[640,128]{1,0:T(8,128)(2,1)S(1)} %pick_by_place.4.refs_3_), channel_id=1, source_target_pairs={{0,4},{4,0},{8,12},{12,8},{16,20},{20,16},{24,28},{28,24},{1,5},{5... | collective-permute-start | bytes 491528 | tf_op jit(solution)/shard_map/ppermute | solution.py:32
  82.0 6.3 %collective-permute-start.23 = (bf16[640,128]{1,0:T(8,128)(2,1)S(1)}, bf16[640,128]{1,0:T(8,128)(2,1)S(1)}, u32[]{:S(2)}, u32[]{:S(2)}) collective-permute-start(bf16[640,128]{1,0:T(8,128)(2,1)S(1)} %pick_by_place.5.refs_3_), channel_id=1, source_target_pairs={{0,4},{4,0},{8,12},{12,8},{16,20},{20,16},{24,28},{28,24},{1,5},{5... | collective-permute-start | bytes 491528 | tf_op jit(solution)/shard_map/ppermute | solution.py:32
  (9 other events, 120.9 us)

commit v7 on v6

--- a/solution.py
+++ b/solution.py
@@ -199,8 +199,8 @@
 
     far = project(first, 1, vis_feats, kv_weight, pair)[0]
     near, last, own = project(later, 3, vis_feats, kv_weight, pair)
-    held = lax.optimization_barrier((far[1], own[0], *early))
-    far, own, early = (far[0], held[0]), (held[1], own[1]), held[2:]
+    held = lax.optimization_barrier((far[1], own[0]))
+    far, own = (far[0], held[0]), (held[1], own[1])
 
     def swap(value, pairs):
         return swap_middle(value) if pairs is MIDDLE else lax.ppermute(value, "head", pairs)
@@ -212,6 +212,9 @@
     for piece in range(2):
         for_far = swap(far[piece], EDGES)
         for_near = swap(near[piece], EDGES)
+        if piece == 1:
+            held = lax.optimization_barrier((for_near, *early))
+            for_near, early = held[0], held[1:]
         for_far = swap(add(far[piece], for_far), MIDDLE)
         for_near = swap(add(near[piece], for_near), MIDDLE)
         for_far = add_in_middle(last[piece], for_far)

time: 90.3 us -> 91.5 us (1.013)
  starting transfers between devices: 30 us -> 33.8 us
  waiting for transfers between devices: 38.5 us -> 37.1 us
  local copies, waits for them, and re-layouts: 2.35 us -> 1.22 us
    ppermute x12, starting transfers between devices: 21.3 us -> 24.7 us  [swap(): lax.ppermute(value, 'head', pairs)]
    ppermute x4, waiting for transfers between devices: 5.95 us -> 4.17 us  [spread(): block = block + lax.ppermute(block, 'ctx', pairs)]
    unnamed x15, local copies, waits for them, and re-layouts: 2.35 us -> 1.22 us
  transfers between devices with their start and end apart: 34 -> 34, of which waited for: 15 -> 14; matrix products, arithmetic and copies ran while one was open for 1% -> 1% of each run, Pallas kernels for 15% -> 13%
where the time goes in v7:
time: 91.5 us; the launch traced here: 91.3 us
  waiting for transfers between devices  37.1 us (41%)
  starting transfers between devices  33.8 us (37%)
  Pallas kernels  18.3 us (20%)
  local copies, waits for them, and re-layouts  1.22 us (1%)
    ppermute x12, waiting for transfers between devices, swap(): lax.ppermute(value, 'head', pairs)  32.9 us
    ppermute x12, starting transfers between devices, swap(): lax.ppermute(value, 'head', pairs)  24.7 us
    pallas_call x4, Pallas kernels, attend(): pl.pallas_call(kernel, in_specs=[VMEM] * len(operands), out_specs=[VMEM]...  7.98 us
    ppermute x4, starting transfers between devices, spread(): block = block + lax.ppermute(block, 'ctx', pairs)  6.49 us
    pallas_call x2, Pallas kernels, project(): pl.pallas_call(kernel, in_specs=[HBM, HBM] if alone else [VMEM, VMEM], ou...  4.59 us
    ppermute x4, waiting for transfers between devices, spread(): block = block + lax.ppermute(block, 'ctx', pairs)  4.17 us
    pallas_call x2, Pallas kernels, finish_chunk(): pl.pallas_call(kernel, in_specs=[SMEM] * 2 + [VMEM] * 4, out_specs=[VMEM]...  2.22 us
    ppermute x10, starting transfers between devices, swapped(): return lax.ppermute(value, axis, pairs)  1.87 us
  transfers between devices with their start and end apart: 34, of which 14 were waited for; matrix products, arithmetic and copies ran while one was open for 1% of the time, Pallas kernels for 13%

profile of v7, /device:TPU:0, one launch (start us, length us, event | category | flops | bytes accessed | tf_op | source)
XLA Modules:
  0.0 91.3 jit_solution(10831562538006064130)
XLA Ops:
  0.0 2.8 %project.3 = (f32[512,128]{1,0:T(8,128)S(1)}, f32[512,128]{1,0:T(8,128)S(1)}) custom-call(bf16[512,2048]{1,0:T(8,128)(2,1)} %feats_ref.3, bf16[2048,1024]{1,0:T(8,128)(2,1)} %weight_ref.3), custom_call_target="tpu_custom_call" | custom-call | flops 536870912 | bytes 3145728 | tf_op jit(solution)/shard_map/project/pallas_call | solution.py:83
  3.8 1.8 %project.2 = (f32[512,128]{1,0:T(8,128)S(1)}, f32[512,128]{1,0:T(8,128)S(1)}, f32[512,128]{1,0:T(8,128)S(1)}, f32[512,128]{1,0:T(8,128)S(1)}, f32[512,128]{1,0:T(8,128)S(1)}, /*index=5*/f32[512,128]{1,0:T(8,128)S(1)}) custom-call(bf16[512,2048]{1,0:T(8,128)(2,1)S(1)} %copy-done.1, bf16[2048,1024]{1,0:T(8,128)(2,1)S(1)} %copy-done), custom_call_target="tpu_custom_call" | custom-call | flops 1610612736 | bytes 5242880 | tf_op jit(solution)/shard_map/project/pallas_call | solution.py:83
  5.7 3.1 %collective-permute-start.13 = (f32[512,128]{1,0:T(8,128)S(1)}, f32[512,128]{1,0:T(8,128)S(1)}, u32[]{:S(2)}, u32[]{:S(2)}) collective-permute-start(f32[512,128]{1,0:T(8,128)S(1)} %get-tuple-element.43), channel_id=1, source_target_pairs={{0,1},{1,0},{2,3},{3,2},{4,5},{5,4},{6,7},{7,6},{8,9},{9,8},{10,11... | collective-permute-start | bytes 786440 | tf_op jit(solution)/shard_map/ppermute | solution.py:206
  8.9 1.9 %collective-permute-start = (f32[512,128]{1,0:T(8,128)S(1)}, f32[512,128]{1,0:T(8,128)S(1)}, u32[]{:S(2)}, u32[]{:S(2)}) collective-permute-start(f32[512,128]{1,0:T(8,128)S(1)} %get-tuple-element.26), channel_id=1, source_target_pairs={{0,1},{1,0},{2,3},{3,2},{4,5},{5,4},{6,7},{7,6},{8,9},{9,8},{10,11... | collective-permute-start | bytes 786440 | tf_op jit(solution)/shard_map/ppermute | solution.py:206
  10.8 5.1 %collective-permute-done.13 = f32[512,128]{1,0:T(8,128)S(1)} collective-permute-done((f32[512,128]{1,0:T(8,128)S(1)}, f32[512,128]{1,0:T(8,128)S(1)}, u32[]{:S(2)}, u32[]{:S(2)}) %collective-permute-start.13) | collective-permute-done | bytes 262176 | tf_op jit(solution)/shard_map/ppermute | solution.py:206
  16.1 3.6 %collective-permute-start.4 = (f32[512,128]{1,0:T(8,128)S(1)}, f32[512,128]{1,0:T(8,128)S(1)}, u32[]{:S(2)}, u32[]{:S(2)}) collective-permute-start(f32[512,128]{1,0:T(8,128)S(1)} %get-tuple-element.36), channel_id=1, source_target_pairs={{0,1},{1,0},{2,3},{3,2},{4,5},{5,4},{6,7},{7,6},{8,9},{9,8},{10,11... | collective-permute-start | bytes 786440 | tf_op jit(solution)/shard_map/ppermute | solution.py:206
  19.7 1.9 %collective-permute-done.1 = f32[512,128]{1,0:T(8,128)S(1)} collective-permute-done((f32[512,128]{1,0:T(8,128)S(1)}, f32[512,128]{1,0:T(8,128)S(1)}, u32[]{:S(2)}, u32[]{:S(2)}) %collective-permute-start.1) | collective-permute-done | bytes 262176 | tf_op jit(solution)/shard_map/ppermute | solution.py:206
  21.9 1.6 %masks.1 = (bf16[128,128]{1,0:T(8,128)(2,1)S(1)}, bf16[1280,128]{1,0:T(8,128)(2,1)S(1)}) custom-call(s32[4]{0:T(128)S(1)} %copy-done.2, s32[512,4]{1,0:T(8,128)S(1)} %copy.8.cross_ref), custom_call_target="tpu_custom_call" | custom-call | tf_op jit(solution)/shard_map/masks/pallas_call | solution.py:290
  23.4 3.8 %collective-permute-done = f32[512,128]{1,0:T(8,128)S(1)} collective-permute-done((f32[512,128]{1,0:T(8,128)S(1)}, f32[512,128]{1,0:T(8,128)S(1)}, u32[]{:S(2)}, u32[]{:S(2)}) %collective-permute-start) | collective-permute-done | bytes 262176 | tf_op jit(solution)/shard_map/ppermute | solution.py:206
  27.4 3.6 %collective-permute-start.15 = (f32[512,128]{1,0:T(8,128)S(1)}, f32[512,128]{1,0:T(8,128)S(1)}, u32[]{:S(2)}, u32[]{:S(2)}) collective-permute-start(f32[512,128]{1,0:T(8,128)S(1)} %add_in_middle.3), channel_id=1, source_target_pairs={{0,1},{1,0},{2,3},{3,2},{4,5},{5,4},{6,7},{7,6},{8,9},{9,8},{10,11... | collective-permute-start | bytes 786440 | tf_op jit(solution)/shard_map/ppermute | solution.py:206
  31.0 1.8 %collective-permute-done.4 = f32[512,128]{1,0:T(8,128)S(1)} collective-permute-done((f32[512,128]{1,0:T(8,128)S(1)}, f32[512,128]{1,0:T(8,128)S(1)}, u32[]{:S(2)}, u32[]{:S(2)}) %collective-permute-start.4) | collective-permute-done | bytes 262176 | tf_op jit(solution)/shard_map/ppermute | solution.py:206
  33.0 3.6 %collective-permute-start.3 = (f32[512,128]{1,0:T(8,128)S(1)}, f32[512,128]{1,0:T(8,128)S(1)}, u32[]{:S(2)}, u32[]{:S(2)}) collective-permute-start(f32[512,128]{1,0:T(8,128)S(1)} %add_in_middle.2), channel_id=1, source_target_pairs={{0,1},{1,0},{2,3},{3,2},{4,5},{5,4},{6,7},{7,6},{8,9},{9,8},{10,11... | collective-permute-start | bytes 786440 | tf_op jit(solution)/shard_map/ppermute | solution.py:206
  36.6 1.8 %collective-permute-done.15.left_ref = f32[512,128]{1,0:T(8,128)S(1)} collective-permute-done((f32[512,128]{1,0:T(8,128)S(1)}, f32[512,128]{1,0:T(8,128)S(1)}, u32[]{:S(2)}, u32[]{:S(2)}) %collective-permute-start.15) | collective-permute-done | bytes 262176 | tf_op jit(solution)/shard_map/ppermute | solution.py:206
  39.6 3.6 %collective-permute-done.3.left_ref = f32[512,128]{1,0:T(8,128)S(1)} collective-permute-done((f32[512,128]{1,0:T(8,128)S(1)}, f32[512,128]{1,0:T(8,128)S(1)}, u32[]{:S(2)}, u32[]{:S(2)}) %collective-permute-start.3) | collective-permute-done | bytes 262176 | tf_op jit(solution)/shard_map/ppermute | solution.py:206
  44.5 1.7 %collective-permute-start.18 = (bf16[640,128]{1,0:T(8,128)(2,1)S(1)}, bf16[640,128]{1,0:T(8,128)(2,1)S(1)}, u32[]{:S(2)}, u32[]{:S(2)}) collective-permute-start(bf16[640,128]{1,0:T(8,128)(2,1)S(1)} %add.37), channel_id=1, source_target_pairs={{0,8},{4,20},{8,0},{12,28},{16,24},{20,4},{24,16},{28,12},{1,9},{5... | collective-permute-start | bytes 491528 | tf_op jit(solution)/shard_map/ppermute | solution.py:484
  46.3 1.3 %collective-permute-start.7 = (bf16[640,128]{1,0:T(8,128)(2,1)S(1)}, bf16[640,128]{1,0:T(8,128)(2,1)S(1)}, u32[]{:S(2)}, u32[]{:S(2)}) collective-permute-start(bf16[640,128]{1,0:T(8,128)(2,1)S(1)} %add.32), channel_id=1, source_target_pairs={{0,8},{4,20},{8,0},{12,28},{16,24},{20,4},{24,16},{28,12},{1,9},{5... | collective-permute-start | bytes 491528 | tf_op jit(solution)/shard_map/ppermute | solution.py:484
  47.6 2.3 %collective-permute-done.18 = bf16[640,128]{1,0:T(8,128)(2,1)S(1)} collective-permute-done((bf16[640,128]{1,0:T(8,128)(2,1)S(1)}, bf16[640,128]{1,0:T(8,128)(2,1)S(1)}, u32[]{:S(2)}, u32[]{:S(2)}) %collective-permute-start.18) | collective-permute-done | bytes 163872 | tf_op jit(solution)/shard_map/ppermute | solution.py:484
  49.9 1.8 %collective-permute-start.19 = (bf16[640,128]{1,0:T(8,128)(2,1)S(1)}, bf16[640,128]{1,0:T(8,128)(2,1)S(1)}, u32[]{:S(2)}, u32[]{:S(2)}) collective-permute-start(bf16[640,128]{1,0:T(8,128)(2,1)S(1)} %add.38), channel_id=1, source_target_pairs={{0,16},{4,12},{8,24},{12,4},{16,0},{20,28},{24,8},{28,20},{1,17},{... | collective-permute-start | bytes 491528 | tf_op jit(solution)/shard_map/ppermute | solution.py:484
  51.7 1.7 %collective-permute-start.8 = (bf16[640,128]{1,0:T(8,128)(2,1)S(1)}, bf16[640,128]{1,0:T(8,128)(2,1)S(1)}, u32[]{:S(2)}, u32[]{:S(2)}) collective-permute-start(bf16[640,128]{1,0:T(8,128)(2,1)S(1)} %add.33), channel_id=1, source_target_pairs={{0,16},{4,12},{8,24},{12,4},{16,0},{20,28},{24,8},{28,20},{1,17},{... | collective-permute-start | bytes 491528 | tf_op jit(solution)/shard_map/ppermute | solution.py:484
  53.4 1.9 %collective-permute-done.19 = bf16[640,128]{1,0:T(8,128)(2,1)S(1)} collective-permute-done((bf16[640,128]{1,0:T(8,128)(2,1)S(1)}, bf16[640,128]{1,0:T(8,128)(2,1)S(1)}, u32[]{:S(2)}, u32[]{:S(2)}) %collective-permute-start.19) | collective-permute-done | bytes 163872 | tf_op jit(solution)/shard_map/ppermute | solution.py:484
  55.4 1.8 %collective-permute-start.20 = (bf16[640,128]{1,0:T(8,128)(2,1)S(1)}, bf16[640,128]{1,0:T(8,128)(2,1)S(1)}, u32[]{:S(2)}, u32[]{:S(2)}) collective-permute-start(bf16[640,128]{1,0:T(8,128)(2,1)S(1)} %add.39.refs_5_), channel_id=1, source_target_pairs={{0,1},{1,0},{2,3},{3,2},{4,5},{5,4},{6,7},{7,6},{8,9},{9,8},{10,11... | collective-permute-start | bytes 491528 | tf_op jit(solution)/shard_map/ppermute | solution.py:511
  57.2 1.7 %collective-permute-start.9 = (bf16[640,128]{1,0:T(8,128)(2,1)S(1)}, bf16[640,128]{1,0:T(8,128)(2,1)S(1)}, u32[]{:S(2)}, u32[]{:S(2)}) collective-permute-start(bf16[640,128]{1,0:T(8,128)(2,1)S(1)} %add.34.refs_3_), channel_id=1, source_target_pairs={{0,1},{1,0},{2,3},{3,2},{4,5},{5,4},{6,7},{7,6},{8,9},{9,8},{10,11... | collective-permute-start | bytes 491528 | tf_op jit(solution)/shard_map/ppermute | solution.py:511
  59.4 2.6 %collective-permute-done.20.refs_5_ = bf16[640,128]{1,0:T(8,128)(2,1)S(1)} collective-permute-done((bf16[640,128]{1,0:T(8,128)(2,1)S(1)}, bf16[640,128]{1,0:T(8,128)(2,1)S(1)}, u32[]{:S(2)}, u32[]{:S(2)}) %collective-permute-start.20) | collective-permute-done | bytes 163872 | tf_op jit(solution)/shard_map/ppermute | solution.py:511
  62.1 1.8 %collective-permute-done.9.refs_3_ = bf16[640,128]{1,0:T(8,128)(2,1)S(1)} collective-permute-done((bf16[640,128]{1,0:T(8,128)(2,1)S(1)}, bf16[640,128]{1,0:T(8,128)(2,1)S(1)}, u32[]{:S(2)}, u32[]{:S(2)}) %collective-permute-start.9) | collective-permute-done | bytes 163872 | tf_op jit(solution)/shard_map/ppermute | solution.py:511
  69.6 3.9 %collective-permute-done.32.end_ref = bf16[640,128]{1,0:T(8,128)(2,1)S(1)} collective-permute-done((bf16[640,128]{1,0:T(8,128)(2,1)S(1)}, bf16[640,128]{1,0:T(8,128)(2,1)S(1)}, u32[]{:S(2)}, u32[]{:S(2)}) %collective-permute-start.32) | collective-permute-done | bytes 163872 | tf_op jit(solution)/shard_map/ppermute | solution.py:511
  73.5 3.5 %collective-permute-done.29.end_ref = bf16[640,128]{1,0:T(8,128)(2,1)S(1)} collective-permute-done((bf16[640,128]{1,0:T(8,128)(2,1)S(1)}, bf16[640,128]{1,0:T(8,128)(2,1)S(1)}, u32[]{:S(2)}, u32[]{:S(2)}) %collective-permute-start.29) | collective-permute-done | bytes 163872 | tf_op jit(solution)/shard_map/ppermute | solution.py:511
  77.6 2.9 %collective-permute-done.22.end_ref = bf16[640,128]{1,0:T(8,128)(2,1)S(1)} collective-permute-done((bf16[640,128]{1,0:T(8,128)(2,1)S(1)}, bf16[640,128]{1,0:T(8,128)(2,1)S(1)}, u32[]{:S(2)}, u32[]{:S(2)}) %collective-permute-start.22) | collective-permute-done | bytes 163872 | tf_op jit(solution)/shard_map/ppermute | solution.py:511
  80.5 2.1 %attend.3.refs_5_ = bf16[128,1024]{1,0:T(8,128)(2,1)S(1)} custom-call(bf16[128,4096]{1,0:T(8,128)(2,1)S(1)} %copy-done.5, bf16[128,128]{1,0:T(8,128)(2,1)S(1)} %get-tuple-element.29.refs_1_.refs_2_, bf16[1280,128]{1,0:T(8,128)(2,1)S(1)} %get-tuple-element.30.refs_2_, bf16[640,128]{1,0:T(8,128)(2,1)S(1)} %add.34.refs_3_, ...), custom_call_target="tpu_custom_call" | custom-call | flops 1006632960 | bytes 262144 | tf_op jit(solution)/shard_map/attend/pallas_call | solution.py:382
  83.6 2.1 %attend.4.refs_6_ = bf16[128,1024]{1,0:T(8,128)(2,1)S(1)} custom-call(bf16[128,4096]{1,0:T(8,128)(2,1)S(1)} %copy-done.5, bf16[128,128]{1,0:T(8,128)(2,1)S(1)} %get-tuple-element.29.refs_1_.refs_2_, bf16[1280,128]{1,0:T(8,128)(2,1)S(1)} %get-tuple-element.30.refs_2_, bf16[640,128]{1,0:T(8,128)(2,1)S(1)} %collective-permute-done.9.refs_3_, ...), custom_call_target="tpu_custom_call" | custom-call | flops 1006632960 | bytes 262144 | tf_op jit(solution)/shard_map/attend/pallas_call | solution.py:382
  85.8 2.1 %attend.5.refs_7_ = bf16[128,1024]{1,0:T(8,128)(2,1)S(1)} custom-call(bf16[128,4096]{1,0:T(8,128)(2,1)S(1)} %copy-done.5, bf16[128,128]{1,0:T(8,128)(2,1)S(1)} %get-tuple-element.29.refs_1_.refs_2_, bf16[1280,128]{1,0:T(8,128)(2,1)S(1)} %get-tuple-element.30.refs_2_, bf16[640,128]{1,0:T(8,128)(2,1)S(1)} %pick_by_place.6.refs_3_, ...), custom_call_target="tpu_custom_call" | custom-call | flops 1006632960 | bytes 262144 | tf_op jit(solution)/shard_map/attend/pallas_call | solution.py:382
  87.9 1.7 %weigh.1 = (bf16[1024,1280]{1,0:T(8,128)(2,1)S(1)}, f32[1024,128]{1,0:T(8,128)S(1)}) custom-call(bf16[128,4096]{1,0:T(8,128)(2,1)S(1)} %copy-done.5, bf16[128,128]{1,0:T(8,128)(2,1)S(1)} %get-tuple-element.29.refs_1_.refs_2_, bf16[1280,128]{1,0:T(8,128)(2,1)S(1)} %get-tuple-element.30.refs_2_, bf16[640,128]{1,0:T(8,128)(2,1)S(1)} %pick_by_place.4.refs_3_, ...), custom_call_target="tpu_custom_call" | custom-call | flops 671088640 | bytes 262144 | tf_op jit(solution)/shard_map/weigh/pallas_call | solution.py:382
  89.6 1.6 %mix_far.1 = bf16[128,4096]{1,0:T(8,128)(2,1)} custom-call(bf16[1024,1280]{1,0:T(8,128)(2,1)S(1)} %get-tuple-element.39.refs_0_, f32[1024,128]{1,0:T(8,128)S(1)} %get-tuple-element.40.refs_1_, bf16[128,128]{1,0:T(8,128)(2,1)S(1)} %get-tuple-element.29.refs_1_.refs_2_, bf16[640,128]{1,0:T(8,128)(2,1)S(1)} %pick_by_place.5.refs_3_, ...), custom_call_target="tpu_custom_call" | custom-call | flops 335544320 | bytes 1048576 | tf_op jit(solution)/shard_map/mix_far/pallas_call | solution.py:439
  (77 shorter events, 12.3 us)
Async XLA Ops:
  5.7 10.3 %collective-permute-start.13 = (f32[512,128]{1,0:T(8,128)S(1)}, f32[512,128]{1,0:T(8,128)S(1)}, u32[]{:S(2)}, u32[]{:S(2)}) collective-permute-start(f32[512,128]{1,0:T(8,128)S(1)} %get-tuple-element.43), channel_id=1, source_target_pairs={{0,1},{1,0},{2,3},{3,2},{4,5},{5,4},{6,7},{7,6},{8,9},{9,8},{10,11... | collective-permute-start | bytes 786440 | tf_op jit(solution)/shard_map/ppermute | solution.py:206
  8.8 12.8 %collective-permute-start.1 = (f32[512,128]{1,0:T(8,128)S(1)}, f32[512,128]{1,0:T(8,128)S(1)}, u32[]{:S(2)}, u32[]{:S(2)}) collective-permute-start(f32[512,128]{1,0:T(8,128)S(1)} %get-tuple-element.35), channel_id=1, source_target_pairs={{0,1},{1,0},{2,3},{3,2},{4,5},{5,4},{6,7},{7,6},{8,9},{9,8},{10,11... | collective-permute-start | bytes 786440 | tf_op jit(solution)/shard_map/ppermute | solution.py:206
  8.9 18.3 %collective-permute-start = (f32[512,128]{1,0:T(8,128)S(1)}, f32[512,128]{1,0:T(8,128)S(1)}, u32[]{:S(2)}, u32[]{:S(2)}) collective-permute-start(f32[512,128]{1,0:T(8,128)S(1)} %get-tuple-element.26), channel_id=1, source_target_pairs={{0,1},{1,0},{2,3},{3,2},{4,5},{5,4},{6,7},{7,6},{8,9},{9,8},{10,11... | collective-permute-start | bytes 786440 | tf_op jit(solution)/shard_map/ppermute | solution.py:206
  16.0 11.3 %collective-permute-start.14 = (f32[512,128]{1,0:T(8,128)S(1)}, f32[512,128]{1,0:T(8,128)S(1)}, u32[]{:S(2)}, u32[]{:S(2)}) collective-permute-start(f32[512,128]{1,0:T(8,128)S(1)} %add.35), channel_id=1, source_target_pairs={{1,2},{2,1},{0,4},{3,7},{5,6},{6,5},{4,0},{7,3},{9,10},{10,9},{8,1... | collective-permute-start | bytes 786440 | tf_op jit(solution)/shard_map/ppermute | solution.py:145
  16.1 16.7 %collective-permute-start.4 = (f32[512,128]{1,0:T(8,128)S(1)}, f32[512,128]{1,0:T(8,128)S(1)}, u32[]{:S(2)}, u32[]{:S(2)}) collective-permute-start(f32[512,128]{1,0:T(8,128)S(1)} %get-tuple-element.36), channel_id=1, source_target_pairs={{0,1},{1,0},{2,3},{3,2},{4,5},{5,4},{6,7},{7,6},{8,9},{9,8},{10,11... | collective-permute-start | bytes 786440 | tf_op jit(solution)/shard_map/ppermute | solution.py:206
  21.6 11.3 %collective-permute-start.2 = (f32[512,128]{1,0:T(8,128)S(1)}, f32[512,128]{1,0:T(8,128)S(1)}, u32[]{:S(2)}, u32[]{:S(2)}) collective-permute-start(f32[512,128]{1,0:T(8,128)S(1)} %add.30), channel_id=1, source_target_pairs={{1,2},{2,1},{0,4},{3,7},{5,6},{6,5},{4,0},{7,3},{9,10},{10,9},{8,1... | collective-permute-start | bytes 786440 | tf_op jit(solution)/shard_map/ppermute | solution.py:145
  27.2 9.4 %collective-permute-start.16 = (f32[512,128]{1,0:T(8,128)S(1)}, f32[512,128]{1,0:T(8,128)S(1)}, u32[]{:S(2)}, u32[]{:S(2)}) collective-permute-start(f32[512,128]{1,0:T(8,128)S(1)} %add.36), channel_id=1, source_target_pairs={{1,2},{2,1},{0,4},{3,7},{5,6},{6,5},{4,0},{7,3},{9,10},{10,9},{8,1... | collective-permute-start | bytes 786440 | tf_op jit(solution)/shard_map/ppermute | solution.py:145
  27.4 11.1 %collective-permute-start.15 = (f32[512,128]{1,0:T(8,128)S(1)}, f32[512,128]{1,0:T(8,128)S(1)}, u32[]{:S(2)}, u32[]{:S(2)}) collective-permute-start(f32[512,128]{1,0:T(8,128)S(1)} %add_in_middle.3), channel_id=1, source_target_pairs={{0,1},{1,0},{2,3},{3,2},{4,5},{5,4},{6,7},{7,6},{8,9},{9,8},{10,11... | collective-permute-start | bytes 786440 | tf_op jit(solution)/shard_map/ppermute | solution.py:206
  32.8 6.7 %collective-permute-start.5 = (f32[512,128]{1,0:T(8,128)S(1)}, f32[512,128]{1,0:T(8,128)S(1)}, u32[]{:S(2)}, u32[]{:S(2)}) collective-permute-start(f32[512,128]{1,0:T(8,128)S(1)} %add.31), channel_id=1, source_target_pairs={{1,2},{2,1},{0,4},{3,7},{5,6},{6,5},{4,0},{7,3},{9,10},{10,9},{8,1... | collective-permute-start | bytes 786440 | tf_op jit(solution)/shard_map/ppermute | solution.py:145
  33.0 10.2 %collective-permute-start.3 = (f32[512,128]{1,0:T(8,128)S(1)}, f32[512,128]{1,0:T(8,128)S(1)}, u32[]{:S(2)}, u32[]{:S(2)}) collective-permute-start(f32[512,128]{1,0:T(8,128)S(1)} %add_in_middle.2), channel_id=1, source_target_pairs={{0,1},{1,0},{2,3},{3,2},{4,5},{5,4},{6,7},{7,6},{8,9},{9,8},{10,11... | collective-permute-start | bytes 786440 | tf_op jit(solution)/shard_map/ppermute | solution.py:206
  39.5 4.9 %collective-permute-start.17 = (bf16[640,128]{1,0:T(8,128)(2,1)S(1)}, bf16[640,128]{1,0:T(8,128)(2,1)S(1)}, u32[]{:S(2)}, u32[]{:S(2)}) collective-permute-start(bf16[640,128]{1,0:T(8,128)(2,1)S(1)} %get-tuple-element.46), channel_id=1, source_target_pairs={{0,4},{4,0},{8,12},{12,8},{16,20},{20,16},{24,28},{28,24},{1,5},{5... | collective-permute-start | bytes 491528 | tf_op jit(solution)/shard_map/ppermute | solution.py:32
  44.5 5.4 %collective-permute-start.18 = (bf16[640,128]{1,0:T(8,128)(2,1)S(1)}, bf16[640,128]{1,0:T(8,128)(2,1)S(1)}, u32[]{:S(2)}, u32[]{:S(2)}) collective-permute-start(bf16[640,128]{1,0:T(8,128)(2,1)S(1)} %add.37), channel_id=1, source_target_pairs={{0,8},{4,20},{8,0},{12,28},{16,24},{20,4},{24,16},{28,12},{1,9},{5... | collective-permute-start | bytes 491528 | tf_op jit(solution)/shard_map/ppermute | solution.py:484
  46.3 5.4 %collective-permute-start.7 = (bf16[640,128]{1,0:T(8,128)(2,1)S(1)}, bf16[640,128]{1,0:T(8,128)(2,1)S(1)}, u32[]{:S(2)}, u32[]{:S(2)}) collective-permute-start(bf16[640,128]{1,0:T(8,128)(2,1)S(1)} %add.32), channel_id=1, source_target_pairs={{0,8},{4,20},{8,0},{12,28},{16,24},{20,4},{24,16},{28,12},{1,9},{5... | collective-permute-start | bytes 491528 | tf_op jit(solution)/shard_map/ppermute | solution.py:484
  49.9 5.4 %collective-permute-start.19 = (bf16[640,128]{1,0:T(8,128)(2,1)S(1)}, bf16[640,128]{1,0:T(8,128)(2,1)S(1)}, u32[]{:S(2)}, u32[]{:S(2)}) collective-permute-start(bf16[640,128]{1,0:T(8,128)(2,1)S(1)} %add.38), channel_id=1, source_target_pairs={{0,16},{4,12},{8,24},{12,4},{16,0},{20,28},{24,8},{28,20},{1,17},{... | collective-permute-start | bytes 491528 | tf_op jit(solution)/shard_map/ppermute | solution.py:484
  51.7 5.4 %collective-permute-start.8 = (bf16[640,128]{1,0:T(8,128)(2,1)S(1)}, bf16[640,128]{1,0:T(8,128)(2,1)S(1)}, u32[]{:S(2)}, u32[]{:S(2)}) collective-permute-start(bf16[640,128]{1,0:T(8,128)(2,1)S(1)} %add.33), channel_id=1, source_target_pairs={{0,16},{4,12},{8,24},{12,4},{16,0},{20,28},{24,8},{28,20},{1,17},{... | collective-permute-start | bytes 491528 | tf_op jit(solution)/shard_map/ppermute | solution.py:484
  55.4 6.7 %collective-permute-start.20 = (bf16[640,128]{1,0:T(8,128)(2,1)S(1)}, bf16[640,128]{1,0:T(8,128)(2,1)S(1)}, u32[]{:S(2)}, u32[]{:S(2)}) collective-permute-start(bf16[640,128]{1,0:T(8,128)(2,1)S(1)} %add.39.refs_5_), channel_id=1, source_target_pairs={{0,1},{1,0},{2,3},{3,2},{4,5},{5,4},{6,7},{7,6},{8,9},{9,8},{10,11... | collective-permute-start | bytes 491528 | tf_op jit(solution)/shard_map/ppermute | solution.py:511
  57.2 6.6 %collective-permute-start.9 = (bf16[640,128]{1,0:T(8,128)(2,1)S(1)}, bf16[640,128]{1,0:T(8,128)(2,1)S(1)}, u32[]{:S(2)}, u32[]{:S(2)}) collective-permute-start(bf16[640,128]{1,0:T(8,128)(2,1)S(1)} %add.34.refs_3_), channel_id=1, source_target_pairs={{0,1},{1,0},{2,3},{3,2},{4,5},{5,4},{6,7},{7,6},{8,9},{9,8},{10,11... | collective-permute-start | bytes 491528 | tf_op jit(solution)/shard_map/ppermute | solution.py:511
  58.9 4.9 %collective-permute-start.31 = (bf16[640,128]{1,0:T(8,128)(2,1)S(1)}, bf16[640,128]{1,0:T(8,128)(2,1)S(1)}, u32[]{:S(2)}, u32[]{:S(2)}) collective-permute-start(bf16[640,128]{1,0:T(8,128)(2,1)S(1)} %add.39.refs_5_), channel_id=1, source_target_pairs={{1,2},{2,1},{0,4},{3,7},{5,6},{6,5},{4,0},{7,3},{9,10},{10,9},{8,1... | collective-permute-start | bytes 491528 | tf_op jit(solution)/shard_map/ppermute | solution.py:145
  58.9 6.2 %collective-permute-start.28 = (bf16[640,128]{1,0:T(8,128)(2,1)S(1)}, bf16[640,128]{1,0:T(8,128)(2,1)S(1)}, u32[]{:S(2)}, u32[]{:S(2)}) collective-permute-start(bf16[640,128]{1,0:T(8,128)(2,1)S(1)} %add.34.refs_3_), channel_id=1, source_target_pairs={{1,2},{2,1},{0,4},{3,7},{5,6},{6,5},{4,0},{7,3},{9,10},{10,9},{8,1... | collective-permute-start | bytes 491528 | tf_op jit(solution)/shard_map/ppermute | solution.py:145
  59.4 7.0 %collective-permute-start.25 = (bf16[640,128]{1,0:T(8,128)(2,1)S(1)}, bf16[640,128]{1,0:T(8,128)(2,1)S(1)}, u32[]{:S(2)}, u32[]{:S(2)}) collective-permute-start(bf16[640,128]{1,0:T(8,128)(2,1)S(1)} %add.39.refs_5_), channel_id=1, source_target_pairs={{0,4},{4,0},{8,12},{12,8},{16,20},{20,16},{24,28},{28,24},{1,5},{5... | collective-permute-start | bytes 491528 | tf_op jit(solution)/shard_map/ppermute | solution.py:32
  62.1 4.9 %collective-permute-start.21 = (bf16[640,128]{1,0:T(8,128)(2,1)S(1)}, bf16[640,128]{1,0:T(8,128)(2,1)S(1)}, u32[]{:S(2)}, u32[]{:S(2)}) collective-permute-start(bf16[640,128]{1,0:T(8,128)(2,1)S(1)} %collective-permute-done.20.refs_5_), channel_id=1, source_target_pairs={{1,2},{2,1},{0,4},{3,7},{5,6},{6,5},{4,0},{7,3},{9,10},{10,9},{8,1... | collective-permute-start | bytes 491528 | tf_op jit(solution)/shard_map/ppermute | solution.py:145
  63.8 4.5 %collective-permute-start.10 = (bf16[640,128]{1,0:T(8,128)(2,1)S(1)}, bf16[640,128]{1,0:T(8,128)(2,1)S(1)}, u32[]{:S(2)}, u32[]{:S(2)}) collective-permute-start(bf16[640,128]{1,0:T(8,128)(2,1)S(1)} %collective-permute-done.9.refs_3_), channel_id=1, source_target_pairs={{1,2},{2,1},{0,4},{3,7},{5,6},{6,5},{4,0},{7,3},{9,10},{10,9},{8,1... | collective-permute-start | bytes 491528 | tf_op jit(solution)/shard_map/ppermute | solution.py:145
  63.8 9.6 %collective-permute-start.32 = (bf16[640,128]{1,0:T(8,128)(2,1)S(1)}, bf16[640,128]{1,0:T(8,128)(2,1)S(1)}, u32[]{:S(2)}, u32[]{:S(2)}) collective-permute-start(bf16[640,128]{1,0:T(8,128)(2,1)S(1)} %collective-permute-done.31.middle_ref), channel_id=1, source_target_pairs={{1,0},{2,3},{5,4},{6,7},{9,8},{10,11},{13,12},{14,15},{17,16},{18,... | collective-permute-start | bytes 491528 | tf_op jit(solution)/shard_map/ppermute | solution.py:511
  65.1 11.9 %collective-permute-start.29 = (bf16[640,128]{1,0:T(8,128)(2,1)S(1)}, bf16[640,128]{1,0:T(8,128)(2,1)S(1)}, u32[]{:S(2)}, u32[]{:S(2)}) collective-permute-start(bf16[640,128]{1,0:T(8,128)(2,1)S(1)} %collective-permute-done.28.middle_ref), channel_id=1, source_target_pairs={{1,0},{2,3},{5,4},{6,7},{9,8},{10,11},{13,12},{14,15},{17,16},{18,... | collective-permute-start | bytes 491528 | tf_op jit(solution)/shard_map/ppermute | solution.py:511
  66.4 10.6 %collective-permute-start.24 = (bf16[640,128]{1,0:T(8,128)(2,1)S(1)}, bf16[640,128]{1,0:T(8,128)(2,1)S(1)}, u32[]{:S(2)}, u32[]{:S(2)}) collective-permute-start(bf16[640,128]{1,0:T(8,128)(2,1)S(1)} %add.34.refs_3_), channel_id=1, source_target_pairs={{0,4},{4,0},{8,12},{12,8},{16,20},{20,16},{24,28},{28,24},{1,5},{5... | collective-permute-start | bytes 491528 | tf_op jit(solution)/shard_map/ppermute | solution.py:32
  67.0 13.5 %collective-permute-start.22 = (bf16[640,128]{1,0:T(8,128)(2,1)S(1)}, bf16[640,128]{1,0:T(8,128)(2,1)S(1)}, u32[]{:S(2)}, u32[]{:S(2)}) collective-permute-start(bf16[640,128]{1,0:T(8,128)(2,1)S(1)} %collective-permute-done.21.middle_ref), channel_id=1, source_target_pairs={{1,0},{2,3},{5,4},{6,7},{9,8},{10,11},{13,12},{14,15},{17,16},{18,... | collective-permute-start | bytes 491528 | tf_op jit(solution)/shard_map/ppermute | solution.py:511
  68.3 14.5 %collective-permute-start.11 = (bf16[640,128]{1,0:T(8,128)(2,1)S(1)}, bf16[640,128]{1,0:T(8,128)(2,1)S(1)}, u32[]{:S(2)}, u32[]{:S(2)}) collective-permute-start(bf16[640,128]{1,0:T(8,128)(2,1)S(1)} %collective-permute-done.10.middle_ref), channel_id=1, source_target_pairs={{1,0},{2,3},{5,4},{6,7},{9,8},{10,11},{13,12},{14,15},{17,16},{18,... | collective-permute-start | bytes 491528 | tf_op jit(solution)/shard_map/ppermute | solution.py:511
  73.5 10.0 %collective-permute-start.27 = (bf16[640,128]{1,0:T(8,128)(2,1)S(1)}, bf16[640,128]{1,0:T(8,128)(2,1)S(1)}, u32[]{:S(2)}, u32[]{:S(2)}) collective-permute-start(bf16[640,128]{1,0:T(8,128)(2,1)S(1)} %collective-permute-done.20.refs_5_), channel_id=1, source_target_pairs={{0,4},{4,0},{8,12},{12,8},{16,20},{20,16},{24,28},{28,24},{1,5},{5... | collective-permute-start | bytes 491528 | tf_op jit(solution)/shard_map/ppermute | solution.py:32
  77.0 6.7 %collective-permute-start.26 = (bf16[640,128]{1,0:T(8,128)(2,1)S(1)}, bf16[640,128]{1,0:T(8,128)(2,1)S(1)}, u32[]{:S(2)}, u32[]{:S(2)}) collective-permute-start(bf16[640,128]{1,0:T(8,128)(2,1)S(1)} %collective-permute-done.9.refs_3_), channel_id=1, source_target_pairs={{0,4},{4,0},{8,12},{12,8},{16,20},{20,16},{24,28},{28,24},{1,5},{5... | collective-permute-start | bytes 491528 | tf_op jit(solution)/shard_map/ppermute | solution.py:32
  77.0 8.7 %collective-permute-start.33 = (bf16[640,128]{1,0:T(8,128)(2,1)S(1)}, bf16[640,128]{1,0:T(8,128)(2,1)S(1)}, u32[]{:S(2)}, u32[]{:S(2)}) collective-permute-start(bf16[640,128]{1,0:T(8,128)(2,1)S(1)} %pick_by_place.7.refs_5_), channel_id=1, source_target_pairs={{0,4},{4,0},{8,12},{12,8},{16,20},{20,16},{24,28},{28,24},{1,5},{5... | collective-permute-start | bytes 491528 | tf_op jit(solution)/shard_map/ppermute | solution.py:32
  80.5 5.3 %collective-permute-start.30 = (bf16[640,128]{1,0:T(8,128)(2,1)S(1)}, bf16[640,128]{1,0:T(8,128)(2,1)S(1)}, u32[]{:S(2)}, u32[]{:S(2)}) collective-permute-start(bf16[640,128]{1,0:T(8,128)(2,1)S(1)} %pick_by_place.6.refs_3_), channel_id=1, source_target_pairs={{0,4},{4,0},{8,12},{12,8},{16,20},{20,16},{24,28},{28,24},{1,5},{5... | collective-permute-start | bytes 491528 | tf_op jit(solution)/shard_map/ppermute | solution.py:32
  82.9 6.7 %collective-permute-start.23 = (bf16[640,128]{1,0:T(8,128)(2,1)S(1)}, bf16[640,128]{1,0:T(8,128)(2,1)S(1)}, u32[]{:S(2)}, u32[]{:S(2)}) collective-permute-start(bf16[640,128]{1,0:T(8,128)(2,1)S(1)} %pick_by_place.5.refs_3_), channel_id=1, source_target_pairs={{0,4},{4,0},{8,12},{12,8},{16,20},{20,16},{24,28},{28,24},{1,5},{5... | collective-permute-start | bytes 491528 | tf_op jit(solution)/shard_map/ppermute | solution.py:32
  (9 other events, 150.4 us)
